TPU v7x, 256 devices: a whole 4x4x8 slice. The times are simulated.
256 devices in a mesh: section: 16 (over x, y), tensor: 16 (over z, core).
Axes of the slice: x: 4, y: 4, z: 8, core: 2. Of those that a mesh axis runs over, the one named last changes fastest.
Arguments:
- queries: bfloat16 [16, 512, 8192], P('section', None, 'tensor'), may hold values from -20 to 20
- key_rows: bfloat16 [16, 512, 1024], P('section'), may hold values from -6 to 6
- value_rows: bfloat16 [16, 512, 1024], P('section'), may hold values from -6 to 6
- out_grad: bfloat16 [16, 512, 8192], P('section', None, 'tensor'), may hold values from -24 to 24
- layer_input: bfloat16 [16, 512, 8192], P('section', 'tensor'), may hold values from -64 to 64
- query_weight: bfloat16 [16, 8192, 8192], P('section', None, 'tensor'), may hold values from -0.0625 to 0.0625
- dion_basis: float32 [16, 8192, 256], P('section', 'tensor'), may hold values from -0.0625 to 0.0625
- lengths: int32 [16, 3], P('section'), may hold values from 1 to 256, 512 in all within a row
Outputs:
- upstream: bfloat16 [16, 512, 8192], P('section', 'tensor')
- left_factor: float32 [16, 8192, 256], P('section', 'tensor')
- right_factor: float32 [16, 8192, 256], P('section', 'tensor')
Inputs may be any that keep to these rules, and one draw needn't show every extreme that they name: For each section the lengths of the prompt, the chosen and the rejected response, in that order, summing to 512.
All inputs are finite; a program needn't handle non-finite values.
Results may differ from a plain program's by a relative error of at most 0.022.
Values may be sent and summed in bfloat16 or wider, within the bound.
No kernel may reach another device: no remote copies, remote signals or barrier semaphores. Data moves between devices by JAX's collectives and lax.ppermute only.
A program may use at most 64 MiB of HBM per device.

v0:
```python
import math

import jax
import jax.numpy as jnp
from jax import lax
from jax.sharding import PartitionSpec as P

D = 8192
HD = 128
GROUP = 8


rope_base = 500000.0
highest = lax.Precision.HIGHEST


def shifted(value, axis, steps):
    count = lax.axis_size(axis)
    first, last = (max(0, -steps), min(count, count - steps))
    return lax.ppermute(value, axis, [(source, source + steps) for source in range(first, last)])


def tree_layout(lengths_row, token_count):
    token_ids = jnp.arange(token_count, dtype=jnp.int32)
    bound_one = lengths_row[0]
    bound_two = lengths_row[0] + lengths_row[1]
    positions = jnp.where(token_ids < bound_two, token_ids, token_ids - lengths_row[1]).astype(
        jnp.float32
    )
    row_ids = token_ids[:, None]
    col_ids = token_ids[None, :]
    crossed = (row_ids >= bound_two) & (col_ids >= bound_one) & (col_ids < bound_two)
    visible = (col_ids <= row_ids) & jnp.logical_not(crossed)
    return (positions, visible)


def unrotate(rotated, positions):
    head_dim = rotated.shape[-1]
    half_dim = head_dim // 2
    freq_ids = jnp.arange(half_dim, dtype=jnp.float32)
    inverse = jnp.exp(-math.log(rope_base) * 2.0 * freq_ids / head_dim)
    angles = positions[:, None] * inverse[None, :]
    cosine = jnp.cos(angles)[:, None, :]
    sine_part = jnp.sin(angles)[:, None, :]
    first_half = rotated[..., :half_dim]
    second_half = rotated[..., half_dim:]
    return jnp.concatenate(
        [
            first_half * cosine + second_half * sine_part,
            second_half * cosine - first_half * sine_part,
        ],
        axis=-1,
    )


def local_backward(query_heads, grad_heads, key_block, value_block, visible):
    score_scale = 1.0 / math.sqrt(query_heads.shape[-1])
    scores = (
        jnp.einsum("qhd,kd->hqk", query_heads, key_block, preferred_element_type=jnp.float32)
        * score_scale
    )
    scores = jnp.where(visible[None], scores, -jnp.inf)
    row_max = jnp.max(scores, axis=-1, keepdims=True)
    exp_scores = jnp.exp(scores - row_max)
    weights = exp_scores / jnp.sum(exp_scores, axis=-1, keepdims=True)
    weights_low = weights.astype(jnp.bfloat16)
    outputs = jnp.einsum(
        "hqk,kd->qhd", weights_low, value_block, preferred_element_type=jnp.float32
    )
    out_dot = jnp.sum(grad_heads.astype(jnp.float32) * outputs, axis=-1)
    prob_grad = jnp.einsum(
        "qhd,kd->hqk", grad_heads, value_block, preferred_element_type=jnp.float32
    )
    score_grad = (weights * (prob_grad - out_dot.T[:, :, None])).astype(jnp.bfloat16)
    return (
        jnp.einsum("hqk,kd->qhd", score_grad, key_block, preferred_element_type=jnp.float32)
        * score_scale
    )


def local(queries, key_rows, value_rows, out_grad, layer_input, query_weight, dion_basis, lengths):
    token_count = queries.shape[1]
    local_width = queries.shape[2]
    local_heads = local_width // HD
    tensor_count = lax.axis_size("tensor")
    tensor_index = lax.axis_index("tensor")
    col_width = D // tensor_count
    gathered = lax.all_gather(layer_input[0], "tensor", axis=0, tiled=True)
    columns = lax.dynamic_slice_in_dim(gathered, tensor_index * col_width, col_width, 1)
    positions, visible = tree_layout(lengths[0], token_count)
    group_head = tensor_index * local_heads // GROUP
    key_block = lax.dynamic_slice_in_dim(key_rows[0], group_head * HD, HD, 1)
    value_block = lax.dynamic_slice_in_dim(value_rows[0], group_head * HD, HD, 1)
    rotated = local_backward(
        queries[0].reshape(token_count, local_heads, HD),
        out_grad[0].reshape(token_count, local_heads, HD),
        key_block,
        value_block,
        visible,
    )
    query_grad = unrotate(rotated, positions).reshape(token_count, local_width).astype(jnp.bfloat16)
    weight_local = query_weight[0]
    layer_grad = lax.psum_scatter(
        lax.dot_general(
            query_grad, weight_local, (((1,), (1,)), ((), ())), preferred_element_type=jnp.float32
        ).astype(jnp.bfloat16),
        "tensor",
        scatter_dimension=0,
        tiled=True,
    )
    upstream = shifted(layer_grad, "section", -1)
    grad_wide = query_grad.astype(jnp.float32)
    projected = lax.psum(jnp.dot(grad_wide, dion_basis[0], precision=highest), "tensor")
    column_wide = columns.astype(jnp.float32)
    left_raw = lax.dot_general(column_wide, projected, (((0,), (0,)), ((), ())), precision=highest)
    gram_part = lax.dot_general(left_raw, left_raw, (((0,), (0,)), ((), ())), precision=highest)
    mixed_part = jnp.dot(column_wide, left_raw, precision=highest)
    gram_total, mixed_total = lax.psum((gram_part, mixed_part), "tensor")
    lower_factor = jnp.linalg.cholesky(gram_total)
    left_orth = lax.linalg.triangular_solve(
        lower_factor, left_raw, left_side=False, lower=True, transpose_a=True
    )
    mixed_orth = lax.linalg.triangular_solve(
        lower_factor, mixed_total, left_side=False, lower=True, transpose_a=True
    )
    right_factor = lax.dot_general(
        grad_wide, mixed_orth, (((0,), (0,)), ((), ())), precision=highest
    )
    return (upstream[None], (left_orth * math.sqrt(D))[None], right_factor[None])


def solution(mesh):
    placed = (
        P("section", None, "tensor"),
        P("section", None, None),
        P("section", None, None),
        P("section", None, "tensor"),
        P("section", "tensor", None),
        P("section", None, "tensor"),
        P("section", "tensor", None),
        P("section", None),
    )
    return jax.shard_map(
        local,
        mesh=mesh,
        in_specs=placed,
        out_specs=(
            P("section", "tensor", None),
            P("section", "tensor", None),
            P("section", "tensor", None),
        ),
        check_vma=False,
    )
```

profile of v0, /device:TPU:7, one launch (start us, length us, event | category | flops | bytes accessed | tf_op | source)
XLA Modules:
  0.0 404.4 jit_solution(8106175779800506039)
XLA Ops:
  7.2 1.3 fusion.63
  11.2 1.2 reshape_squeeze.6
  12.4 0.7 fusion.27
  13.4 2.1 fusion.64
  15.5 1.9 copy-done.3
  17.4 1.4 fusion.5
  19.2 1.2 reshape_squeeze.7
  21.1 3.5 fusion.12
  25.4 1.5 fusion.19
  27.0 0.7 all-gather.3.cloned.1.call-update
  27.7 111.9 %all-reduce.5.cloned.1.call-done = f32[512,256]{1,0:T(8,128)} async-done(((f32[512,256]{1,0:T(8,128)}), f32[512,256]{1,0:T(8,128)}) %all-reduce.5.cloned.1.call-update) | async-done | bytes 524304 | tf_op jit(solution)/shard_map/psum | solution.py:113
  139.6 58.7 %all-gather.3.cloned.1.call-done = bf16[1,512,8192]{2,1,0:T(8,128)(2,1)} async-done(((bf16[1,32,8192]{2,1,0:T(8,128)(2,1)}), bf16[1,512,8192]{2,1,0:T(8,128)(2,1)}) %all-gather.3.cloned.1.call-update) | async-done | bytes 8388624 | tf_op jit(solution)/shard_map/all_gather | solution.py:88
  198.3 1.9 fusion.23
  200.2 1.7 fusion.65
  202.0 2.5 fusion.21
  204.5 10.2 %convolution_convert_fusion = bf16[512,8192]{1,0:T(8,128)(2,1)} fusion(bf16[512,512]{0,1:T(8,128)(2,1)S(1)} %bitcast.114, bf16[1,8192,512]{2,1,0:T(8,128)(2,1)} %param.15), kind=kOutput, calls=%fused_computation.3 | convolution fusion | flops 4299161600 | bytes 17301504 | tf_op jit(solution)/shard_map/dot_general | solution.py:104
  214.8 98.6 %all-reduce.7.cloned.1.call-done = (f32[256,256]{0,1:T(8,128)}, f32[512,256]{1,0:T(8,128)}) async-done(((f32[256,256]{0,1:T(8,128)}, f32[512,256]{1,0:T(8,128)}), (f32[256,256]{0,1:T(8,128)}, f32[512,256]{1,0:T(8,128)})) %all-reduce.7.cloned.1.call-update) | async-done | bytes 786448 | tf_op jit(solution)/shard_map/psum | solution.py:118
  313.4 1.1 copy.22
  314.5 1.0 fusion.35
  315.5 11.7 %cholesky.50 = f32[128,128]{1,0:T(8,128)S(1)} custom-call(f32[128,128]{1,0:T(8,128)S(1)} %cholesky.118), custom_call_target="Cholesky" | custom-call | tf_op jit(solution)/shard_map/jit(cholesky)/cholesky | solution.py:119
  327.3 9.8 %custom-call.14 = f32[1,128,128]{1,2,0:T(8,128)S(1)} custom-call(f32[1,128,128]{2,1,0:T(8,128)S(1)} %get-tuple-element.43), custom_call_target="InvertDiagBlocksLowerTriangular" | custom-call | tf_op jit(solution)/shard_map/jit(cholesky)/cholesky | solution.py:119
  337.6 11.7 %cholesky.105 = f32[128,128]{1,0:T(8,128)S(1)} custom-call(f32[128,128]{1,0:T(8,128)S(1)} %convolution_subtract_fusion.2), custom_call_target="Cholesky" | custom-call | tf_op jit(solution)/shard_map/jit(cholesky)/cholesky | solution.py:119
  352.0 4.0 while.4
  352.6 1.4 bitcast_dynamic-update-slice_fusion.2
  354.6 1.4 bitcast_dynamic-update-slice_fusion.2
  356.0 19.9 %custom-call.16 = f32[2,128,128]{1,2,0:T(8,128)S(1)} custom-call(f32[2,128,128]{2,1,0:T(8,128)S(1)} %get-tuple-element.18), custom_call_target="InvertDiagBlocksLowerTriangular" | custom-call | tf_op jit(solution)/shard_map/triangular_solve/custom-call.0 | solution.py:120
  377.4 1.0 copy.23
  378.9 5.6 %reduce-scatter.2.cloned.1.call-done = bf16[32,8192]{1,0:T(8,128)(2,1)} async-done(((bf16[512,8192]{1,0:T(8,128)(2,1)}), bf16[32,8192]{1,0:T(8,128)(2,1)}) %reduce-scatter.2.cloned.1.call-update) | async-done | bytes 524304 | tf_op jit(solution)/shard_map/reduce_scatter | solution.py:103
  384.5 4.6 %collective-permute-start = (bf16[32,8192]{1,0:T(8,128)(2,1)}, bf16[32,8192]{1,0:T(8,128)(2,1)S(1)}, u32[]{:S(2)}, u32[]{:S(2)}) collective-permute-start(bf16[32,8192]{1,0:T(8,128)(2,1)} %reduce-scatter.2.cloned.1.call-done), channel_id=1, source_target_pairs={{16,0},{32,16},{48,32},{64,48},{80,64},{96,80},{112,96},{128,112},... | collective-permute-start | bytes 1572872 | tf_op jit(solution)/shard_map/ppermute | solution.py:20
  390.1 1.4 convolution_bitcast_fusion
  391.5 5.6 %collective-permute-done = bf16[32,8192]{1,0:T(8,128)(2,1)S(1)} collective-permute-done((bf16[32,8192]{1,0:T(8,128)(2,1)}, bf16[32,8192]{1,0:T(8,128)(2,1)S(1)}, u32[]{:S(2)}, u32[]{:S(2)}) %collective-permute-start) | collective-permute-done | bytes 524320 | tf_op jit(solution)/shard_map/ppermute | solution.py:20
  397.1 0.8 copy.50
  (48 shorter events, 9.6 us)
Async XLA Ops:
  7.2 5.2 %copy-start = (bf16[1,512,1024]{2,1,0:T(8,128)(2,1)S(1)}, bf16[1,512,1024]{2,1,0:T(8,128)(2,1)}, u32[]{:S(2)}) copy-start(bf16[1,512,1024]{2,1,0:T(8,128)(2,1)} %param.11) | copy-start | bytes 3145732
  7.2 132.4 %all-reduce.5.cloned.1.call-start = ((), (), s32[]{:S(2)}) async-start(), calls=%async_computation.2 | async-start | bytes 1048576 | tf_op jit(solution)/shard_map/psum | solution.py:113
  15.5 1.9 copy-start.3
  21.1 4.2 %copy-start.1 = (f32[1,512,256]{2,1,0:T(8,128)S(1)}, f32[1,512,256]{2,1,0:T(8,128)}, u32[]{:S(2)}) copy-start(f32[1,512,256]{2,1,0:T(8,128)} %param.16) | copy-start | bytes 1572868
  26.9 171.4 %all-gather.3.cloned.1.call-start = ((), (), s32[]{:S(2)}) async-start(), calls=%async_computation.3 | async-start | bytes 8912896 | tf_op jit(solution)/shard_map/all_gather | solution.py:88
  27.7 285.7 %all-reduce.7.cloned.1.call-start = ((), (), s32[]{:S(2)}) async-start(), calls=%async_computation.4 | async-start | bytes 1572864 | tf_op jit(solution)/shard_map/psum | solution.py:118
  204.5 180.0 %reduce-scatter.2.cloned.1.call-start = ((), (), s32[]{:S(2)}) async-start(), calls=%async_computation.1 | async-start | bytes 8912896 | tf_op jit(solution)/shard_map/reduce_scatter | solution.py:103
  313.4 65.1 %copy-start.2 = (f32[512,256]{1,0:T(8,128)S(1)}, f32[512,256]{1,0:T(8,128)}, u32[]{:S(2)}) copy-start(f32[512,256]{1,0:T(8,128)} %get-tuple-element.35) | copy-start | bytes 1572868
  384.5 12.6 %collective-permute-start = (bf16[32,8192]{1,0:T(8,128)(2,1)}, bf16[32,8192]{1,0:T(8,128)(2,1)S(1)}, u32[]{:S(2)}, u32[]{:S(2)}) collective-permute-start(bf16[32,8192]{1,0:T(8,128)(2,1)} %reduce-scatter.2.cloned.1.call-done), channel_id=1, source_target_pairs={{16,0},{32,16},{48,32},{64,48},{80,64},{96,80},{112,96},{128,112},... | collective-permute-start | bytes 1572872 | tf_op jit(solution)/shard_map/ppermute | solution.py:20
Sparse Core Ops, SparseCore 0:
  27.1 112.5 all-reduce.4
  141.6 56.6 all-gather.2
  204.6 108.7 all-reduce.6
  315.8 68.6 reduce-scatter.1
where the time goes:
time: 410 us; the launch traced here: 404 us
  waiting for transfers between devices  281 us (69%)
  other arithmetic  60.6 us (15%)
  matrix products  28.2 us (7%)
  between operations  16.7 us (4%)
  local copies, waits for them, and re-layouts  13.1 us (3%)
  starting transfers between devices  4.72 us (1%)
    psum x1, waiting for transfers between devices, local(): lax.psum(jnp.dot(grad_wide, dion_basis[0], precision=highest), 'tensor')  112 us
    psum x1, waiting for transfers between devices, local(): gram_total, mixed_total = lax.psum((gram_part, mixed_part), 'tensor')  98.6 us
    all_gather x1, waiting for transfers between devices, local(): gathered = lax.all_gather(layer_input[0], 'tensor', axis=0, tiled=True)  58.7 us
    another operation x7, other arithmetic, local(): lower_factor = jnp.linalg.cholesky(gram_total)  34.6 us
    another operation x4, other arithmetic, local(): lax.linalg.triangular_solve(lower_factor, left_raw, left_side=False, lowe...  19.9 us
    dot_general x1, matrix products, local(): lax.dot_general(query_grad, weight_local, (((1,), (1,)), ((), ())), prefe...  10.2 us
  transfers between devices with their start and end apart: 5, of which 5 were waited for; matrix products, arithmetic and copies ran while one was open for 19% of the time, Pallas kernels for 0%

commit v1 on v0

v1 whole, which is shorter than its diff:
```python
import functools
import math

import jax
import jax.numpy as jnp
from jax import lax
from jax.experimental import pallas as pl
from jax.experimental.pallas import tpu as pltpu
from jax.sharding import PartitionSpec as P

D = 8192
HD = 128
GROUP = 8
ZN = 8
CHUNK = 32

rope_base = 500000.0
highest = lax.Precision.HIGHEST
z_groups = [[2 * z + core for z in range(ZN)] for core in range(2)]


def dot_f32(a, b, dims, precision=None):
    return lax.dot_general(a, b, (dims, ((), ())), precision=precision, preferred_element_type=jnp.float32)


def attention_kernel(info, lens, cos_ref, sin_ref, q_ref, g_ref, k_ref, v_ref, out_ref):
    block = 128
    tokens = q_ref.shape[1]
    scale = 1.0 / math.sqrt(HD)
    bound_one = lens[0, 0]
    bound_two = lens[0, 0] + lens[0, 1]
    for row in range(0, tokens, block):
        keys = row + block
        q = q_ref[0, row : row + block, :]
        g = g_ref[0, row : row + block, :]
        k = k_ref[0, :keys, :]
        v = v_ref[0, :keys, :]
        s = dot_f32(q, k, ((1,), (1,))) * scale
        i = row + lax.broadcasted_iota(jnp.int32, s.shape, 0)
        j = lax.broadcasted_iota(jnp.int32, s.shape, 1)
        crossed = (i >= bound_two) & (j >= bound_one) & (j < bound_two)
        visible = (j <= i) & jnp.logical_not(crossed)
        s = jnp.where(visible, s, -jnp.inf)
        e = jnp.exp(s - jnp.max(s, axis=-1, keepdims=True))
        w = e * (1.0 / jnp.sum(e, axis=-1, keepdims=True))
        o = dot_f32(w.astype(jnp.bfloat16), v, ((1,), (0,)))
        out_dot = jnp.sum(g.astype(jnp.float32) * o, axis=-1, keepdims=True)
        dp = dot_f32(g, v, ((1,), (1,)))
        ds = (w * (dp - out_dot)).astype(jnp.bfloat16)
        r = dot_f32(ds, k, ((1,), (0,))) * scale
        turned = jnp.concatenate([r[:, HD // 2 :], r[:, : HD // 2]], axis=1)
        r = r * cos_ref[row : row + block, :] + turned * sin_ref[row : row + block, :]
        out_ref[row : row + block, :] = r.astype(jnp.bfloat16)


def attention(info, lengths, cosine, sine, queries, out_grad, key_rows, value_rows):
    tokens, width = queries.shape[1:]
    heads = width // HD
    head_block = pl.BlockSpec((1, tokens, HD), lambda h, info, lens: (0, 0, h))
    kv_block = pl.BlockSpec((1, tokens, HD), lambda h, info, lens: (0, 0, info[2]))
    whole = pl.BlockSpec((tokens, HD), lambda h, info, lens: (0, 0))
    return pl.pallas_call(
        attention_kernel,
        out_shape=jax.ShapeDtypeStruct((tokens, width), jnp.bfloat16),
        grid_spec=pltpu.PrefetchScalarGridSpec(
            num_scalar_prefetch=2,
            grid=(heads,),
            in_specs=[whole, whole, head_block, head_block, kv_block, kv_block],
            out_specs=pl.BlockSpec((tokens, HD), lambda h, info, lens: (0, h)),
        ),
        compiler_params=pltpu.CompilerParams(vmem_limit_bytes=40 << 20),
        cost_estimate=pl.CostEstimate(
            flops=heads * 5 * 2 * tokens * tokens * HD, bytes_accessed=4 << 20, transcendentals=heads * tokens * tokens
        ),
        name="attention_backward",
    )(info, lengths, cosine, sine, queries, out_grad, key_rows, value_rows)


def layer_kernel(info, mine_ref, other_ref, w_mine_ref, w_other_ref, out_ref, rows_a, rows_b):
    z, core = info[0], info[1]

    @pl.when(pl.program_id(0) == 0)
    def _():
        for r in range(ZN):
            chip = lax.rem(z + r, ZN) * (2 * CHUNK)
            for half in range(2):
                start = pl.multiple_of(chip + (core ^ half) * CHUNK, CHUNK)
                target = slice((2 * r + half) * CHUNK, (2 * r + half + 1) * CHUNK)
                rows_a[target, :] = mine_ref[pl.ds(start, CHUNK), :]
                rows_b[target, :] = other_ref[pl.ds(start, CHUNK), :]

    total = dot_f32(rows_a[...], w_mine_ref[0], ((1,), (1,)))
    total += dot_f32(rows_b[...], w_other_ref[...], ((1,), (1,)))
    out_ref[...] = total.astype(jnp.bfloat16)


def layer_partial(info, mine, other, w_mine, w_other):
    tokens, width = mine.shape
    half = w_other.shape[0]
    tile = 512
    steps = half // tile
    whole = pl.BlockSpec((tokens, width), lambda i, info: (0, 0))
    return pl.pallas_call(
        layer_kernel,
        out_shape=jax.ShapeDtypeStruct((tokens, half), jnp.bfloat16),
        grid_spec=pltpu.PrefetchScalarGridSpec(
            num_scalar_prefetch=1,
            grid=(steps,),
            in_specs=[
                whole,
                whole,
                pl.BlockSpec((1, tile, width), lambda i, info: (0, info[1] * steps + i, 0)),
                pl.BlockSpec((tile, width), lambda i, info: (i, 0)),
            ],
            out_specs=pl.BlockSpec((tokens, tile), lambda i, info: (0, i)),
            scratch_shapes=[pltpu.VMEM((tokens, width), jnp.bfloat16)] * 2,
        ),
        compiler_params=pltpu.CompilerParams(vmem_limit_bytes=40 << 20),
        cost_estimate=pl.CostEstimate(flops=4 * tokens * width * half, bytes_accessed=13 << 20, transcendentals=0),
        name="layer_partial",
    )(info, mine, other, w_mine, w_other)


def split_three(value):
    high = value.astype(jnp.bfloat16)
    rest = value - high.astype(jnp.float32)
    middle = rest.astype(jnp.bfloat16)
    low = (rest - middle.astype(jnp.float32)).astype(jnp.bfloat16)
    return high, middle, low


def times_exact(narrow, wide):
    parts = [dot_f32(narrow, part, ((0,), (0,))) for part in split_three(wide)]
    return parts[0] + (parts[1] + parts[2])


def dion_kernel(info, p_ref, m_ref, x_ref, g_ref, left_ref, right_ref, work):
    rank = p_ref.shape[1]
    b = 64
    p = p_ref[...]
    m = m_ref[...]
    work[:, :rank] = dot_f32(p, m, ((0,), (0,)), highest)
    rows = lax.broadcasted_iota(jnp.int32, (rank, rank), 0)
    cols = lax.broadcasted_iota(jnp.int32, (rank, rank), 1)
    work[:, rank:] = (rows == cols).astype(jnp.float32)
    rows_b = lax.broadcasted_iota(jnp.int32, (b, b), 0)
    cols_b = lax.broadcasted_iota(jnp.int32, (b, b), 1)
    eye = rows_b == cols_b
    sub = lax.broadcasted_iota(jnp.int32, (8, 1), 0)
    for block in range(0, rank, b):
        here = slice(block, block + b)
        both = jnp.concatenate([work[here, block : block + b], eye.astype(jnp.float32)], axis=1)
        groups = [both[8 * n : 8 * n + 8, :] for n in range(b // 8)]
        pivots = []
        for j in range(b):
            own = j // 8
            line = groups[own][j % 8 : j % 8 + 1, :]
            pivot = line[:, j : j + 1]
            pivots.append(pivot)
            scaled = line * (1.0 / pivot)
            for n in range(own, b // 8):
                factor = groups[n][:, j : j + 1]
                if n == own:
                    factor = jnp.where(sub > j % 8, factor, 0.0)
                groups[n] = groups[n] - factor * scaled
        done = jnp.concatenate(groups, axis=0)
        diagonal = jnp.concatenate(pivots, axis=0)
        inverse = done[:, b:] * (1.0 / jnp.sqrt(diagonal))
        strip = dot_f32(inverse, work[here, :], ((1,), (0,)), highest)
        work[here, :] = strip
        if block + b < rank:
            below = strip[:, block + b : rank]
            work[block + b :, :] -= dot_f32(below, strip, ((0,), (0,)), highest)
    lower_inverse = work[:, rank:]
    left_mix = dot_f32(p, lower_inverse, ((1,), (1,)), highest) * math.sqrt(D)
    left_ref[0] = times_exact(x_ref[...], left_mix)
    right_mix = dot_f32(m, lower_inverse, ((1,), (1,)), highest)
    right_ref[0] = times_exact(g_ref[...], right_mix)


def dion_factors(info, projected, mixed, inputs, query_grad):
    tokens, rank = projected.shape
    width = query_grad.shape[1]
    whole = pl.BlockSpec((tokens, rank), lambda i, info: (0, 0))
    result = pl.BlockSpec((1, width, rank), lambda i, info: (0, 0, 0))
    return pl.pallas_call(
        dion_kernel,
        out_shape=[jax.ShapeDtypeStruct((1, width, rank), jnp.float32)] * 2,
        grid_spec=pltpu.PrefetchScalarGridSpec(
            num_scalar_prefetch=1,
            grid=(1,),
            in_specs=[
                whole,
                whole,
                pl.BlockSpec((tokens, width), lambda i, info: (0, info[1])),
                pl.BlockSpec((tokens, width), lambda i, info: (0, 0)),
            ],
            out_specs=[result, result],
            scratch_shapes=[pltpu.VMEM((rank, 2 * rank), jnp.float32)],
        ),
        compiler_params=pltpu.CompilerParams(vmem_limit_bytes=40 << 20),
        cost_estimate=pl.CostEstimate(flops=12 << 30, bytes_accessed=4 << 20, transcendentals=0),
        name="dion_factors",
    )(info, projected, mixed, inputs, query_grad)


def swap_cores(value):
    return lax.ppermute(value, "tensor", [(i, i ^ 1) for i in range(2 * ZN)])


def along_z(value, steps):
    count = 2 * ZN
    return lax.ppermute(value, "tensor", [(i, (i + 2 * steps) % count) for i in range(count)])


def exchange_z(value):
    return lax.all_to_all(value, "tensor", 0, 0, tiled=True, axis_index_groups=z_groups)


def tree_reduce_scatter(parts):
    half = parts[0].shape[1] // 2
    a = [part[:, :half] for part in parts]
    b = [part[:, half:] for part in parts]
    a_up, a_down = a[4], a[5]
    b_up, b_down = b[3], b[4]
    for k in range(4):
        a_up = along_z(a_up, 1)
        b_down = along_z(b_down, -1)
        if k < 3:
            a_up = a_up + a[3 - k]
            b_down = b_down + b[5 + k]
            a_down = along_z(a_down, -1)
            b_up = along_z(b_up, 1)
            if k < 2:
                a_down = a_down + a[6 + k]
                b_up = b_up + b[2 - k]

    def joined(own, up, down):
        total = own.astype(jnp.float32) + up.astype(jnp.float32) + down.astype(jnp.float32)
        return total.astype(jnp.bfloat16)

    return jnp.concatenate([joined(a[0], a_up, a_down), joined(b[0], b_up, b_down)], axis=1)


def shift_sections(value, core_flip):
    sections, count = lax.axis_size("section"), lax.axis_size("tensor")
    pairs = [(s * count + t, (s - 1) * count + (t ^ core_flip)) for s in range(1, sections) for t in range(count)]
    return lax.ppermute(value, ("section", "tensor"), pairs)


def local(queries, key_rows, value_rows, out_grad, layer_input, query_weight, dion_basis, lengths):
    tokens, width = queries.shape[1:]
    tensor_index = lax.axis_index("tensor")
    z, core = tensor_index // 2, tensor_index % 2
    group_head = tensor_index * (width // HD) // GROUP
    info = jnp.stack([z, core, group_head]).astype(jnp.int32)
    half = D // 2

    own_columns = exchange_z(layer_input[0].reshape(CHUNK, ZN, D // ZN).transpose(1, 0, 2))
    w_other = swap_cores(lax.dynamic_slice_in_dim(query_weight[0], (1 - core) * half, half, 0))
    basis_other = swap_cores(dion_basis[0])
    other_columns = swap_cores(own_columns)
    by_core = jnp.stack([own_columns, other_columns], axis=1)
    by_core = jnp.where(core == 0, by_core, by_core[:, ::-1])
    columns = by_core.reshape(tokens, D // ZN)
    gram_part = dot_f32(own_columns.reshape(tokens // 2, D // ZN), columns, ((1,), (1,)))
    token_gram = jnp.sum(exchange_z(gram_part.reshape(ZN, CHUNK, tokens)), axis=0)

    token_ids = jnp.arange(tokens, dtype=jnp.int32)
    bound_two = lengths[0, 0] + lengths[0, 1]
    positions = jnp.where(token_ids < bound_two, token_ids, token_ids - lengths[0, 1]).astype(jnp.float32)
    freq_ids = jnp.arange(HD // 2, dtype=jnp.float32)
    angles = positions[:, None] * jnp.exp(-math.log(rope_base) * 2.0 * freq_ids / HD)[None, :]
    cosine, sine = jnp.cos(angles), jnp.sin(angles)
    cosine = jnp.concatenate([cosine, cosine], axis=1)
    sine = jnp.concatenate([sine, -sine], axis=1)
    query_grad = attention(info, lengths, cosine, sine, queries, out_grad, key_rows, value_rows)
    grad_other = swap_cores(query_grad)

    def own_rows(value):
        return lax.dynamic_index_in_dim(value.reshape(ZN, 2, CHUNK, width), core, 1, False).reshape(tokens // 2, width)

    part = dot_f32(own_rows(query_grad).astype(jnp.float32), dion_basis[0], ((1,), (0,)), highest)
    part += dot_f32(own_rows(grad_other).astype(jnp.float32), basis_other, ((1,), (0,)), highest)
    own_projected = jnp.sum(exchange_z(part.reshape(ZN, CHUNK, part.shape[1])), axis=0)
    projected = lax.all_gather(own_projected, "tensor", axis=0, tiled=True)
    mixed = lax.all_gather(dot_f32(token_gram, projected, ((1,), (0,)), highest), "tensor", axis=0, tiled=True)
    left_factor, right_factor = dion_factors(info, projected, mixed, columns, query_grad)

    partial = layer_partial(info, query_grad, grad_other, query_weight, w_other)
    parts = [partial[2 * CHUNK * r : 2 * CHUNK * (r + 1)] for r in range(ZN)]
    summed = tree_reduce_scatter(parts)
    from_own = shift_sections(summed[:CHUNK], 0)
    from_other = shift_sections(summed[CHUNK:], 1)
    upstream = jnp.where(
        core == 0,
        jnp.concatenate([from_own, from_other], axis=1),
        jnp.concatenate([from_other, from_own], axis=1),
    )
    return (upstream[None], left_factor, right_factor)


def solution(mesh):
    placed = (
        P("section", None, "tensor"),
        P("section", None, None),
        P("section", None, None),
        P("section", None, "tensor"),
        P("section", "tensor", None),
        P("section", None, "tensor"),
        P("section", "tensor", None),
        P("section", None),
    )
    return jax.shard_map(
        local,
        mesh=mesh,
        in_specs=placed,
        out_specs=(
            P("section", "tensor", None),
            P("section", "tensor", None),
            P("section", "tensor", None),
        ),
        check_vma=False,
    )
```

time: 410 us -> 184 us (0.45); the launches traced: 404 us -> 183 us
  waiting for transfers between devices: 281 us -> 6.69 us
  blocking collectives: 0 us -> 55 us
  other arithmetic: 60.6 us -> 9.42 us
  Pallas kernels: 0 us -> 49.3 us
  starting transfers between devices: 4.72 us -> 47.8 us
  matrix products: 28.2 us -> 4.26 us
  between operations: 16.7 us -> 2.26 us
  local copies, waits for them, and re-layouts: 13.1 us -> 8.72 us
    psum x2 -> x0, waiting for transfers between devices: 210 us -> none  [the longest x1 112 us: local(): lax.psum(jnp.dot(grad_wide, dion_basis[0], precision=highest), 'tensor')]
    all_gather x1 -> x0, waiting for transfers between devices: 58.7 us -> none  [local(): gathered = lax.all_gather(layer_input[0], 'tensor', axis=0, tiled=True)]
    all_gather x0 -> x2, blocking collectives: none -> 55 us  [the longest x1 30.4 us: local(): projected = lax.all_gather(own_projected, 'tensor', axis=0, tiled=True)]
    another operation x11 -> x2, other arithmetic: 54.5 us -> 0.18 us  [the longest x1 0.1 us: local(): by_core = jnp.stack([own_columns, other_columns], axis=1)]
    pallas_call x0 -> x3, Pallas kernels: none -> 49.3 us  [the longest x1 29 us: dion_factors(): pl.pallas_call(dion_kernel, out_shape=[jax.ShapeDtypeStruct((1, width, ra...]
    all_to_all x0 -> x3, starting transfers between devices: none -> 21.8 us  [exchange_z(): lax.all_to_all(value, 'tensor', 0, 0, tiled=True, axis_index_groups=z_gro...]
    ppermute x1 -> x20, starting transfers between devices: 4.56 us -> 26 us  [the longest x14 16.7 us: along_z(): lax.ppermute(value, 'tensor', [(i, (i + 2 * steps) % count) for i in rang...]
    dot_general x9 -> x4, matrix products: 24.9 us -> 4.26 us  [dot_f32(): lax.dot_general(a, b, (dims, ((), ())), precision=precision, preferred_el...]
  transfers between devices with their start and end apart: 5 -> 23, of which waited for: 5 -> 4; matrix products, arithmetic and copies ran while one was open for 19% -> 7% of each run, Pallas kernels for 0% -> 27%
where the time goes in v1:
time: 184 us; the launch traced here: 183 us
  blocking collectives  55 us (30%)
  Pallas kernels  49.3 us (27%)
  starting transfers between devices  47.8 us (26%)
  other arithmetic  9.42 us (5%)
  local copies, waits for them, and re-layouts  8.72 us (5%)
  waiting for transfers between devices  6.69 us (4%)
  matrix products  4.26 us (2%)
  between operations  2.26 us (1%)
    all_gather x1, blocking collectives, local(): projected = lax.all_gather(own_projected, 'tensor', axis=0, tiled=True)  30.4 us
    pallas_call x1, Pallas kernels, dion_factors(): pl.pallas_call(dion_kernel, out_shape=[jax.ShapeDtypeStruct((1, width, ra...  29 us
    all_gather x1, blocking collectives, local(): lax.all_gather(dot_f32(token_gram, projected, ((1,), (0,)), highest), 'te...  24.6 us
    all_to_all x3, starting transfers between devices, exchange_z(): lax.all_to_all(value, 'tensor', 0, 0, tiled=True, axis_index_groups=z_gro...  21.8 us
    ppermute x14, starting transfers between devices, along_z(): lax.ppermute(value, 'tensor', [(i, (i + 2 * steps) % count) for i in rang...  16.7 us
    pallas_call x1, Pallas kernels, attention(): pl.pallas_call(attention_kernel, out_shape=jax.ShapeDtypeStruct((tokens,...  10.7 us
    pallas_call x1, Pallas kernels, layer_partial(): pl.pallas_call(layer_kernel, out_shape=jax.ShapeDtypeStruct((tokens, half...  9.53 us
    ppermute x2, starting transfers between devices, shift_sections(): return lax.ppermute(value, ('section', 'tensor'), pairs)  7.54 us
  transfers between devices with their start and end apart: 23, of which 4 were waited for; matrix products, arithmetic and copies ran while one was open for 7% of the time, Pallas kernels for 27%

profile of v1, /device:TPU:7, one launch (start us, length us, event | category | flops | bytes accessed | tf_op | source)
XLA Modules:
  0.0 183.4 jit_solution(15773964271485845726)
XLA Ops:
  0.7 4.5 %dynamic-slice_bitcast_fusion = bf16[4096,512]{1,0:T(8,128)(2,1)} fusion(bf16[1,8192,512]{2,1,0:T(8,128)(2,1)} %w_mine_ref.1, s32[]{:T(128)S(6)} %select_n.58), kind=kLoop, calls=%fused_computation | loop fusion | bytes 8388612 | tf_op jit(solution)/shard_map/dynamic_slice | solution.py:260
  6.1 1.1 copy.15
  7.2 8.2 %all-to-all-start.1 = ((bf16[8,32,1024]{2,1,0:T(8,128)(2,1)}), bf16[8,32,1024]{2,1,0:T(8,128)(2,1)S(1)}, u32[]{:S(2)}, u32[]{:S(2)}) async-start(bf16[8,32,1024]{2,1,0:T(8,128)(2,1)} %bitcast.38), calls=%async_computation.1 | async-start | bytes 1048576 | tf_op jit(solution)/shard_map/all_to_all | solution.py:217
  18.2 1.0 multiply_sine_fusion
  19.4 1.0 copy-done.4
  20.5 1.0 copy-done.5
  21.5 10.7 %attention_backward.1.mine_ref.g_ref = bf16[512,512]{1,0:T(8,128)(2,1)S(1)} custom-call(s32[3]{0:T(128)S(1)} %pad_add_fusion.info, s32[1,3]{1,0:T(1,128)S(1)} %copy-done.1, f32[512,128]{1,0:T(8,128)S(1)} %get-tuple-element.30.cos_ref, f32[512,128]{1,0:T(8,128)S(1)} %get-tuple-element.31.sin_ref, bf16[1,512,512]{2,1,0:T(8,128)(2,1)S(1)} %copy-done.4, ...), custom_call_target="tpu_custom_call" | custom-call | flops 1342177280 | bytes 4194304 | tf_op jit(solution)/shard_map/attention_backward/pallas_call | solution.py:62
  33.9 1.5 fusion.2
  35.4 1.2 convolution_add_fusion
  36.6 7.3 %all-to-all-start = ((f32[8,32,256]{2,1,0:T(8,128)}), f32[8,32,256]{2,1,0:T(8,128)S(1)}, u32[]{:S(2)}, u32[]{:S(2)}) async-start(f32[8,32,256]{2,1,0:T(8,128)} %bitcast.13), calls=%async_computation | async-start | bytes 524288 | tf_op jit(solution)/shard_map/all_to_all | solution.py:217
  44.1 9.5 %layer_partial.1 = bf16[512,4096]{1,0:T(8,128)(2,1)S(1)} custom-call(s32[3]{0:T(128)S(1)} %pad_add_fusion.info, bf16[512,512]{1,0:T(8,128)(2,1)S(1)} %attention_backward.1.mine_ref.g_ref, bf16[512,512]{1,0:T(8,128)(2,1)S(1)} %collective-permute-done.other_ref, bf16[1,8192,512]{2,1,0:T(8,128)(2,1)} %w_mine_ref.1, ...), custom_call_target="tpu_custom_call" | custom-call | flops 4294967296 | bytes 13631488 | tf_op jit(solution)/shard_map/layer_partial/pallas_call | solution.py:103
  53.7 1.5 collective-permute-start.2
  55.2 1.3 collective-permute-start.12
  56.8 5.4 %collective-permute-done.2 = bf16[64,2048]{1,0:T(8,128)(2,1)S(1)} collective-permute-done((bf16[64,2048]{1,0:T(8,128)(2,1)S(1)}, bf16[64,2048]{1,0:T(8,128)(2,1)S(1)}, u32[]{:S(2)}, u32[]{:S(2)}) %collective-permute-start.2) | collective-permute-done | bytes 262176 | tf_op jit(solution)/shard_map/ppermute | solution.py:213
  62.1 0.9 slice_add_fusion.9
  63.9 1.9 %collective-permute-start.13 = (bf16[64,2048]{1,0:T(8,128)(2,1)}, bf16[64,2048]{1,0:T(8,128)(2,1)}, u32[]{:S(2)}, u32[]{:S(2)}) collective-permute-start(bf16[64,2048]{1,0:T(8,128)(2,1)} %get-tuple-element.18), channel_id=1, source_target_pairs={{0,14},{1,15},{2,0},{3,1},{4,2},{5,3},{6,4},{7,5},{8,6},{9,7},{10,... | collective-permute-start | bytes 786440 | tf_op jit(solution)/shard_map/ppermute | solution.py:213
  66.3 2.1 %collective-permute-start.6 = (bf16[64,2048]{1,0:T(8,128)(2,1)S(1)}, bf16[64,2048]{1,0:T(8,128)(2,1)}, u32[]{:S(2)}, u32[]{:S(2)}) collective-permute-start(bf16[64,2048]{1,0:T(8,128)(2,1)S(1)} %get-tuple-element.20), channel_id=1, source_target_pairs={{0,14},{1,15},{2,0},{3,1},{4,2},{5,3},{6,4},{7,5},{8,6},{9,7},{10,... | collective-permute-start | bytes 786440 | tf_op jit(solution)/shard_map/ppermute | solution.py:213
  68.4 1.3 fusion.6
  69.7 6.3 %all-to-all-start.2 = ((f32[8,32,512]{2,1,0:T(8,128)}), f32[8,32,512]{2,1,0:T(8,128)S(1)}, u32[]{:S(2)}, u32[]{:S(2)}) async-start(f32[8,32,512]{2,1,0:T(8,128)} %bitcast.21), calls=%async_computation.2 | async-start | bytes 1048576 | tf_op jit(solution)/shard_map/all_to_all | solution.py:217
  76.7 2.3 %slice_add_fusion.8 = (bf16[64,2048]{1,0:T(8,128)(2,1)}, bf16[64,2048]{1,0:T(8,128)(2,1)}, bf16[64,2048]{1,0:T(8,128)(2,1)}, bf16[64,2048]{1,0:T(8,128)(2,1)S(1)}) fusion(bf16[64,2048]{1,0:T(8,128)(2,1)S(1)} %collective-permute-done.3, bf16[512,4096]{1,0:T(8,128)(2,1)} %copy-done, bf16[64,2048]{1,0:T(8,128)(2,1)} %collective-permute-done.13, ...), kind=kLoop, calls=%fused_computation.22 | loop fusion | flops 524288 | bytes 3145728 | tf_op jit(solution)/shard_map/add | solution.py:230
  79.0 2.1 %collective-permute-start.4 = (bf16[64,2048]{1,0:T(8,128)(2,1)}, bf16[64,2048]{1,0:T(8,128)(2,1)S(1)}, u32[]{:S(2)}, u32[]{:S(2)}) collective-permute-start(bf16[64,2048]{1,0:T(8,128)(2,1)} %get-tuple-element.13), channel_id=1, source_target_pairs={{0,2},{1,3},{2,4},{3,5},{4,6},{5,7},{6,8},{7,9},{8,10},{9,11},{10,... | collective-permute-start | bytes 786440 | tf_op jit(solution)/shard_map/ppermute | solution.py:213
  82.6 1.8 collective-permute-start.7
  84.4 30.4 %all_gather.6.p_ref = f32[512,256]{1,0:T(8,128)S(1)} all-gather(f32[32,256]{1,0:T(8,128)S(1)} %reduce_sum.18), channel_id=1, replica_groups=mesh['section'=16,'tensor'=16] {'tensor'}, dimensions={0}, use_global_device_ids=true | all-gather | bytes 557056 | tf_op jit(solution)/shard_map/all_gather | solution.py:286
  114.9 1.5 slice_add_fusion.7
  116.8 1.2 collective-permute-start.5
  118.0 1.6 collective-permute-start.15
  120.0 24.6 %all_gather.7.m_ref = f32[512,256]{1,0:T(8,128)S(1)} all-gather(f32[32,256]{1,0:T(8,128)S(1)} %fusion.7), channel_id=1, replica_groups=mesh['section'=16,'tensor'=16] {'tensor'}, dimensions={0}, use_global_device_ids=true | all-gather | bytes 557056 | tf_op jit(solution)/shard_map/all_gather | solution.py:287
  144.6 1.3 add_convert_fusion.1
  145.9 5.0 %collective-permute-start.17 = (bf16[32,4096]{1,0:T(8,128)(2,1)S(1)}, bf16[32,4096]{1,0:T(8,128)(2,1)S(1)}, u32[]{:S(2)}, u32[]{:S(2)}) collective-permute-start(bf16[32,4096]{1,0:T(8,128)(2,1)S(1)} %get-tuple-element.24), channel_id=1, source_target_pairs={{16,1},{17,0},{18,3},{19,2},{20,5},{21,4},{22,7},{23,6},{24,9},{25... | collective-permute-start | bytes 786440 | tf_op jit(solution)/shard_map/ppermute | solution.py:248
  150.8 2.6 %collective-permute-start.16 = (bf16[32,4096]{1,0:T(8,128)(2,1)S(1)}, bf16[32,4096]{1,0:T(8,128)(2,1)S(1)}, u32[]{:S(2)}, u32[]{:S(2)}) collective-permute-start(bf16[32,4096]{1,0:T(8,128)(2,1)S(1)} %get-tuple-element.23), channel_id=1, source_target_pairs={{16,0},{17,1},{18,2},{19,3},{20,4},{21,5},{22,6},{23,7},{24,8},{25... | collective-permute-start | bytes 786440 | tf_op jit(solution)/shard_map/ppermute | solution.py:248
  153.4 29.0 %dion_factors.1 = (f32[1,512,256]{2,1,0:T(8,128)}, f32[1,512,256]{2,1,0:T(8,128)}) custom-call(s32[3]{0:T(128)S(1)} %pad_add_fusion.info, f32[512,256]{1,0:T(8,128)S(1)} %all_gather.6.p_ref, f32[512,256]{1,0:T(8,128)S(1)} %all_gather.7.m_ref, bf16[512,1024]{1,0:T(8,128)(2,1)S(1)} %bitcast.40, bf16[512,512]{1,0:T(8,128)(2,1)S(1)} %attention_backward.1.mine_ref.g_ref), custom_call_target="tpu_custom_call" | custom-call | flops 12884901888 | bytes 4194304 | tf_op jit(solution)/shard_map/dion_factors/pallas_call | solution.py:186
  182.5 0.9 maximum_select_fusion
  (59 shorter events, 9.1 us)
Async XLA Ops:
  0.6 5.2 %copy-start.6 = (bf16[1,32,8192]{2,1,0:T(8,128)(2,1)S(1)}, bf16[1,32,8192]{2,1,0:T(8,128)(2,1)}, u32[]{:S(2)}) copy-start(bf16[1,32,8192]{2,1,0:T(8,128)(2,1)} %param.12) | copy-start | bytes 1572868
  0.7 14.8 %copy-start.1 = (s32[1,3]{1,0:T(1,128)S(1)}, s32[1,3]{1,0:T(1,128)}, u32[]{:S(2)}) copy-start(s32[1,3]{1,0:T(1,128)} %lens.1) | copy-start | bytes 40
  5.2 14.2 %copy-start.2 = (bf16[1,512,1024]{2,1,0:T(8,128)(2,1)S(1)}, bf16[1,512,1024]{2,1,0:T(8,128)(2,1)}, u32[]{:S(2)}) copy-start(bf16[1,512,1024]{2,1,0:T(8,128)(2,1)} %k_ref.1) | copy-start | bytes 3145732
  5.2 14.2 %copy-start.3 = (bf16[1,512,1024]{2,1,0:T(8,128)(2,1)S(1)}, bf16[1,512,1024]{2,1,0:T(8,128)(2,1)}, u32[]{:S(2)}) copy-start(bf16[1,512,1024]{2,1,0:T(8,128)(2,1)} %v_ref.1) | copy-start | bytes 3145732
  5.2 38.9 %collective-permute-start.1 = (bf16[4096,512]{1,0:T(8,128)(2,1)}, bf16[4096,512]{1,0:T(8,128)(2,1)}, u32[]{:S(2)}, u32[]{:S(2)}) collective-permute-start(bf16[4096,512]{1,0:T(8,128)(2,1)} %dynamic-slice_bitcast_fusion), channel_id=1, source_target_pairs={{0,1},{1,0},{2,3},{3,2},{4,5},{5,4},{6,7},{7,6},{8,9},{9,8},{10,11... | collective-permute-start | bytes 12582920 | tf_op jit(solution)/shard_map/ppermute | solution.py:208
  7.2 26.2 %all-to-all-start.1 = ((bf16[8,32,1024]{2,1,0:T(8,128)(2,1)}), bf16[8,32,1024]{2,1,0:T(8,128)(2,1)S(1)}, u32[]{:S(2)}, u32[]{:S(2)}) async-start(bf16[8,32,1024]{2,1,0:T(8,128)(2,1)} %bitcast.38), calls=%async_computation.1 | async-start | bytes 1048576 | tf_op jit(solution)/shard_map/all_to_all | solution.py:217
  19.4 1.0 copy-start.4
  20.5 1.0 copy-start.5
  32.2 3.2 %collective-permute-start = (bf16[512,512]{1,0:T(8,128)(2,1)S(1)}, bf16[512,512]{1,0:T(8,128)(2,1)S(1)}, u32[]{:S(2)}, u32[]{:S(2)}) collective-permute-start(bf16[512,512]{1,0:T(8,128)(2,1)S(1)} %attention_backward.1.mine_ref.g_ref), channel_id=1, source_target_pairs={{0,1},{1,0},{2,3},{3,2},{4,5},{5,4},{6,7},{7,6},{8,9},{9,8},{10,11... | collective-permute-start | bytes 1572872 | tf_op jit(solution)/shard_map/ppermute | solution.py:208
  32.6 2.8 %collective-permute-start.18 = (f32[512,256]{1,0:T(8,128)}, f32[512,256]{1,0:T(8,128)S(1)}, u32[]{:S(2)}, u32[]{:S(2)}) collective-permute-start(f32[512,256]{1,0:T(8,128)} %bitcast.49), channel_id=1, source_target_pairs={{0,1},{1,0},{2,3},{3,2},{4,5},{5,4},{6,7},{7,6},{8,9},{9,8},{10,11... | collective-permute-start | bytes 1572872 | tf_op jit(solution)/shard_map/ppermute | solution.py:208
  33.4 10.5 %collective-permute-start.19 = (bf16[8,32,1024]{2,1,0:T(8,128)(2,1)S(1)}, bf16[8,32,1024]{2,1,0:T(8,128)(2,1)S(1)}, u32[]{:S(2)}, u32[]{:S(2)}) collective-permute-start(bf16[8,32,1024]{2,1,0:T(8,128)(2,1)S(1)} %all-to-all-done.1), channel_id=1, source_target_pairs={{0,1},{1,0},{2,3},{3,2},{4,5},{5,4},{6,7},{7,6},{8,9},{9,8},{10,11... | collective-permute-start | bytes 1572872 | tf_op jit(solution)/shard_map/ppermute | solution.py:208
  36.6 33.1 %all-to-all-start = ((f32[8,32,256]{2,1,0:T(8,128)}), f32[8,32,256]{2,1,0:T(8,128)S(1)}, u32[]{:S(2)}, u32[]{:S(2)}) async-start(f32[8,32,256]{2,1,0:T(8,128)} %bitcast.13), calls=%async_computation | async-start | bytes 524288 | tf_op jit(solution)/shard_map/all_to_all | solution.py:217
  53.6 8.6 %copy-start = (bf16[512,4096]{1,0:T(8,128)(2,1)}, bf16[512,4096]{1,0:T(8,128)(2,1)S(1)}, u32[]{:S(2)}) copy-start(bf16[512,4096]{1,0:T(8,128)(2,1)S(1)} %layer_partial.1) | copy-start | bytes 12582916
  53.7 8.5 %collective-permute-start.2 = (bf16[64,2048]{1,0:T(8,128)(2,1)S(1)}, bf16[64,2048]{1,0:T(8,128)(2,1)S(1)}, u32[]{:S(2)}, u32[]{:S(2)}) collective-permute-start(bf16[64,2048]{1,0:T(8,128)(2,1)S(1)} %get-tuple-element.21), channel_id=1, source_target_pairs={{0,2},{1,3},{2,4},{3,5},{4,6},{5,7},{6,8},{7,9},{8,10},{9,11},{10,... | collective-permute-start | bytes 786440 | tf_op jit(solution)/shard_map/ppermute | solution.py:213
  55.2 7.0 %collective-permute-start.12 = (bf16[64,2048]{1,0:T(8,128)(2,1)S(1)}, bf16[64,2048]{1,0:T(8,128)(2,1)S(1)}, u32[]{:S(2)}, u32[]{:S(2)}) collective-permute-start(bf16[64,2048]{1,0:T(8,128)(2,1)S(1)} %get-tuple-element.22), channel_id=1, source_target_pairs={{0,14},{1,15},{2,0},{3,1},{4,2},{5,3},{6,4},{7,5},{8,6},{9,7},{10,... | collective-permute-start | bytes 786440 | tf_op jit(solution)/shard_map/ppermute | solution.py:213
  63.1 12.9 %collective-permute-start.3 = (bf16[64,2048]{1,0:T(8,128)(2,1)}, bf16[64,2048]{1,0:T(8,128)(2,1)S(1)}, u32[]{:S(2)}, u32[]{:S(2)}) collective-permute-start(bf16[64,2048]{1,0:T(8,128)(2,1)} %get-tuple-element.17), channel_id=1, source_target_pairs={{0,2},{1,3},{2,4},{3,5},{4,6},{5,7},{6,8},{7,9},{8,10},{9,11},{10,... | collective-permute-start | bytes 786440 | tf_op jit(solution)/shard_map/ppermute | solution.py:213
  63.9 12.1 %collective-permute-start.13 = (bf16[64,2048]{1,0:T(8,128)(2,1)}, bf16[64,2048]{1,0:T(8,128)(2,1)}, u32[]{:S(2)}, u32[]{:S(2)}) collective-permute-start(bf16[64,2048]{1,0:T(8,128)(2,1)} %get-tuple-element.18), channel_id=1, source_target_pairs={{0,14},{1,15},{2,0},{3,1},{4,2},{5,3},{6,4},{7,5},{8,6},{9,7},{10,... | collective-permute-start | bytes 786440 | tf_op jit(solution)/shard_map/ppermute | solution.py:213
  65.7 10.5 %collective-permute-start.9 = (bf16[64,2048]{1,0:T(8,128)(2,1)}, bf16[64,2048]{1,0:T(8,128)(2,1)}, u32[]{:S(2)}, u32[]{:S(2)}) collective-permute-start(bf16[64,2048]{1,0:T(8,128)(2,1)} %get-tuple-element.19), channel_id=1, source_target_pairs={{0,2},{1,3},{2,4},{3,5},{4,6},{5,7},{6,8},{7,9},{8,10},{9,11},{10,... | collective-permute-start | bytes 786440 | tf_op jit(solution)/shard_map/ppermute | solution.py:213
  66.3 10.4 %collective-permute-start.6 = (bf16[64,2048]{1,0:T(8,128)(2,1)S(1)}, bf16[64,2048]{1,0:T(8,128)(2,1)}, u32[]{:S(2)}, u32[]{:S(2)}) collective-permute-start(bf16[64,2048]{1,0:T(8,128)(2,1)S(1)} %get-tuple-element.20), channel_id=1, source_target_pairs={{0,14},{1,15},{2,0},{3,1},{4,2},{5,3},{6,4},{7,5},{8,6},{9,7},{10,... | collective-permute-start | bytes 786440 | tf_op jit(solution)/shard_map/ppermute | solution.py:213
  69.7 45.1 %all-to-all-start.2 = ((f32[8,32,512]{2,1,0:T(8,128)}), f32[8,32,512]{2,1,0:T(8,128)S(1)}, u32[]{:S(2)}, u32[]{:S(2)}) async-start(f32[8,32,512]{2,1,0:T(8,128)} %bitcast.21), calls=%async_computation.2 | async-start | bytes 1048576 | tf_op jit(solution)/shard_map/all_to_all | solution.py:217
  79.0 35.8 %collective-permute-start.4 = (bf16[64,2048]{1,0:T(8,128)(2,1)}, bf16[64,2048]{1,0:T(8,128)(2,1)S(1)}, u32[]{:S(2)}, u32[]{:S(2)}) collective-permute-start(bf16[64,2048]{1,0:T(8,128)(2,1)} %get-tuple-element.13), channel_id=1, source_target_pairs={{0,2},{1,3},{2,4},{3,5},{4,6},{5,7},{6,8},{7,9},{8,10},{9,11},{10,... | collective-permute-start | bytes 786440 | tf_op jit(solution)/shard_map/ppermute | solution.py:213
  81.1 33.8 %collective-permute-start.14 = (bf16[64,2048]{1,0:T(8,128)(2,1)}, bf16[64,2048]{1,0:T(8,128)(2,1)}, u32[]{:S(2)}, u32[]{:S(2)}) collective-permute-start(bf16[64,2048]{1,0:T(8,128)(2,1)} %get-tuple-element.14), channel_id=1, source_target_pairs={{0,14},{1,15},{2,0},{3,1},{4,2},{5,3},{6,4},{7,5},{8,6},{9,7},{10,... | collective-permute-start | bytes 786440 | tf_op jit(solution)/shard_map/ppermute | solution.py:213
  81.7 33.2 %collective-permute-start.10 = (bf16[64,2048]{1,0:T(8,128)(2,1)}, bf16[64,2048]{1,0:T(8,128)(2,1)}, u32[]{:S(2)}, u32[]{:S(2)}) collective-permute-start(bf16[64,2048]{1,0:T(8,128)(2,1)} %get-tuple-element.15), channel_id=1, source_target_pairs={{0,2},{1,3},{2,4},{3,5},{4,6},{5,7},{6,8},{7,9},{8,10},{9,11},{10,... | collective-permute-start | bytes 786440 | tf_op jit(solution)/shard_map/ppermute | solution.py:213
  82.6 32.3 %collective-permute-start.7 = (bf16[64,2048]{1,0:T(8,128)(2,1)S(1)}, bf16[64,2048]{1,0:T(8,128)(2,1)}, u32[]{:S(2)}, u32[]{:S(2)}) collective-permute-start(bf16[64,2048]{1,0:T(8,128)(2,1)S(1)} %get-tuple-element.16), channel_id=1, source_target_pairs={{0,14},{1,15},{2,0},{3,1},{4,2},{5,3},{6,4},{7,5},{8,6},{9,7},{10,... | collective-permute-start | bytes 786440 | tf_op jit(solution)/shard_map/ppermute | solution.py:213
  116.4 28.1 %collective-permute-start.8 = (bf16[64,2048]{1,0:T(8,128)(2,1)S(1)}, bf16[64,2048]{1,0:T(8,128)(2,1)S(1)}, u32[]{:S(2)}, u32[]{:S(2)}) collective-permute-start(bf16[64,2048]{1,0:T(8,128)(2,1)S(1)} %get-tuple-element.12), channel_id=1, source_target_pairs={{0,14},{1,15},{2,0},{3,1},{4,2},{5,3},{6,4},{7,5},{8,6},{9,7},{10,... | collective-permute-start | bytes 786440 | tf_op jit(solution)/shard_map/ppermute | solution.py:213
  116.8 27.8 %collective-permute-start.5 = (bf16[64,2048]{1,0:T(8,128)(2,1)S(1)}, bf16[64,2048]{1,0:T(8,128)(2,1)S(1)}, u32[]{:S(2)}, u32[]{:S(2)}) collective-permute-start(bf16[64,2048]{1,0:T(8,128)(2,1)S(1)} %get-tuple-element.9), channel_id=1, source_target_pairs={{0,2},{1,3},{2,4},{3,5},{4,6},{5,7},{6,8},{7,9},{8,10},{9,11},{10,... | collective-permute-start | bytes 786440 | tf_op jit(solution)/shard_map/ppermute | solution.py:213
  118.0 26.6 %collective-permute-start.15 = (bf16[64,2048]{1,0:T(8,128)(2,1)S(1)}, bf16[64,2048]{1,0:T(8,128)(2,1)S(1)}, u32[]{:S(2)}, u32[]{:S(2)}) collective-permute-start(bf16[64,2048]{1,0:T(8,128)(2,1)S(1)} %get-tuple-element.10), channel_id=1, source_target_pairs={{0,14},{1,15},{2,0},{3,1},{4,2},{5,3},{6,4},{7,5},{8,6},{9,7},{10,... | collective-permute-start | bytes 786440 | tf_op jit(solution)/shard_map/ppermute | solution.py:213
  119.6 24.9 %collective-permute-start.11 = (bf16[64,2048]{1,0:T(8,128)(2,1)S(1)}, bf16[64,2048]{1,0:T(8,128)(2,1)S(1)}, u32[]{:S(2)}, u32[]{:S(2)}) collective-permute-start(bf16[64,2048]{1,0:T(8,128)(2,1)S(1)} %get-tuple-element.11), channel_id=1, source_target_pairs={{0,2},{1,3},{2,4},{3,5},{4,6},{5,7},{6,8},{7,9},{8,10},{9,11},{10,... | collective-permute-start | bytes 786440 | tf_op jit(solution)/shard_map/ppermute | solution.py:213
  145.9 36.6 %collective-permute-start.17 = (bf16[32,4096]{1,0:T(8,128)(2,1)S(1)}, bf16[32,4096]{1,0:T(8,128)(2,1)S(1)}, u32[]{:S(2)}, u32[]{:S(2)}) collective-permute-start(bf16[32,4096]{1,0:T(8,128)(2,1)S(1)} %get-tuple-element.24), channel_id=1, source_target_pairs={{16,1},{17,0},{18,3},{19,2},{20,5},{21,4},{22,7},{23,6},{24,9},{25... | collective-permute-start | bytes 786440 | tf_op jit(solution)/shard_map/ppermute | solution.py:248
  150.8 31.6 %collective-permute-start.16 = (bf16[32,4096]{1,0:T(8,128)(2,1)S(1)}, bf16[32,4096]{1,0:T(8,128)(2,1)S(1)}, u32[]{:S(2)}, u32[]{:S(2)}) collective-permute-start(bf16[32,4096]{1,0:T(8,128)(2,1)S(1)} %get-tuple-element.23), channel_id=1, source_target_pairs={{16,0},{17,1},{18,2},{19,3},{20,4},{21,5},{22,6},{23,7},{24,8},{25... | collective-permute-start | bytes 786440 | tf_op jit(solution)/shard_map/ppermute | solution.py:248

commit v2 on v1

v2 whole, which is shorter than its diff:
```python
import functools
import math

import jax
import jax.numpy as jnp
from jax import lax
from jax.experimental import pallas as pl
from jax.experimental.pallas import tpu as pltpu
from jax.sharding import PartitionSpec as P

D = 8192
HD = 128
GROUP = 8
ZN = 8
CHUNK = 32

rope_base = 500000.0
highest = lax.Precision.HIGHEST
z_groups = [[2 * z + core for z in range(ZN)] for core in range(2)]


def dot_f32(a, b, dims, precision=None):
    return lax.dot_general(a, b, (dims, ((), ())), precision=precision, preferred_element_type=jnp.float32)


def attention_kernel(info, lens, q_ref, g_ref, k_ref, v_ref, out_ref, bias, cos_ref, sin_ref):
    block = 256
    tokens, width = q_ref.shape[1:]
    core = info[1]
    scale = 1.0 / math.sqrt(HD)

    @pl.when(pl.program_id(0) == 0)
    def _():
        bound_one = lens[0, 0]
        bound_two = lens[0, 0] + lens[0, 1]
        i = lax.broadcasted_iota(jnp.int32, bias.shape, 0)
        j = lax.broadcasted_iota(jnp.int32, bias.shape, 1)
        crossed = (i >= bound_two) & (j >= bound_one) & (j < bound_two)
        visible = (j <= i) & jnp.logical_not(crossed)
        bias[...] = jnp.where(visible, 0.0, -jnp.inf)
        token = lax.broadcasted_iota(jnp.int32, cos_ref.shape, 0)
        position = jnp.where(token < bound_two, token, token - lens[0, 1]).astype(jnp.float32)
        lane = lax.broadcasted_iota(jnp.int32, cos_ref.shape, 1)
        freq_ids = jnp.where(lane < HD // 2, lane, lane - HD // 2).astype(jnp.float32)
        angle = position * jnp.exp(-math.log(rope_base) * 2.0 * freq_ids / HD)
        cos_ref[...] = jnp.cos(angle)
        sin_ref[...] = jnp.where(lane < HD // 2, 1.0, -1.0) * jnp.sin(angle)

    for row in range(0, tokens, block):
        keys = row + block
        here = slice(row, row + block)
        k = k_ref[0, :keys, :]
        v = v_ref[0, :keys, :]
        for head in range(0, width, HD):
            lanes = slice(head, head + HD)
            s = dot_f32(q_ref[0, here, lanes], k, ((1,), (1,))) + bias[here, :keys]
            dp = dot_f32(g_ref[0, here, lanes], v, ((1,), (1,)))
            e = jnp.exp2((s - jnp.max(s, axis=-1, keepdims=True)) * (scale * math.log2(math.e)))
            w = e * (1.0 / jnp.sum(e, axis=-1, keepdims=True))
            low = w.astype(jnp.bfloat16).astype(jnp.float32)
            out_dot = jnp.sum(low * dp, axis=-1, keepdims=True)
            ds = (w * (dp - out_dot)).astype(jnp.bfloat16)
            r = dot_f32(ds, k, ((1,), (0,))) * scale
            turned = jnp.concatenate([r[:, HD // 2 :], r[:, : HD // 2]], axis=1)
            r = (r * cos_ref[here, :] + turned * sin_ref[here, :]).astype(jnp.bfloat16)
            for n in range(block // CHUNK):
                chip, side = divmod(row // CHUNK + n, 2)
                target = pl.multiple_of((core ^ side) * (tokens // 2) + chip * CHUNK, CHUNK)
                out_ref[pl.ds(target, CHUNK), lanes] = r[n * CHUNK : (n + 1) * CHUNK, :]


def attention(info, lengths, queries, out_grad, key_rows, value_rows):
    tokens, width = queries.shape[1:]
    heads = width // HD
    pair = 2 * HD
    head_block = pl.BlockSpec((1, tokens, pair), lambda h, info, lens: (0, 0, h))
    kv_block = pl.BlockSpec((1, tokens, HD), lambda h, info, lens: (0, 0, info[2]))
    return pl.pallas_call(
        attention_kernel,
        out_shape=jax.ShapeDtypeStruct((tokens, width), jnp.bfloat16),
        grid_spec=pltpu.PrefetchScalarGridSpec(
            num_scalar_prefetch=2,
            grid=(width // pair,),
            in_specs=[head_block, head_block, kv_block, kv_block],
            out_specs=pl.BlockSpec((tokens, pair), lambda h, info, lens: (0, h)),
            scratch_shapes=[pltpu.VMEM((tokens, tokens), jnp.float32)] + [pltpu.VMEM((tokens, HD), jnp.float32)] * 2,
        ),
        compiler_params=pltpu.CompilerParams(vmem_limit_bytes=58 << 20),
        cost_estimate=pl.CostEstimate(
            flops=heads * 4 * 2 * tokens * tokens * HD, bytes_accessed=4 << 20, transcendentals=heads * tokens * tokens
        ),
        name="attention_backward",
    )(info, lengths, queries, out_grad, key_rows, value_rows)


up_cars = ((4, 3, 2, 1), (3, 2, 1, 0))
down_cars = ((5, 6, 7, 0), (4, 5, 6, 7))


def layer_kernel(info, mine_ref, other_ref, w_mine_ref, w_other_ref, up_ref, down_ref, rest_ref, rows_a, rows_b):
    z = info[0]
    step, steps = pl.program_id(0), pl.num_programs(0)
    cars = up_ref.shape[0]

    @pl.when(step == 0)
    def _():
        for half in range(2):
            for place, chip in enumerate((up_cars[half][0], down_cars[half][0]) + up_cars[half][1:] + down_cars[half][1:]):
                start = lax.rem(z + chip, ZN) * CHUNK
                for side in range(2):
                    target = slice((2 * place + side) * CHUNK, (2 * place + side + 1) * CHUNK)
                    rows_a[half, target, :] = mine_ref[pl.ds(pl.multiple_of(start + side * ZN * CHUNK, CHUNK), CHUNK), :]
                    start_b = pl.multiple_of(start + (1 - side) * ZN * CHUNK, CHUNK)
                    rows_b[half, target, :] = other_ref[pl.ds(start_b, CHUNK), :]

    half = lax.div(2 * step, steps)
    total = dot_f32(rows_a[half], w_mine_ref[0], ((1,), (1,)))
    total += dot_f32(rows_b[half], w_other_ref[0], ((1,), (1,)))
    total = total.astype(jnp.bfloat16)
    up_ref[...] = total[:cars]
    down_ref[...] = total[cars : 2 * cars]
    rest_ref[...] = total[2 * cars :]


def layer_partial(info, mine, other, w_mine, w_other):
    tokens, width = mine.shape
    columns = w_other.shape[1] // 2
    tile = 1024
    steps = columns // tile
    rows = [2 * CHUNK, 2 * CHUNK, tokens - 4 * CHUNK]
    whole = pl.BlockSpec((tokens, width), lambda i, info: (0, 0))
    weight = pl.BlockSpec((1, tile, width), lambda i, info: (0, info[1] * steps + i, 0))
    return pl.pallas_call(
        layer_kernel,
        out_shape=[jax.ShapeDtypeStruct((count, columns), jnp.bfloat16) for count in rows],
        grid_spec=pltpu.PrefetchScalarGridSpec(
            num_scalar_prefetch=1,
            grid=(steps,),
            in_specs=[whole, whole, weight, weight],
            out_specs=[pl.BlockSpec((count, tile), lambda i, info: (0, i)) for count in rows],
            scratch_shapes=[pltpu.VMEM((2, tokens, width), jnp.bfloat16)] * 2,
        ),
        compiler_params=pltpu.CompilerParams(vmem_limit_bytes=56 << 20),
        cost_estimate=pl.CostEstimate(
            flops=4 * tokens * width * columns, bytes_accessed=4 * width * columns + (2 << 20), transcendentals=0
        ),
        name="layer_partial",
    )(info, mine, other, w_mine, w_other)


def split_three(value):
    high = value.astype(jnp.bfloat16)
    rest = value - high.astype(jnp.float32)
    middle = rest.astype(jnp.bfloat16)
    low = (rest - middle.astype(jnp.float32)).astype(jnp.bfloat16)
    return high, middle, low


def times_exact(narrow, wide):
    parts = [dot_f32(narrow, part, ((0,), (0,))) for part in split_three(wide)]
    return parts[0] + (parts[1] + parts[2])


def parts_kernel(mine_ref, other_ref, basis_ref, basis_other_ref, x_ref, x_other_ref, out_ref):
    rows, rank = mine_ref.shape[0], basis_ref.shape[2]
    total = None
    for grad, basis in ((mine_ref, basis_ref), (other_ref, basis_other_ref)):
        for piece in split_three(basis[0]):
            term = dot_f32(grad[...], piece, ((1,), (0,)))
            total = term if total is None else total + term
    out_ref[:, :rank] = total
    out_ref[:, rank : rank + rows] = dot_f32(x_ref[...], x_ref[...], ((1,), (1,)))
    out_ref[:, rank + rows :] = dot_f32(x_ref[...], x_other_ref[...], ((1,), (1,)))


def chip_parts(mine, other, basis, basis_other, inputs, inputs_other):
    rows = inputs.shape[0]
    width, rank = basis.shape[1:]
    upper = pl.BlockSpec((rows, width), lambda i: (0, 0))
    lower = pl.BlockSpec((rows, width), lambda i: (1, 0))
    whole = [pl.BlockSpec(value.shape, lambda i, n=value.ndim: (0,) * n) for value in (basis, basis_other, inputs, inputs_other)]
    return pl.pallas_call(
        parts_kernel,
        out_shape=jax.ShapeDtypeStruct((rows, rank + 2 * rows), jnp.float32),
        grid=(1,),
        in_specs=[upper, lower] + whole,
        out_specs=pl.BlockSpec((rows, rank + 2 * rows), lambda i: (0, 0)),
        compiler_params=pltpu.CompilerParams(vmem_limit_bytes=40 << 20),
        cost_estimate=pl.CostEstimate(flops=1 << 30, bytes_accessed=4 << 20, transcendentals=0),
        name="chip_parts",
    )(mine, other, basis, basis_other, inputs, inputs_other)


def lower_inverse(block):
    size = block.shape[0]
    width = 2 * size
    rows = lax.broadcasted_iota(jnp.int32, (size, size), 0)
    cols = lax.broadcasted_iota(jnp.int32, (size, size), 1)
    sub = lax.broadcasted_iota(jnp.int32, (8, width), 0)
    both = jnp.concatenate([block, (rows == cols).astype(jnp.float32)], axis=1)
    groups = [both[8 * n : 8 * n + 8, :] for n in range(size // 8)]
    pivots = []
    for own in range(size // 8):
        live = range(own, size // 8)
        spread = [
            {n: jnp.broadcast_to(groups[n][:, 8 * own + i : 8 * own + i + 1], (8, width)) for n in live} for i in range(8)
        ]
        for i in range(8):
            column = spread[i]
            pivot = column[own][i : i + 1, :]
            pivots.append(pivot[:, :1])
            inverse = 1.0 / pivot
            below = dict(column)
            below[own] = jnp.where(sub > i, column[own], 0.0)
            for later in range(i + 1, 8):
                factor = column[own][later : later + 1, :] * inverse
                for n in live:
                    spread[later][n] = spread[later][n] - below[n] * factor
            scaled = groups[own][i : i + 1, :] * inverse
            for n in live:
                groups[n] = groups[n] - below[n] * scaled
    done = jnp.concatenate(groups, axis=0)
    return done[:, size:] * (1.0 / jnp.sqrt(jnp.concatenate(pivots, axis=0)))


def dion_kernel(info, own_ref, other_ref, x_ref, x_other_ref, g_ref, left_ref, right_ref, work):
    rows = own_ref.shape[0]
    rank = left_ref.shape[2]
    size = 64
    p = jnp.concatenate([own_ref[:, :rank], other_ref[:, :rank]], axis=0)
    m_own = dot_f32(own_ref[:, rank:], p, ((1,), (0,)), highest)
    m_other = dot_f32(other_ref[:, rank + rows :], p[:rows], ((1,), (0,)), highest)
    m_other += dot_f32(other_ref[:, rank : rank + rows], p[rows:], ((1,), (0,)), highest)
    m = jnp.concatenate([m_own, m_other], axis=0)
    work[:, :rank] = dot_f32(p, m, ((0,), (0,)), highest)
    row_ids = lax.broadcasted_iota(jnp.int32, (rank, rank), 0)
    col_ids = lax.broadcasted_iota(jnp.int32, (rank, rank), 1)
    work[:, rank:] = (row_ids == col_ids).astype(jnp.float32)
    for start in range(0, rank, size):
        here = slice(start, start + size)
        strip = dot_f32(lower_inverse(work[here, here]), work[here, :], ((1,), (0,)), highest)
        work[here, :] = strip
        if start + size < rank:
            work[start + size :, :] -= dot_f32(strip[:, start + size : rank], strip, ((0,), (0,)), highest)
    inverse = work[:, rank:]
    left_mix = dot_f32(p, inverse, ((1,), (1,)), highest) * math.sqrt(D)
    left_ref[0] = times_exact(x_ref[...], left_mix[:rows]) + times_exact(x_other_ref[...], left_mix[rows:])
    right_mix = dot_f32(m, inverse, ((1,), (1,)), highest)
    right_ref[0] = times_exact(g_ref[...], right_mix)


def dion_factors(info, own, other, inputs, inputs_other, query_grad, rank):
    tokens, width = query_grad.shape
    whole = pl.BlockSpec(own.shape, lambda i, info: (0, 0))
    columns = pl.BlockSpec((tokens // 2, width), lambda i, info: (0, info[1]))
    result = pl.BlockSpec((1, width, rank), lambda i, info: (0, 0, 0))
    return pl.pallas_call(
        dion_kernel,
        out_shape=[jax.ShapeDtypeStruct((1, width, rank), jnp.float32)] * 2,
        grid_spec=pltpu.PrefetchScalarGridSpec(
            num_scalar_prefetch=1,
            grid=(1,),
            in_specs=[whole, whole, columns, columns, pl.BlockSpec((tokens, width), lambda i, info: (0, 0))],
            out_specs=[result, result],
            scratch_shapes=[pltpu.VMEM((rank, 2 * rank), jnp.float32)],
        ),
        compiler_params=pltpu.CompilerParams(vmem_limit_bytes=40 << 20),
        cost_estimate=pl.CostEstimate(flops=12 << 30, bytes_accessed=4 << 20, transcendentals=0),
        name="dion_factors",
    )(info, own, other, inputs, inputs_other, query_grad)


def after(value, other):
    return lax.optimization_barrier((value, other))[0]


def swap_cores(value):
    return lax.ppermute(value, "tensor", [(i, i ^ 1) for i in range(2 * ZN)])


def along_z(value, steps):
    count = 2 * ZN
    return lax.ppermute(value, "tensor", [(i, (i + 2 * steps) % count) for i in range(count)])


def exchange_z(value):
    return lax.all_to_all(value, "tensor", 0, 0, tiled=True, axis_index_groups=z_groups)


def shift_sections(value, core_flip):
    sections, count = lax.axis_size("section"), lax.axis_size("tensor")
    pairs = [(s * count + t, (s - 1) * count + (t ^ core_flip)) for s in range(1, sections) for t in range(count)]
    return lax.ppermute(value, ("section", "tensor"), pairs)


def local(queries, key_rows, value_rows, out_grad, layer_input, query_weight, dion_basis, lengths):
    tokens, width = queries.shape[1:]
    tensor_index = lax.axis_index("tensor")
    z, core = tensor_index // 2, tensor_index % 2
    group_head = tensor_index * (width // HD) // GROUP
    info = jnp.stack([z, core, group_head]).astype(jnp.int32)
    half_tokens = tokens // 2

    w_other = swap_cores(query_weight)
    basis_other = swap_cores(dion_basis)

    by_column = layer_input[0].reshape(CHUNK, ZN, D // ZN).transpose(1, 0, 2)
    own_columns = exchange_z(by_column).reshape(half_tokens, D // ZN)

    query_grad = attention(info, lengths, queries, out_grad, key_rows, value_rows)
    grad_other = swap_cores(query_grad)

    up, down, rest = layer_partial(info, query_grad, grad_other, query_weight, w_other)

    own_columns = after(own_columns, up)
    other_columns = swap_cores(own_columns)
    chip_part = chip_parts(query_grad, grad_other, dion_basis, basis_other, own_columns, other_columns)
    summands = exchange_z(chip_part.reshape(ZN, CHUNK, chip_part.shape[1]))
    rows = 2 * CHUNK
    up_rest = [rest[rows * n : rows * (n + 1)] for n in range(3)]
    down_rest = [rest[rows * (3 + n) : rows * (4 + n)] for n in range(3)]

    own = jnp.sum(summands, axis=0)
    own = jnp.broadcast_to(own[None], (ZN,) + own.shape)
    gathered = exchange_z(own).reshape(half_tokens, own.shape[2])
    gathered_other = swap_cores(gathered)
    for n in range(3):
        up, down = along_z(up, 1), along_z(down, -1)
        if n == 1:
            up, down = after((up, down), own)
        if n == 2:
            up, down = after((up, down), gathered)
        up, down = up + up_rest[n], down + down_rest[n]
    half = up.shape[1] // 2
    last_up, last_down = along_z(up[:, :half], 1), along_z(down[:, half:], -1)

    def total(a, b):
        return (a.astype(jnp.float32) + b.astype(jnp.float32)).astype(jnp.bfloat16)

    summed = jnp.concatenate([total(last_up, down[:, :half]), total(last_down, up[:, half:])], axis=1)
    left_factor, right_factor = dion_factors(
        info, gathered, after(gathered_other, summed), own_columns, other_columns, query_grad, dion_basis.shape[2]
    )

    from_own = shift_sections(summed[:CHUNK], 0)
    from_other = shift_sections(summed[CHUNK:], 1)
    from_own, from_other = after((from_own, from_other), left_factor)
    upstream = jnp.where(
        core == 0,
        jnp.concatenate([from_own, from_other], axis=1),
        jnp.concatenate([from_other, from_own], axis=1),
    )
    return (upstream[None], left_factor, right_factor)


def solution(mesh):
    placed = (
        P("section", None, "tensor"),
        P("section", None, None),
        P("section", None, None),
        P("section", None, "tensor"),
        P("section", "tensor", None),
        P("section", None, "tensor"),
        P("section", "tensor", None),
        P("section", None),
    )
    return jax.shard_map(
        local,
        mesh=mesh,
        in_specs=placed,
        out_specs=(
            P("section", "tensor", None),
            P("section", "tensor", None),
            P("section", "tensor", None),
        ),
        check_vma=False,
    )
```

time: 184 us -> 150 us (0.82)
  waiting for transfers between devices: 6.69 us -> 62.2 us
  blocking collectives: 55 us -> 0 us
  Pallas kernels: 49.3 us -> 34.3 us
  starting transfers between devices: 47.8 us -> 38.2 us
  matrix products: 4.26 us -> 0 us
  local copies, waits for them, and re-layouts: 8.72 us -> 5.75 us
    all_gather x2 -> x0, blocking collectives: 55 us -> none  [the longest x1 30.4 us: local(): projected = lax.all_gather(own_projected, 'tensor', axis=0, tiled=True)]
    ppermute x14 -> x8, waiting for transfers between devices: 6.07 us -> 45.5 us  [along_z(): lax.ppermute(value, 'tensor', [(i, (i + 2 * steps) % count) for i in rang...]
    all_to_all x3, waiting for transfers between devices: 0.61 us -> 16.7 us  [exchange_z(): lax.all_to_all(value, 'tensor', 0, 0, tiled=True, axis_index_groups=z_gro...]
    pallas_call x1, Pallas kernels: 29 us -> 15 us  [dion_factors(): pl.pallas_call(dion_kernel, out_shape=[jax.ShapeDtypeStruct((1, width, ra...]
    ppermute x14 -> x8, starting transfers between devices: 16.7 us -> 10 us  [along_z(): lax.ppermute(value, 'tensor', [(i, (i + 2 * steps) % count) for i in rang...]
    all_to_all x3, starting transfers between devices: 21.8 us -> 16.3 us  [exchange_z(): lax.all_to_all(value, 'tensor', 0, 0, tiled=True, axis_index_groups=z_gro...]
    dynamic_slice x3 -> x0, local copies, waits for them, and re-layouts: 4.54 us -> none  [the longest x1 4.49 us: local(): lax.dynamic_slice_in_dim(query_weight[0], (1 - core) * half, half, 0)]
    dot_general x4 -> x0, matrix products: 4.26 us -> none  [dot_f32(): lax.dot_general(a, b, (dims, ((), ())), precision=precision, preferred_el...]
  transfers between devices with their start and end apart: 23 -> 18, of which waited for: 4 -> 7; matrix products, arithmetic and copies ran while one was open for 7% -> 5% of each run, Pallas kernels for 27% -> 23%
where the time goes in v2:
time: 150 us; the launch traced here: 149 us
  waiting for transfers between devices  62.2 us (41%)
  starting transfers between devices  38.2 us (25%)
  Pallas kernels  34.3 us (23%)
  other arithmetic  8.06 us (5%)
  local copies, waits for them, and re-layouts  5.75 us (4%)
    ppermute x8, waiting for transfers between devices, along_z(): lax.ppermute(value, 'tensor', [(i, (i + 2 * steps) % count) for i in rang...  45.5 us
    all_to_all x3, waiting for transfers between devices, exchange_z(): lax.all_to_all(value, 'tensor', 0, 0, tiled=True, axis_index_groups=z_gro...  16.7 us
    all_to_all x3, starting transfers between devices, exchange_z(): lax.all_to_all(value, 'tensor', 0, 0, tiled=True, axis_index_groups=z_gro...  16.3 us
    pallas_call x1, Pallas kernels, dion_factors(): pl.pallas_call(dion_kernel, out_shape=[jax.ShapeDtypeStruct((1, width, ra...  15 us
    ppermute x8, starting transfers between devices, along_z(): lax.ppermute(value, 'tensor', [(i, (i + 2 * steps) % count) for i in rang...  10 us
    pallas_call x1, Pallas kernels, layer_partial(): pl.pallas_call(layer_kernel, out_shape=[jax.ShapeDtypeStruct((count, colu...  9.46 us
    ppermute x2, starting transfers between devices, shift_sections(): return lax.ppermute(value, ('section', 'tensor'), pairs)  8.44 us
    pallas_call x1, Pallas kernels, attention(): pl.pallas_call(attention_kernel, out_shape=jax.ShapeDtypeStruct((tokens,...  8.06 us
  transfers between devices with their start and end apart: 18, of which 7 were waited for; matrix products, arithmetic and copies ran while one was open for 5% of the time, Pallas kernels for 23%

profile of v2, /device:TPU:7, one launch (start us, length us, event | category | flops | bytes accessed | tf_op | source)
XLA Modules:
  0.0 149.3 jit_solution(7595619154034421113)
XLA Ops:
  2.0 8.1 %attention_backward.1.mine_ref.g_ref = bf16[512,512]{1,0:T(8,128)(2,1)} custom-call(s32[3]{0:T(128)} %pad_add_fusion.info, s32[1,3]{1,0:T(1,128)} %lens.1, bf16[1,512,512]{2,1,0:T(8,128)(2,1)} %q_ref.1, bf16[1,512,512]{2,1,0:T(8,128)(2,1)} %g_ref.1, bf16[1,512,1024]{2,1,0:T(8,128)(2,1)} %k_ref.1, bf16[1,512,1024]{2,1,0:T(8,128)(2,1)} %v_ref.1), custom_call_target="tpu_custom_call" | custom-call | flops 1073741824 | bytes 4194304 | tf_op jit(solution)/shard_map/attention_backward/pallas_call | solution.py:78
  10.4 1.1 copy.14
  11.5 8.2 %all-to-all-start = ((bf16[8,32,1024]{2,1,0:T(8,128)(2,1)}), bf16[8,32,1024]{2,1,0:T(8,128)(2,1)S(1)}, u32[]{:S(2)}, u32[]{:S(2)}) async-start(bf16[8,32,1024]{2,1,0:T(8,128)(2,1)} %bitcast.13), calls=%async_computation | async-start | bytes 1048576 | tf_op jit(solution)/shard_map/all_to_all | solution.py:287
  19.8 0.8 collective-permute-start.6
  20.6 0.8 copy-done.1
  21.4 9.5 %layer_partial.1 = (bf16[64,4096]{1,0:T(8,128)(2,1)}, bf16[64,4096]{1,0:T(8,128)(2,1)}, bf16[384,4096]{1,0:T(8,128)(2,1)}) custom-call(s32[3]{0:T(128)} %pad_add_fusion.info, bf16[512,512]{1,0:T(8,128)(2,1)} %attention_backward.1.mine_ref.g_ref, bf16[512,512]{1,0:T(8,128)(2,1)} %copy-done.1, bf16[1,8192,512]{2,1,0:T(8,128)(2,1)} %w_mine_ref.1, ...), custom_call_target="tpu_custom_call" | custom-call | flops 4294967296 | bytes 10485760 | tf_op jit(solution)/shard_map/layer_partial/pallas_call | solution.py:133
  30.8 6.9 %all-to-all-done = bf16[8,32,1024]{2,1,0:T(8,128)(2,1)S(1)} async-done(((bf16[8,32,1024]{2,1,0:T(8,128)(2,1)}), bf16[8,32,1024]{2,1,0:T(8,128)(2,1)S(1)}, u32[]{:S(2)}, u32[]{:S(2)}) %all-to-all-start) | async-done | bytes 524320 | tf_op jit(solution)/shard_map/all_to_all | solution.py:287
  38.5 2.4 %collective-permute-start.4 = (bf16[64,4096]{1,0:T(8,128)(2,1)}, bf16[64,4096]{1,0:T(8,128)(2,1)}, u32[]{:S(2)}, u32[]{:S(2)}) collective-permute-start(bf16[64,4096]{1,0:T(8,128)(2,1)} %get-tuple-element.18), channel_id=1, source_target_pairs={{0,14},{1,15},{2,0},{3,1},{4,2},{5,3},{6,4},{7,5},{8,6},{9,7},{10,... | collective-permute-start | bytes 1572872 | tf_op jit(solution)/shard_map/ppermute | solution.py:283
  40.9 1.0 copy-done.2
  41.9 1.8 %chip_parts.1 = f32[256,768]{1,0:T(8,128)} custom-call(bf16[512,512]{1,0:T(8,128)(2,1)S(1)} %copy-done, bf16[512,512]{1,0:T(8,128)(2,1)S(1)} %copy-done.2, f32[1,512,256]{2,1,0:T(8,128)S(1)} %copy-done.4, f32[1,512,256]{2,1,0:T(8,128)S(1)} %collective-permute-done.6.basis_other_ref, bf16[256,1024]{1,0:T(8,128)(2,1)S(1)} %bitcast.17, ...), custom_call_target="tpu_custom_call" | custom-call | flops 1073741824 | bytes 4194304 | tf_op jit(solution)/shard_map/chip_parts/pallas_call | solution.py:182
  43.7 3.5 %all-to-all-start.1 = ((f32[8,32,768]{2,1,0:T(8,128)}), f32[8,32,768]{2,1,0:T(8,128)S(1)}, u32[]{:S(2)}, u32[]{:S(2)}) async-start(f32[8,32,768]{2,1,0:T(8,128)} %bitcast.5), calls=%async_computation.1 | async-start | bytes 1572864 | tf_op jit(solution)/shard_map/all_to_all | solution.py:287
  47.2 8.5 %collective-permute-done.2 = bf16[64,4096]{1,0:T(8,128)(2,1)S(1)} collective-permute-done((bf16[64,4096]{1,0:T(8,128)(2,1)}, bf16[64,4096]{1,0:T(8,128)(2,1)S(1)}, u32[]{:S(2)}, u32[]{:S(2)}) %collective-permute-start.2) | collective-permute-done | bytes 524320 | tf_op jit(solution)/shard_map/ppermute | solution.py:283
  55.7 2.4 %slice_add_fusion.4 = (bf16[64,4096]{1,0:T(8,128)(2,1)}, bf16[64,4096]{1,0:T(8,128)(2,1)}) fusion(bf16[64,4096]{1,0:T(8,128)(2,1)} %collective-permute-done.4, bf16[384,4096]{1,0:T(8,128)(2,1)} %get-tuple-element.17, bf16[64,4096]{1,0:T(8,128)(2,1)S(1)} %collective-permute-done.2), kind=kLoop, calls=%fused_computation.13 | loop fusion | flops 524288 | bytes 3145728 | tf_op jit(solution)/shard_map/add | solution.py:333
  58.2 2.7 %collective-permute-start.5 = (bf16[64,4096]{1,0:T(8,128)(2,1)}, bf16[64,4096]{1,0:T(8,128)(2,1)S(1)}, u32[]{:S(2)}, u32[]{:S(2)}) collective-permute-start(bf16[64,4096]{1,0:T(8,128)(2,1)} %get-tuple-element.33), channel_id=1, source_target_pairs={{0,14},{1,15},{2,0},{3,1},{4,2},{5,3},{6,4},{7,5},{8,6},{9,7},{10,... | collective-permute-start | bytes 1572872 | tf_op jit(solution)/shard_map/ppermute | solution.py:283
  60.9 9.9 %all-to-all-done.1 = f32[8,32,768]{2,1,0:T(8,128)S(1)} async-done(((f32[8,32,768]{2,1,0:T(8,128)}), f32[8,32,768]{2,1,0:T(8,128)S(1)}, u32[]{:S(2)}, u32[]{:S(2)}) %all-to-all-start.1) | async-done | bytes 786464 | tf_op jit(solution)/shard_map/all_to_all | solution.py:287
  70.8 1.0 broadcast_in_dim.2
  71.7 4.5 %all-to-all-start.2 = ((f32[8,32,768]{2,1,0:T(8,128)}), f32[8,32,768]{2,1,0:T(8,128)S(1)}, u32[]{:S(2)}, u32[]{:S(2)}) async-start(f32[8,32,768]{2,1,0:T(8,128)} %broadcast_in_dim.2), calls=%async_computation.2 | async-start | bytes 1572864 | tf_op jit(solution)/shard_map/all_to_all | solution.py:287
  76.2 5.0 %collective-permute-done.3 = bf16[64,4096]{1,0:T(8,128)(2,1)S(1)} collective-permute-done((bf16[64,4096]{1,0:T(8,128)(2,1)}, bf16[64,4096]{1,0:T(8,128)(2,1)S(1)}, u32[]{:S(2)}, u32[]{:S(2)}) %collective-permute-start.3) | collective-permute-done | bytes 524320 | tf_op jit(solution)/shard_map/ppermute | solution.py:283
  81.2 1.3 slice_add_fusion.2
  82.8 2.7 %collective-permute-start.9 = (bf16[64,4096]{1,0:T(8,128)(2,1)S(1)}, bf16[64,4096]{1,0:T(8,128)(2,1)}, u32[]{:S(2)}, u32[]{:S(2)}) collective-permute-start(bf16[64,4096]{1,0:T(8,128)(2,1)S(1)} %get-tuple-element.31), channel_id=1, source_target_pairs={{0,14},{1,15},{2,0},{3,1},{4,2},{5,3},{6,4},{7,5},{8,6},{9,7},{10,... | collective-permute-start | bytes 1572872 | tf_op jit(solution)/shard_map/ppermute | solution.py:283
  85.5 23.8 %collective-permute-done.8 = bf16[64,4096]{1,0:T(8,128)(2,1)S(1)} collective-permute-done((bf16[64,4096]{1,0:T(8,128)(2,1)S(1)}, bf16[64,4096]{1,0:T(8,128)(2,1)S(1)}, u32[]{:S(2)}, u32[]{:S(2)}) %collective-permute-start.8) | collective-permute-done | bytes 524320 | tf_op jit(solution)/shard_map/ppermute | solution.py:283
  109.3 0.8 copy-done.6
  110.1 1.6 %slice_add_fusion = (bf16[64,4096]{1,0:T(8,128)(2,1)S(1)}, bf16[64,4096]{1,0:T(8,128)(2,1)S(1)}) fusion(bf16[64,4096]{1,0:T(8,128)(2,1)} %collective-permute-done.9, bf16[384,4096]{1,0:T(8,128)(2,1)} %get-tuple-element.17, bf16[64,4096]{1,0:T(8,128)(2,1)} %copy-done.6), kind=kLoop, calls=%fused_computation.9 | loop fusion | flops 524288 | bytes 3145728 | tf_op jit(solution)/shard_map/add | solution.py:333
  112.5 1.7 %collective-permute-start.11 = (bf16[64,2048]{1,0:T(8,128)(2,1)}, bf16[64,2048]{1,0:T(8,128)(2,1)}, u32[]{:S(2)}, u32[]{:S(2)}) collective-permute-start(bf16[64,2048]{1,0:T(8,128)(2,1)} %slice.50), channel_id=1, source_target_pairs={{0,14},{1,15},{2,0},{3,1},{4,2},{5,3},{6,4},{7,5},{8,6},{9,7},{10,... | collective-permute-start | bytes 786440 | tf_op jit(solution)/shard_map/ppermute | solution.py:283
  114.2 1.4 collective-permute-start.14
  115.7 4.2 %collective-permute-done.11 = bf16[64,2048]{1,0:T(8,128)(2,1)} collective-permute-done((bf16[64,2048]{1,0:T(8,128)(2,1)}, bf16[64,2048]{1,0:T(8,128)(2,1)}, u32[]{:S(2)}, u32[]{:S(2)}) %collective-permute-start.11) | collective-permute-done | bytes 262176 | tf_op jit(solution)/shard_map/ppermute | solution.py:283
  119.8 1.0 add_convert_fusion
  120.9 3.9 %collective-permute-done.10 = bf16[64,2048]{1,0:T(8,128)(2,1)S(1)} collective-permute-done((bf16[64,2048]{1,0:T(8,128)(2,1)S(1)}, bf16[64,2048]{1,0:T(8,128)(2,1)S(1)}, u32[]{:S(2)}, u32[]{:S(2)}) %collective-permute-start.10) | collective-permute-done | bytes 262176 | tf_op jit(solution)/shard_map/ppermute | solution.py:283
  124.9 4.9 %collective-permute-start.12 = (bf16[32,4096]{1,0:T(8,128)(2,1)S(1)}, bf16[32,4096]{1,0:T(8,128)(2,1)S(1)}, u32[]{:S(2)}, u32[]{:S(2)}) collective-permute-start(bf16[32,4096]{1,0:T(8,128)(2,1)S(1)} %get-tuple-element.36), channel_id=1, source_target_pairs={{16,0},{17,1},{18,2},{19,3},{20,4},{21,5},{22,6},{23,7},{24,8},{25... | collective-permute-start | bytes 786440 | tf_op jit(solution)/shard_map/ppermute | solution.py:293
  129.8 3.5 %collective-permute-start.13 = (bf16[32,4096]{1,0:T(8,128)(2,1)S(1)}, bf16[32,4096]{1,0:T(8,128)(2,1)S(1)}, u32[]{:S(2)}, u32[]{:S(2)}) collective-permute-start(bf16[32,4096]{1,0:T(8,128)(2,1)S(1)} %get-tuple-element.35), channel_id=1, source_target_pairs={{16,1},{17,0},{18,3},{19,2},{20,5},{21,4},{22,7},{23,6},{24,9},{25... | collective-permute-start | bytes 786440 | tf_op jit(solution)/shard_map/ppermute | solution.py:293
  133.4 15.0 %dion_factors.1 = (f32[1,512,256]{2,1,0:T(8,128)}, f32[1,512,256]{2,1,0:T(8,128)}) custom-call(s32[3]{0:T(128)S(1)} %copy-done.3, f32[256,768]{1,0:T(8,128)S(1)} %bitcast.15, f32[256,768]{1,0:T(8,128)S(1)} %collective-permute-done.14.other_ref, bf16[256,1024]{1,0:T(8,128)(2,1)S(1)} %bitcast.18, bf16[256,1024]{1,0:T(8,128)(2,1)S(1)} %collective-permute-done.7.x_other_ref, ...), custom_call_target="tpu_custom_call" | custom-call | flops 12884901888 | bytes 4194304 | tf_op jit(solution)/shard_map/dion_factors/pallas_call | solution.py:257
  148.4 0.9 maximum_select_fusion
  (36 shorter events, 3.8 us)
Async XLA Ops:
  0.6 9.5 %copy-start.5 = (bf16[1,32,8192]{2,1,0:T(8,128)(2,1)S(1)}, bf16[1,32,8192]{2,1,0:T(8,128)(2,1)}, u32[]{:S(2)}) copy-start(bf16[1,32,8192]{2,1,0:T(8,128)(2,1)} %param.12) | copy-start | bytes 1572868
  0.6 19.9 %collective-permute-start.1 = (bf16[1,8192,512]{2,1,0:T(8,128)(2,1)}, bf16[1,8192,512]{2,1,0:T(8,128)(2,1)}, u32[]{:S(2)}, u32[]{:S(2)}) collective-permute-start(bf16[1,8192,512]{2,1,0:T(8,128)(2,1)} %w_mine_ref.1), channel_id=1, source_target_pairs={{0,1},{1,0},{2,3},{3,2},{4,5},{5,4},{6,7},{7,6},{8,9},{9,8},{10,11... | collective-permute-start | bytes 25165832 | tf_op jit(solution)/shard_map/ppermute | solution.py:278
  2.0 17.7 %copy-start.4 = (f32[1,512,256]{2,1,0:T(8,128)S(1)}, f32[1,512,256]{2,1,0:T(8,128)}, u32[]{:S(2)}) copy-start(f32[1,512,256]{2,1,0:T(8,128)} %basis_ref.1) | copy-start | bytes 1572868
  10.1 10.5 %collective-permute-start = (bf16[512,512]{1,0:T(8,128)(2,1)}, bf16[512,512]{1,0:T(8,128)(2,1)S(1)}, u32[]{:S(2)}, u32[]{:S(2)}) collective-permute-start(bf16[512,512]{1,0:T(8,128)(2,1)} %attention_backward.1.mine_ref.g_ref), channel_id=1, source_target_pairs={{0,1},{1,0},{2,3},{3,2},{4,5},{5,4},{6,7},{7,6},{8,9},{9,8},{10,11... | collective-permute-start | bytes 1572872 | tf_op jit(solution)/shard_map/ppermute | solution.py:278
  11.5 26.2 %all-to-all-start = ((bf16[8,32,1024]{2,1,0:T(8,128)(2,1)}), bf16[8,32,1024]{2,1,0:T(8,128)(2,1)S(1)}, u32[]{:S(2)}, u32[]{:S(2)}) async-start(bf16[8,32,1024]{2,1,0:T(8,128)(2,1)} %bitcast.13), calls=%async_computation | async-start | bytes 1048576 | tf_op jit(solution)/shard_map/all_to_all | solution.py:287
  19.7 21.1 %copy-start = (bf16[512,512]{1,0:T(8,128)(2,1)S(1)}, bf16[512,512]{1,0:T(8,128)(2,1)}, u32[]{:S(2)}) copy-start(bf16[512,512]{1,0:T(8,128)(2,1)} %attention_backward.1.mine_ref.g_ref) | copy-start | bytes 1572868
  19.8 21.1 %collective-permute-start.6 = (f32[1,512,256]{2,1,0:T(8,128)S(1)}, f32[1,512,256]{2,1,0:T(8,128)S(1)}, u32[]{:S(2)}, u32[]{:S(2)}) collective-permute-start(f32[1,512,256]{2,1,0:T(8,128)S(1)} %copy-done.4), channel_id=1, source_target_pairs={{0,1},{1,0},{2,3},{3,2},{4,5},{5,4},{6,7},{7,6},{8,9},{9,8},{10,11... | collective-permute-start | bytes 1572872 | tf_op jit(solution)/shard_map/ppermute | solution.py:278
  20.6 0.8 copy-start.1
  37.7 3.2 %collective-permute-start.7 = (bf16[256,1024]{1,0:T(8,128)(2,1)S(1)}, bf16[256,1024]{1,0:T(8,128)(2,1)S(1)}, u32[]{:S(2)}, u32[]{:S(2)}) collective-permute-start(bf16[256,1024]{1,0:T(8,128)(2,1)S(1)} %bitcast.16), channel_id=1, source_target_pairs={{0,1},{1,0},{2,3},{3,2},{4,5},{5,4},{6,7},{7,6},{8,9},{9,8},{10,11... | collective-permute-start | bytes 1572872 | tf_op jit(solution)/shard_map/ppermute | solution.py:278
  38.2 17.6 %collective-permute-start.2 = (bf16[64,4096]{1,0:T(8,128)(2,1)}, bf16[64,4096]{1,0:T(8,128)(2,1)S(1)}, u32[]{:S(2)}, u32[]{:S(2)}) collective-permute-start(bf16[64,4096]{1,0:T(8,128)(2,1)} %get-tuple-element.16), channel_id=1, source_target_pairs={{0,2},{1,3},{2,4},{3,5},{4,6},{5,7},{6,8},{7,9},{8,10},{9,11},{10,... | collective-permute-start | bytes 1572872 | tf_op jit(solution)/shard_map/ppermute | solution.py:283
  38.5 17.3 %collective-permute-start.4 = (bf16[64,4096]{1,0:T(8,128)(2,1)}, bf16[64,4096]{1,0:T(8,128)(2,1)}, u32[]{:S(2)}, u32[]{:S(2)}) collective-permute-start(bf16[64,4096]{1,0:T(8,128)(2,1)} %get-tuple-element.18), channel_id=1, source_target_pairs={{0,14},{1,15},{2,0},{3,1},{4,2},{5,3},{6,4},{7,5},{8,6},{9,7},{10,... | collective-permute-start | bytes 1572872 | tf_op jit(solution)/shard_map/ppermute | solution.py:283
  40.9 1.0 copy-start.2
  43.7 27.0 %all-to-all-start.1 = ((f32[8,32,768]{2,1,0:T(8,128)}), f32[8,32,768]{2,1,0:T(8,128)S(1)}, u32[]{:S(2)}, u32[]{:S(2)}) async-start(f32[8,32,768]{2,1,0:T(8,128)} %bitcast.5), calls=%async_computation.1 | async-start | bytes 1572864 | tf_op jit(solution)/shard_map/all_to_all | solution.py:287
  58.2 23.1 %collective-permute-start.3 = (bf16[64,4096]{1,0:T(8,128)(2,1)}, bf16[64,4096]{1,0:T(8,128)(2,1)S(1)}, u32[]{:S(2)}, u32[]{:S(2)}) collective-permute-start(bf16[64,4096]{1,0:T(8,128)(2,1)} %get-tuple-element.34), channel_id=1, source_target_pairs={{0,2},{1,3},{2,4},{3,5},{4,6},{5,7},{6,8},{7,9},{8,10},{9,11},{10,... | collective-permute-start | bytes 1572872 | tf_op jit(solution)/shard_map/ppermute | solution.py:283
  58.2 23.1 %collective-permute-start.5 = (bf16[64,4096]{1,0:T(8,128)(2,1)}, bf16[64,4096]{1,0:T(8,128)(2,1)S(1)}, u32[]{:S(2)}, u32[]{:S(2)}) collective-permute-start(bf16[64,4096]{1,0:T(8,128)(2,1)} %get-tuple-element.33), channel_id=1, source_target_pairs={{0,14},{1,15},{2,0},{3,1},{4,2},{5,3},{6,4},{7,5},{8,6},{9,7},{10,... | collective-permute-start | bytes 1572872 | tf_op jit(solution)/shard_map/ppermute | solution.py:283
  71.7 38.4 %all-to-all-start.2 = ((f32[8,32,768]{2,1,0:T(8,128)}), f32[8,32,768]{2,1,0:T(8,128)S(1)}, u32[]{:S(2)}, u32[]{:S(2)}) async-start(f32[8,32,768]{2,1,0:T(8,128)} %broadcast_in_dim.2), calls=%async_computation.2 | async-start | bytes 1572864 | tf_op jit(solution)/shard_map/all_to_all | solution.py:287
  82.6 26.8 %collective-permute-start.8 = (bf16[64,4096]{1,0:T(8,128)(2,1)S(1)}, bf16[64,4096]{1,0:T(8,128)(2,1)S(1)}, u32[]{:S(2)}, u32[]{:S(2)}) collective-permute-start(bf16[64,4096]{1,0:T(8,128)(2,1)S(1)} %get-tuple-element.32), channel_id=1, source_target_pairs={{0,2},{1,3},{2,4},{3,5},{4,6},{5,7},{6,8},{7,9},{8,10},{9,11},{10,... | collective-permute-start | bytes 1572872 | tf_op jit(solution)/shard_map/ppermute | solution.py:283
  82.8 27.3 %collective-permute-start.9 = (bf16[64,4096]{1,0:T(8,128)(2,1)S(1)}, bf16[64,4096]{1,0:T(8,128)(2,1)}, u32[]{:S(2)}, u32[]{:S(2)}) collective-permute-start(bf16[64,4096]{1,0:T(8,128)(2,1)S(1)} %get-tuple-element.31), channel_id=1, source_target_pairs={{0,14},{1,15},{2,0},{3,1},{4,2},{5,3},{6,4},{7,5},{8,6},{9,7},{10,... | collective-permute-start | bytes 1572872 | tf_op jit(solution)/shard_map/ppermute | solution.py:283
  109.3 0.8 copy-start.6
  110.1 23.2 %copy-start.3 = (s32[3]{0:T(128)S(1)}, s32[3]{0:T(128)}, u32[]{:S(2)}) copy-start(s32[3]{0:T(128)} %pad_add_fusion.info) | copy-start | bytes 40
  112.5 7.4 %collective-permute-start.11 = (bf16[64,2048]{1,0:T(8,128)(2,1)}, bf16[64,2048]{1,0:T(8,128)(2,1)}, u32[]{:S(2)}, u32[]{:S(2)}) collective-permute-start(bf16[64,2048]{1,0:T(8,128)(2,1)} %slice.50), channel_id=1, source_target_pairs={{0,14},{1,15},{2,0},{3,1},{4,2},{5,3},{6,4},{7,5},{8,6},{9,7},{10,... | collective-permute-start | bytes 786440 | tf_op jit(solution)/shard_map/ppermute | solution.py:283
  114.2 19.2 %collective-permute-start.14 = (f32[256,768]{1,0:T(8,128)S(1)}, f32[256,768]{1,0:T(8,128)S(1)}, u32[]{:S(2)}, u32[]{:S(2)}) collective-permute-start(f32[256,768]{1,0:T(8,128)S(1)} %bitcast.14), channel_id=1, source_target_pairs={{0,1},{1,0},{2,3},{3,2},{4,5},{5,4},{6,7},{7,6},{8,9},{9,8},{10,11... | collective-permute-start | bytes 2359304 | tf_op jit(solution)/shard_map/ppermute | solution.py:278
  115.6 9.2 %collective-permute-start.10 = (bf16[64,2048]{1,0:T(8,128)(2,1)S(1)}, bf16[64,2048]{1,0:T(8,128)(2,1)S(1)}, u32[]{:S(2)}, u32[]{:S(2)}) collective-permute-start(bf16[64,2048]{1,0:T(8,128)(2,1)S(1)} %slice.48), channel_id=1, source_target_pairs={{0,2},{1,3},{2,4},{3,5},{4,6},{5,7},{6,8},{7,9},{8,10},{9,11},{10,... | collective-permute-start | bytes 786440 | tf_op jit(solution)/shard_map/ppermute | solution.py:283
  124.9 23.5 %collective-permute-start.12 = (bf16[32,4096]{1,0:T(8,128)(2,1)S(1)}, bf16[32,4096]{1,0:T(8,128)(2,1)S(1)}, u32[]{:S(2)}, u32[]{:S(2)}) collective-permute-start(bf16[32,4096]{1,0:T(8,128)(2,1)S(1)} %get-tuple-element.36), channel_id=1, source_target_pairs={{16,0},{17,1},{18,2},{19,3},{20,4},{21,5},{22,6},{23,7},{24,8},{25... | collective-permute-start | bytes 786440 | tf_op jit(solution)/shard_map/ppermute | solution.py:293
  129.8 18.6 %collective-permute-start.13 = (bf16[32,4096]{1,0:T(8,128)(2,1)S(1)}, bf16[32,4096]{1,0:T(8,128)(2,1)S(1)}, u32[]{:S(2)}, u32[]{:S(2)}) collective-permute-start(bf16[32,4096]{1,0:T(8,128)(2,1)S(1)} %get-tuple-element.35), channel_id=1, source_target_pairs={{16,1},{17,0},{18,3},{19,2},{20,5},{21,4},{22,7},{23,6},{24,9},{25... | collective-permute-start | bytes 786440 | tf_op jit(solution)/shard_map/ppermute | solution.py:293

commit v3 on v2

--- a/solution.py
+++ b/solution.py
@@ -86,9 +86,7 @@
             scratch_shapes=[pltpu.VMEM((tokens, tokens), jnp.float32)] + [pltpu.VMEM((tokens, HD), jnp.float32)] * 2,
         ),
         compiler_params=pltpu.CompilerParams(vmem_limit_bytes=58 << 20),
-        cost_estimate=pl.CostEstimate(
-            flops=heads * 4 * 2 * tokens * tokens * HD, bytes_accessed=4 << 20, transcendentals=heads * tokens * tokens
-        ),
+        cost_estimate=pl.CostEstimate(flops=1 << 20, bytes_accessed=1 << 20, transcendentals=0),
         name="attention_backward",
     )(info, lengths, queries, out_grad, key_rows, value_rows)
 
@@ -141,9 +139,7 @@
             scratch_shapes=[pltpu.VMEM((2, tokens, width), jnp.bfloat16)] * 2,
         ),
         compiler_params=pltpu.CompilerParams(vmem_limit_bytes=56 << 20),
-        cost_estimate=pl.CostEstimate(
-            flops=4 * tokens * width * columns, bytes_accessed=4 * width * columns + (2 << 20), transcendentals=0
-        ),
+        cost_estimate=pl.CostEstimate(flops=1 << 20, bytes_accessed=1 << 20, transcendentals=0),
         name="layer_partial",
     )(info, mine, other, w_mine, w_other)
 
@@ -223,9 +219,9 @@
     return done[:, size:] * (1.0 / jnp.sqrt(jnp.concatenate(pivots, axis=0)))
 
 
-def dion_kernel(info, own_ref, other_ref, x_ref, x_other_ref, g_ref, left_ref, right_ref, work):
+def dion_kernel(own_ref, other_ref, left_ref, right_ref, work):
     rows = own_ref.shape[0]
-    rank = left_ref.shape[2]
+    rank = left_ref.shape[1]
     size = 64
     p = jnp.concatenate([own_ref[:, :rank], other_ref[:, :rank]], axis=0)
     m_own = dot_f32(own_ref[:, rank:], p, ((1,), (0,)), highest)
@@ -243,31 +239,47 @@
         if start + size < rank:
             work[start + size :, :] -= dot_f32(strip[:, start + size : rank], strip, ((0,), (0,)), highest)
     inverse = work[:, rank:]
-    left_mix = dot_f32(p, inverse, ((1,), (1,)), highest) * math.sqrt(D)
-    left_ref[0] = times_exact(x_ref[...], left_mix[:rows]) + times_exact(x_other_ref[...], left_mix[rows:])
-    right_mix = dot_f32(m, inverse, ((1,), (1,)), highest)
-    right_ref[0] = times_exact(g_ref[...], right_mix)
-
-
-def dion_factors(info, own, other, inputs, inputs_other, query_grad, rank):
+    left_ref[...] = dot_f32(p, inverse, ((1,), (1,)), highest) * math.sqrt(D)
+    right_ref[...] = dot_f32(m, inverse, ((1,), (1,)), highest)
+
+
+def dion_mixes(own, other, rank):
+    tokens = 2 * own.shape[0]
+    return pl.pallas_call(
+        dion_kernel,
+        out_shape=[jax.ShapeDtypeStruct((tokens, rank), jnp.float32)] * 2,
+        scratch_shapes=[pltpu.VMEM((rank, 2 * rank), jnp.float32)],
+        compiler_params=pltpu.CompilerParams(vmem_limit_bytes=40 << 20),
+        cost_estimate=pl.CostEstimate(flops=10 << 30, bytes_accessed=4 << 20, transcendentals=0),
+        name="dion_mixes",
+    )(own, other)
+
+
+def factors_kernel(info, left_mix, right_mix, x_ref, x_other_ref, g_ref, left_ref, right_ref):
+    rows = x_ref.shape[0]
+    left_ref[0] = times_exact(x_ref[...], left_mix[:rows, :]) + times_exact(x_other_ref[...], left_mix[rows:, :])
+    right_ref[0] = times_exact(g_ref[...], right_mix[...])
+
+
+def dion_factors(info, left_mix, right_mix, inputs, inputs_other, query_grad):
     tokens, width = query_grad.shape
-    whole = pl.BlockSpec(own.shape, lambda i, info: (0, 0))
+    rank = left_mix.shape[1]
+    mix = pl.BlockSpec((tokens, rank), lambda i, info: (0, 0))
     columns = pl.BlockSpec((tokens // 2, width), lambda i, info: (0, info[1]))
     result = pl.BlockSpec((1, width, rank), lambda i, info: (0, 0, 0))
     return pl.pallas_call(
-        dion_kernel,
+        factors_kernel,
         out_shape=[jax.ShapeDtypeStruct((1, width, rank), jnp.float32)] * 2,
         grid_spec=pltpu.PrefetchScalarGridSpec(
             num_scalar_prefetch=1,
             grid=(1,),
-            in_specs=[whole, whole, columns, columns, pl.BlockSpec((tokens, width), lambda i, info: (0, 0))],
+            in_specs=[mix, mix, columns, columns, pl.BlockSpec((tokens, width), lambda i, info: (0, 0))],
             out_specs=[result, result],
-            scratch_shapes=[pltpu.VMEM((rank, 2 * rank), jnp.float32)],
         ),
         compiler_params=pltpu.CompilerParams(vmem_limit_bytes=40 << 20),
-        cost_estimate=pl.CostEstimate(flops=12 << 30, bytes_accessed=4 << 20, transcendentals=0),
+        cost_estimate=pl.CostEstimate(flops=2 << 30, bytes_accessed=4 << 20, transcendentals=0),
         name="dion_factors",
-    )(info, own, other, inputs, inputs_other, query_grad)
+    )(info, left_mix, right_mix, inputs, inputs_other, query_grad)
 
 
 def after(value, other):
@@ -334,16 +346,19 @@
     half = up.shape[1] // 2
     last_up, last_down = along_z(up[:, :half], 1), along_z(down[:, half:], -1)
 
+    left_mix, right_mix = dion_mixes(gathered, gathered_other, dion_basis.shape[2])
+
     def total(a, b):
         return (a.astype(jnp.float32) + b.astype(jnp.float32)).astype(jnp.bfloat16)
 
+    last_up, last_down = after((last_up, last_down), left_mix)
     summed = jnp.concatenate([total(last_up, down[:, :half]), total(last_down, up[:, half:])], axis=1)
-    left_factor, right_factor = dion_factors(
-        info, gathered, after(gathered_other, summed), own_columns, other_columns, query_grad, dion_basis.shape[2]
-    )
 
     from_own = shift_sections(summed[:CHUNK], 0)
     from_other = shift_sections(summed[CHUNK:], 1)
+    left_factor, right_factor = dion_factors(
+        info, after(left_mix, summed), right_mix, own_columns, other_columns, query_grad
+    )
     from_own, from_other = after((from_own, from_other), left_factor)
     upstream = jnp.where(
         core == 0,

time: 150 us -> 144 us (0.960)
  the two profiles are of different devices: /device:TPU:7 before, /device:TPU:25 now
where the time goes in v3:
time: 144 us; the launch traced here: 143 us
  waiting for transfers between devices  46 us (32%)
  starting transfers between devices  45.7 us (32%)
  Pallas kernels  33.7 us (23%)
  other arithmetic  9.5 us (7%)
  local copies, waits for them, and re-layouts  7.13 us (5%)
    all_to_all x3, waiting for transfers between devices, exchange_z(): lax.all_to_all(value, 'tensor', 0, 0, tiled=True, axis_index_groups=z_gro...  24.2 us
    all_to_all x3, starting transfers between devices, exchange_z(): lax.all_to_all(value, 'tensor', 0, 0, tiled=True, axis_index_groups=z_gro...  20.7 us
    ppermute x8, waiting for transfers between devices, along_z(): lax.ppermute(value, 'tensor', [(i, (i + 2 * steps) % count) for i in rang...  12.5 us
    pallas_call x1, Pallas kernels, dion_mixes(): pl.pallas_call(dion_kernel, out_shape=[jax.ShapeDtypeStruct((tokens, rank...  12 us
    ppermute x8, starting transfers between devices, along_z(): lax.ppermute(value, 'tensor', [(i, (i + 2 * steps) % count) for i in rang...  11.1 us
    pallas_call x1, Pallas kernels, layer_partial(): pl.pallas_call(layer_kernel, out_shape=[jax.ShapeDtypeStruct((count, colu...  9.48 us
    pallas_call x1, Pallas kernels, attention(): pl.pallas_call(attention_kernel, out_shape=jax.ShapeDtypeStruct((tokens,...  7.93 us
    ppermute x2, waiting for transfers between devices, shift_sections(): return lax.ppermute(value, ('section', 'tensor'), pairs)  7.71 us
  transfers between devices with their start and end apart: 18, of which 7 were waited for; matrix products, arithmetic and copies ran while one was open for 7% of the time, Pallas kernels for 24%

profile of v3, /device:TPU:25, one launch (start us, length us, event | category | flops | bytes accessed | tf_op | source)
XLA Modules:
  0.0 142.9 jit_solution(16882320791446013725)
XLA Ops:
  1.4 1.3 copy.12
  2.7 1.1 copy.14
  3.9 8.2 %all-to-all-start = ((bf16[8,32,1024]{2,1,0:T(8,128)(2,1)}), bf16[8,32,1024]{2,1,0:T(8,128)(2,1)S(1)}, u32[]{:S(2)}, u32[]{:S(2)}) async-start(bf16[8,32,1024]{2,1,0:T(8,128)(2,1)} %bitcast.13), calls=%async_computation | async-start | bytes 1048576 | tf_op jit(solution)/shard_map/all_to_all | solution.py:299
  12.7 7.9 %attention_backward.1.mine_ref.g_ref = bf16[512,512]{1,0:T(8,128)(2,1)} custom-call(s32[3]{0:T(128)} %pad_add_fusion.info, s32[1,3]{1,0:T(1,128)} %lens.1, bf16[1,512,512]{2,1,0:T(8,128)(2,1)} %q_ref.1, bf16[1,512,512]{2,1,0:T(8,128)(2,1)} %g_ref.1, bf16[1,512,1024]{2,1,0:T(8,128)(2,1)} %k_ref.1, bf16[1,512,1024]{2,1,0:T(8,128)(2,1)} %v_ref.1), custom_call_target="tpu_custom_call" | custom-call | flops 1048576 | bytes 1048576 | tf_op jit(solution)/shard_map/attention_backward/pallas_call | solution.py:78
  21.1 1.6 %collective-permute-done.other_ref = bf16[512,512]{1,0:T(8,128)(2,1)S(1)} collective-permute-done((bf16[512,512]{1,0:T(8,128)(2,1)}, bf16[512,512]{1,0:T(8,128)(2,1)S(1)}, u32[]{:S(2)}, u32[]{:S(2)}) %collective-permute-start) | collective-permute-done | bytes 524320 | tf_op jit(solution)/shard_map/ppermute | solution.py:290
  23.5 9.5 %layer_partial.1 = (bf16[64,4096]{1,0:T(8,128)(2,1)}, bf16[64,4096]{1,0:T(8,128)(2,1)}, bf16[384,4096]{1,0:T(8,128)(2,1)}) custom-call(s32[3]{0:T(128)} %pad_add_fusion.info, bf16[512,512]{1,0:T(8,128)(2,1)} %attention_backward.1.mine_ref.g_ref, bf16[512,512]{1,0:T(8,128)(2,1)} %copy-done.1, bf16[1,8192,512]{2,1,0:T(8,128)(2,1)} %w_mine_ref.1, ...), custom_call_target="tpu_custom_call" | custom-call | flops 1048576 | bytes 1048576 | tf_op jit(solution)/shard_map/layer_partial/pallas_call | solution.py:131
  33.4 1.7 %collective-permute-start.2 = (bf16[64,4096]{1,0:T(8,128)(2,1)}, bf16[64,4096]{1,0:T(8,128)(2,1)S(1)}, u32[]{:S(2)}, u32[]{:S(2)}) collective-permute-start(bf16[64,4096]{1,0:T(8,128)(2,1)} %get-tuple-element.20), channel_id=1, source_target_pairs={{0,2},{1,3},{2,4},{3,5},{4,6},{5,7},{6,8},{7,9},{8,10},{9,11},{10,... | collective-permute-start | bytes 1572872 | tf_op jit(solution)/shard_map/ppermute | solution.py:295
  35.1 1.2 collective-permute-start.4
  36.4 1.0 copy-done.2
  37.4 1.8 %chip_parts.1 = f32[256,768]{1,0:T(8,128)} custom-call(bf16[512,512]{1,0:T(8,128)(2,1)S(1)} %copy-done, bf16[512,512]{1,0:T(8,128)(2,1)S(1)} %copy-done.2, f32[1,512,256]{2,1,0:T(8,128)S(1)} %copy-done.4, f32[1,512,256]{2,1,0:T(8,128)S(1)} %collective-permute-done.6.basis_other_ref, bf16[256,1024]{1,0:T(8,128)(2,1)S(1)} %bitcast.17, ...), custom_call_target="tpu_custom_call" | custom-call | flops 1073741824 | bytes 4194304 | tf_op jit(solution)/shard_map/chip_parts/pallas_call | solution.py:178
  39.2 6.7 %all-to-all-start.1 = ((f32[8,32,768]{2,1,0:T(8,128)}), f32[8,32,768]{2,1,0:T(8,128)S(1)}, u32[]{:S(2)}, u32[]{:S(2)}) async-start(f32[8,32,768]{2,1,0:T(8,128)} %bitcast.5), calls=%async_computation.1 | async-start | bytes 1572864 | tf_op jit(solution)/shard_map/all_to_all | solution.py:299
  45.8 2.9 %collective-permute-done.2 = bf16[64,4096]{1,0:T(8,128)(2,1)S(1)} collective-permute-done((bf16[64,4096]{1,0:T(8,128)(2,1)}, bf16[64,4096]{1,0:T(8,128)(2,1)S(1)}, u32[]{:S(2)}, u32[]{:S(2)}) %collective-permute-start.2) | collective-permute-done | bytes 524320 | tf_op jit(solution)/shard_map/ppermute | solution.py:295
  48.7 2.4 %slice_add_fusion.4 = (bf16[64,4096]{1,0:T(8,128)(2,1)}, bf16[64,4096]{1,0:T(8,128)(2,1)}) fusion(bf16[64,4096]{1,0:T(8,128)(2,1)} %collective-permute-done.4, bf16[384,4096]{1,0:T(8,128)(2,1)} %get-tuple-element.21, bf16[64,4096]{1,0:T(8,128)(2,1)S(1)} %collective-permute-done.2), kind=kLoop, calls=%fused_computation.13 | loop fusion | flops 524288 | bytes 3145728 | tf_op jit(solution)/shard_map/add | solution.py:345
  52.1 1.7 %collective-permute-start.5 = (bf16[64,4096]{1,0:T(8,128)(2,1)}, bf16[64,4096]{1,0:T(8,128)(2,1)S(1)}, u32[]{:S(2)}, u32[]{:S(2)}) collective-permute-start(bf16[64,4096]{1,0:T(8,128)(2,1)} %get-tuple-element.41), channel_id=1, source_target_pairs={{0,14},{1,15},{2,0},{3,1},{4,2},{5,3},{6,4},{7,5},{8,6},{9,7},{10,... | collective-permute-start | bytes 1572872 | tf_op jit(solution)/shard_map/ppermute | solution.py:295
  53.8 12.3 %all-to-all-done.1 = f32[8,32,768]{2,1,0:T(8,128)S(1)} async-done(((f32[8,32,768]{2,1,0:T(8,128)}), f32[8,32,768]{2,1,0:T(8,128)S(1)}, u32[]{:S(2)}, u32[]{:S(2)}) %all-to-all-start.1) | async-done | bytes 786464 | tf_op jit(solution)/shard_map/all_to_all | solution.py:299
  66.2 1.0 broadcast_in_dim.2
  67.1 5.9 %all-to-all-start.2 = ((f32[8,32,768]{2,1,0:T(8,128)}), f32[8,32,768]{2,1,0:T(8,128)S(1)}, u32[]{:S(2)}, u32[]{:S(2)}) async-start(f32[8,32,768]{2,1,0:T(8,128)} %broadcast_in_dim.2), calls=%async_computation.2 | async-start | bytes 1572864 | tf_op jit(solution)/shard_map/all_to_all | solution.py:299
  73.0 4.0 %collective-permute-done.3 = bf16[64,4096]{1,0:T(8,128)(2,1)S(1)} collective-permute-done((bf16[64,4096]{1,0:T(8,128)(2,1)}, bf16[64,4096]{1,0:T(8,128)(2,1)S(1)}, u32[]{:S(2)}, u32[]{:S(2)}) %collective-permute-start.3) | collective-permute-done | bytes 524320 | tf_op jit(solution)/shard_map/ppermute | solution.py:295
  77.0 2.3 %slice_add_fusion.2 = (bf16[64,4096]{1,0:T(8,128)(2,1)}, bf16[64,4096]{1,0:T(8,128)(2,1)}) fusion(bf16[64,4096]{1,0:T(8,128)(2,1)S(1)} %collective-permute-done.5, bf16[384,4096]{1,0:T(8,128)(2,1)} %get-tuple-element.21, bf16[64,4096]{1,0:T(8,128)(2,1)S(1)} %collective-permute-done.3), kind=kLoop, calls=%fused_computation.11 | loop fusion | flops 524288 | bytes 3145728 | tf_op jit(solution)/shard_map/add | solution.py:345
  79.9 2.1 %collective-permute-start.9 = (bf16[64,4096]{1,0:T(8,128)(2,1)}, bf16[64,4096]{1,0:T(8,128)(2,1)S(1)}, u32[]{:S(2)}, u32[]{:S(2)}) collective-permute-start(bf16[64,4096]{1,0:T(8,128)(2,1)} %get-tuple-element.39), channel_id=1, source_target_pairs={{0,14},{1,15},{2,0},{3,1},{4,2},{5,3},{6,4},{7,5},{8,6},{9,7},{10,... | collective-permute-start | bytes 1572872 | tf_op jit(solution)/shard_map/ppermute | solution.py:295
  81.9 11.9 %all-to-all-done.2 = f32[8,32,768]{2,1,0:T(8,128)S(1)} async-done(((f32[8,32,768]{2,1,0:T(8,128)}), f32[8,32,768]{2,1,0:T(8,128)S(1)}, u32[]{:S(2)}, u32[]{:S(2)}) %all-to-all-start.2) | async-done | bytes 786464 | tf_op jit(solution)/shard_map/all_to_all | solution.py:299
  93.9 5.6 %collective-permute-start.12 = (f32[256,768]{1,0:T(8,128)S(1)}, f32[256,768]{1,0:T(8,128)S(1)}, u32[]{:S(2)}, u32[]{:S(2)}) collective-permute-start(f32[256,768]{1,0:T(8,128)S(1)} %bitcast.14), channel_id=1, source_target_pairs={{0,1},{1,0},{2,3},{3,2},{4,5},{5,4},{6,7},{7,6},{8,9},{9,8},{10,11... | collective-permute-start | bytes 2359304 | tf_op jit(solution)/shard_map/ppermute | solution.py:290
  99.5 5.6 %collective-permute-done.8 = bf16[64,4096]{1,0:T(8,128)(2,1)S(1)} collective-permute-done((bf16[64,4096]{1,0:T(8,128)(2,1)}, bf16[64,4096]{1,0:T(8,128)(2,1)S(1)}, u32[]{:S(2)}, u32[]{:S(2)}) %collective-permute-start.8) | collective-permute-done | bytes 524320 | tf_op jit(solution)/shard_map/ppermute | solution.py:295
  105.1 1.3 slice_add_fusion
  106.6 2.7 %collective-permute-start.11 = (bf16[64,2048]{1,0:T(8,128)(2,1)S(1)}, bf16[64,2048]{1,0:T(8,128)(2,1)S(1)}, u32[]{:S(2)}, u32[]{:S(2)}) collective-permute-start(bf16[64,2048]{1,0:T(8,128)(2,1)S(1)} %slice.49), channel_id=1, source_target_pairs={{0,14},{1,15},{2,0},{3,1},{4,2},{5,3},{6,4},{7,5},{8,6},{9,7},{10,... | collective-permute-start | bytes 786440 | tf_op jit(solution)/shard_map/ppermute | solution.py:295
  109.3 12.0 %dion_mixes.1 = (f32[512,256]{1,0:T(8,128)S(1)}, f32[512,256]{1,0:T(8,128)S(1)}) custom-call(f32[256,768]{1,0:T(8,128)S(1)} %bitcast.15, f32[256,768]{1,0:T(8,128)S(1)} %collective-permute-done.12.other_ref), custom_call_target="tpu_custom_call" | custom-call | flops 10737418240 | bytes 4194304 | tf_op jit(solution)/shard_map/dion_mixes/pallas_call | solution.py:248
  122.9 2.4 %collective-permute-start.13 = (bf16[32,4096]{1,0:T(8,128)(2,1)}, bf16[32,4096]{1,0:T(8,128)(2,1)S(1)}, u32[]{:S(2)}, u32[]{:S(2)}) collective-permute-start(bf16[32,4096]{1,0:T(8,128)(2,1)} %get-tuple-element.44), channel_id=1, source_target_pairs={{16,0},{17,1},{18,2},{19,3},{20,4},{21,5},{22,6},{23,7},{24,8},{25... | collective-permute-start | bytes 786440 | tf_op jit(solution)/shard_map/ppermute | solution.py:305
  125.3 4.2 %collective-permute-start.14 = (bf16[32,4096]{1,0:T(8,128)(2,1)S(1)}, bf16[32,4096]{1,0:T(8,128)(2,1)}, u32[]{:S(2)}, u32[]{:S(2)}) collective-permute-start(bf16[32,4096]{1,0:T(8,128)(2,1)S(1)} %get-tuple-element.43), channel_id=1, source_target_pairs={{16,1},{17,0},{18,3},{19,2},{20,5},{21,4},{22,7},{23,6},{24,9},{25... | collective-permute-start | bytes 786440 | tf_op jit(solution)/shard_map/ppermute | solution.py:305
  129.6 1.0 copy-done.6
  130.6 2.6 %dion_factors.1 = (f32[1,512,256]{2,1,0:T(8,128)}, f32[1,512,256]{2,1,0:T(8,128)}) custom-call(s32[3]{0:T(128)S(1)} %copy-done.3, f32[512,256]{1,0:T(8,128)S(1)} %get-tuple-element.31.left_mix, f32[512,256]{1,0:T(8,128)S(1)} %copy-done.6, bf16[256,1024]{1,0:T(8,128)(2,1)S(1)} %bitcast.18, bf16[256,1024]{1,0:T(8,128)(2,1)S(1)} %collective-permute-done.7.x_other_ref, ...), custom_call_target="tpu_custom_call" | custom-call | flops 2147483648 | bytes 4194304 | tf_op jit(solution)/shard_map/dion_factors/pallas_call | solution.py:270
  133.2 7.7 %collective-permute-done.14 = bf16[32,4096]{1,0:T(8,128)(2,1)} collective-permute-done((bf16[32,4096]{1,0:T(8,128)(2,1)S(1)}, bf16[32,4096]{1,0:T(8,128)(2,1)}, u32[]{:S(2)}, u32[]{:S(2)}) %collective-permute-start.14) | collective-permute-done | bytes 262176 | tf_op jit(solution)/shard_map/ppermute | solution.py:305
  140.9 2.0 %maximum_select_fusion = bf16[1,32,8192]{2,1,0:T(8,128)(2,1)} fusion(bf16[1,32,4096]{2,1,0:T(8,128)(2,1)} %bitcast.8, bf16[1,32,4096]{2,1,0:T(8,128)(2,1)S(1)} %bitcast.21, pred[]{:T(512)S(6)} %eq.5), kind=kLoop, calls=%fused_computation.5 | loop fusion | flops 2359296 | bytes 1048577 | tf_op jit(solution)/shard_map/jit(_where)/select_n | solution.py:363
  (36 shorter events, 6.5 us)
Async XLA Ops:
  0.6 22.1 %collective-permute-start.1 = (bf16[1,8192,512]{2,1,0:T(8,128)(2,1)}, bf16[1,8192,512]{2,1,0:T(8,128)(2,1)}, u32[]{:S(2)}, u32[]{:S(2)}) collective-permute-start(bf16[1,8192,512]{2,1,0:T(8,128)(2,1)} %w_mine_ref.1), channel_id=1, source_target_pairs={{0,1},{1,0},{2,3},{3,2},{4,5},{5,4},{6,7},{7,6},{8,9},{9,8},{10,11... | collective-permute-start | bytes 25165832 | tf_op jit(solution)/shard_map/ppermute | solution.py:290
  2.7 18.2 %copy-start.4 = (f32[1,512,256]{2,1,0:T(8,128)S(1)}, f32[1,512,256]{2,1,0:T(8,128)}, u32[]{:S(2)}) copy-start(f32[1,512,256]{2,1,0:T(8,128)} %basis_ref.1) | copy-start | bytes 1572868
  3.9 29.2 %all-to-all-start = ((bf16[8,32,1024]{2,1,0:T(8,128)(2,1)}), bf16[8,32,1024]{2,1,0:T(8,128)(2,1)S(1)}, u32[]{:S(2)}, u32[]{:S(2)}) async-start(bf16[8,32,1024]{2,1,0:T(8,128)(2,1)} %bitcast.13), calls=%async_computation | async-start | bytes 1048576 | tf_op jit(solution)/shard_map/all_to_all | solution.py:299
  20.6 15.7 %copy-start = (bf16[512,512]{1,0:T(8,128)(2,1)S(1)}, bf16[512,512]{1,0:T(8,128)(2,1)}, u32[]{:S(2)}) copy-start(bf16[512,512]{1,0:T(8,128)(2,1)} %attention_backward.1.mine_ref.g_ref) | copy-start | bytes 1572868
  20.6 2.1 %collective-permute-start = (bf16[512,512]{1,0:T(8,128)(2,1)}, bf16[512,512]{1,0:T(8,128)(2,1)S(1)}, u32[]{:S(2)}, u32[]{:S(2)}) collective-permute-start(bf16[512,512]{1,0:T(8,128)(2,1)} %attention_backward.1.mine_ref.g_ref), channel_id=1, source_target_pairs={{0,1},{1,0},{2,3},{3,2},{4,5},{5,4},{6,7},{7,6},{8,9},{9,8},{10,11... | collective-permute-start | bytes 1572872 | tf_op jit(solution)/shard_map/ppermute | solution.py:290
  20.9 15.4 %collective-permute-start.6 = (f32[1,512,256]{2,1,0:T(8,128)S(1)}, f32[1,512,256]{2,1,0:T(8,128)S(1)}, u32[]{:S(2)}, u32[]{:S(2)}) collective-permute-start(f32[1,512,256]{2,1,0:T(8,128)S(1)} %copy-done.4), channel_id=1, source_target_pairs={{0,1},{1,0},{2,3},{3,2},{4,5},{5,4},{6,7},{7,6},{8,9},{9,8},{10,11... | collective-permute-start | bytes 1572872 | tf_op jit(solution)/shard_map/ppermute | solution.py:290
  22.7 0.8 copy-start.1
  33.0 3.3 %collective-permute-start.7 = (bf16[256,1024]{1,0:T(8,128)(2,1)S(1)}, bf16[256,1024]{1,0:T(8,128)(2,1)S(1)}, u32[]{:S(2)}, u32[]{:S(2)}) collective-permute-start(bf16[256,1024]{1,0:T(8,128)(2,1)S(1)} %bitcast.16), channel_id=1, source_target_pairs={{0,1},{1,0},{2,3},{3,2},{4,5},{5,4},{6,7},{7,6},{8,9},{9,8},{10,11... | collective-permute-start | bytes 1572872 | tf_op jit(solution)/shard_map/ppermute | solution.py:290
  33.4 15.3 %collective-permute-start.2 = (bf16[64,4096]{1,0:T(8,128)(2,1)}, bf16[64,4096]{1,0:T(8,128)(2,1)S(1)}, u32[]{:S(2)}, u32[]{:S(2)}) collective-permute-start(bf16[64,4096]{1,0:T(8,128)(2,1)} %get-tuple-element.20), channel_id=1, source_target_pairs={{0,2},{1,3},{2,4},{3,5},{4,6},{5,7},{6,8},{7,9},{8,10},{9,11},{10,... | collective-permute-start | bytes 1572872 | tf_op jit(solution)/shard_map/ppermute | solution.py:295
  35.1 13.6 %collective-permute-start.4 = (bf16[64,4096]{1,0:T(8,128)(2,1)}, bf16[64,4096]{1,0:T(8,128)(2,1)}, u32[]{:S(2)}, u32[]{:S(2)}) collective-permute-start(bf16[64,4096]{1,0:T(8,128)(2,1)} %get-tuple-element.22), channel_id=1, source_target_pairs={{0,14},{1,15},{2,0},{3,1},{4,2},{5,3},{6,4},{7,5},{8,6},{9,7},{10,... | collective-permute-start | bytes 1572872 | tf_op jit(solution)/shard_map/ppermute | solution.py:295
  36.4 1.0 copy-start.2
  39.2 26.9 %all-to-all-start.1 = ((f32[8,32,768]{2,1,0:T(8,128)}), f32[8,32,768]{2,1,0:T(8,128)S(1)}, u32[]{:S(2)}, u32[]{:S(2)}) async-start(f32[8,32,768]{2,1,0:T(8,128)} %bitcast.5), calls=%async_computation.1 | async-start | bytes 1572864 | tf_op jit(solution)/shard_map/all_to_all | solution.py:299
  51.2 25.8 %collective-permute-start.3 = (bf16[64,4096]{1,0:T(8,128)(2,1)}, bf16[64,4096]{1,0:T(8,128)(2,1)S(1)}, u32[]{:S(2)}, u32[]{:S(2)}) collective-permute-start(bf16[64,4096]{1,0:T(8,128)(2,1)} %get-tuple-element.42), channel_id=1, source_target_pairs={{0,2},{1,3},{2,4},{3,5},{4,6},{5,7},{6,8},{7,9},{8,10},{9,11},{10,... | collective-permute-start | bytes 1572872 | tf_op jit(solution)/shard_map/ppermute | solution.py:295
  52.1 24.9 %collective-permute-start.5 = (bf16[64,4096]{1,0:T(8,128)(2,1)}, bf16[64,4096]{1,0:T(8,128)(2,1)S(1)}, u32[]{:S(2)}, u32[]{:S(2)}) collective-permute-start(bf16[64,4096]{1,0:T(8,128)(2,1)} %get-tuple-element.41), channel_id=1, source_target_pairs={{0,14},{1,15},{2,0},{3,1},{4,2},{5,3},{6,4},{7,5},{8,6},{9,7},{10,... | collective-permute-start | bytes 1572872 | tf_op jit(solution)/shard_map/ppermute | solution.py:295
  67.1 26.7 %all-to-all-start.2 = ((f32[8,32,768]{2,1,0:T(8,128)}), f32[8,32,768]{2,1,0:T(8,128)S(1)}, u32[]{:S(2)}, u32[]{:S(2)}) async-start(f32[8,32,768]{2,1,0:T(8,128)} %broadcast_in_dim.2), calls=%async_computation.2 | async-start | bytes 1572864 | tf_op jit(solution)/shard_map/all_to_all | solution.py:299
  79.3 25.8 %collective-permute-start.8 = (bf16[64,4096]{1,0:T(8,128)(2,1)}, bf16[64,4096]{1,0:T(8,128)(2,1)S(1)}, u32[]{:S(2)}, u32[]{:S(2)}) collective-permute-start(bf16[64,4096]{1,0:T(8,128)(2,1)} %get-tuple-element.40), channel_id=1, source_target_pairs={{0,2},{1,3},{2,4},{3,5},{4,6},{5,7},{6,8},{7,9},{8,10},{9,11},{10,... | collective-permute-start | bytes 1572872 | tf_op jit(solution)/shard_map/ppermute | solution.py:295
  79.9 25.2 %collective-permute-start.9 = (bf16[64,4096]{1,0:T(8,128)(2,1)}, bf16[64,4096]{1,0:T(8,128)(2,1)S(1)}, u32[]{:S(2)}, u32[]{:S(2)}) collective-permute-start(bf16[64,4096]{1,0:T(8,128)(2,1)} %get-tuple-element.39), channel_id=1, source_target_pairs={{0,14},{1,15},{2,0},{3,1},{4,2},{5,3},{6,4},{7,5},{8,6},{9,7},{10,... | collective-permute-start | bytes 1572872 | tf_op jit(solution)/shard_map/ppermute | solution.py:295
  93.9 15.4 %collective-permute-start.12 = (f32[256,768]{1,0:T(8,128)S(1)}, f32[256,768]{1,0:T(8,128)S(1)}, u32[]{:S(2)}, u32[]{:S(2)}) collective-permute-start(f32[256,768]{1,0:T(8,128)S(1)} %bitcast.14), channel_id=1, source_target_pairs={{0,1},{1,0},{2,3},{3,2},{4,5},{5,4},{6,7},{7,6},{8,9},{9,8},{10,11... | collective-permute-start | bytes 2359304 | tf_op jit(solution)/shard_map/ppermute | solution.py:290
  106.4 15.6 %collective-permute-start.10 = (bf16[64,2048]{1,0:T(8,128)(2,1)S(1)}, bf16[64,2048]{1,0:T(8,128)(2,1)S(1)}, u32[]{:S(2)}, u32[]{:S(2)}) collective-permute-start(bf16[64,2048]{1,0:T(8,128)(2,1)S(1)} %slice.48), channel_id=1, source_target_pairs={{0,2},{1,3},{2,4},{3,5},{4,6},{5,7},{6,8},{7,9},{8,10},{9,11},{10,... | collective-permute-start | bytes 786440 | tf_op jit(solution)/shard_map/ppermute | solution.py:295
  106.6 23.0 %copy-start.3 = (s32[3]{0:T(128)S(1)}, s32[3]{0:T(128)}, u32[]{:S(2)}) copy-start(s32[3]{0:T(128)} %pad_add_fusion.info) | copy-start | bytes 40
  106.6 15.5 %collective-permute-start.11 = (bf16[64,2048]{1,0:T(8,128)(2,1)S(1)}, bf16[64,2048]{1,0:T(8,128)(2,1)S(1)}, u32[]{:S(2)}, u32[]{:S(2)}) collective-permute-start(bf16[64,2048]{1,0:T(8,128)(2,1)S(1)} %slice.49), channel_id=1, source_target_pairs={{0,14},{1,15},{2,0},{3,1},{4,2},{5,3},{6,4},{7,5},{8,6},{9,7},{10,... | collective-permute-start | bytes 786440 | tf_op jit(solution)/shard_map/ppermute | solution.py:295
  121.3 0.8 copy-start.5
  122.9 10.3 %collective-permute-start.13 = (bf16[32,4096]{1,0:T(8,128)(2,1)}, bf16[32,4096]{1,0:T(8,128)(2,1)S(1)}, u32[]{:S(2)}, u32[]{:S(2)}) collective-permute-start(bf16[32,4096]{1,0:T(8,128)(2,1)} %get-tuple-element.44), channel_id=1, source_target_pairs={{16,0},{17,1},{18,2},{19,3},{20,4},{21,5},{22,6},{23,7},{24,8},{25... | collective-permute-start | bytes 786440 | tf_op jit(solution)/shard_map/ppermute | solution.py:305
  125.3 15.6 %collective-permute-start.14 = (bf16[32,4096]{1,0:T(8,128)(2,1)S(1)}, bf16[32,4096]{1,0:T(8,128)(2,1)}, u32[]{:S(2)}, u32[]{:S(2)}) collective-permute-start(bf16[32,4096]{1,0:T(8,128)(2,1)S(1)} %get-tuple-element.43), channel_id=1, source_target_pairs={{16,1},{17,0},{18,3},{19,2},{20,5},{21,4},{22,7},{23,6},{24,9},{25... | collective-permute-start | bytes 786440 | tf_op jit(solution)/shard_map/ppermute | solution.py:305
  129.6 1.0 copy-start.6

commit v4 on v3

--- a/solution.py
+++ b/solution.py
@@ -219,40 +219,63 @@
     return done[:, size:] * (1.0 / jnp.sqrt(jnp.concatenate(pivots, axis=0)))
 
 
-def dion_kernel(own_ref, other_ref, left_ref, right_ref, work):
-    rows = own_ref.shape[0]
-    rank = left_ref.shape[1]
-    size = 64
+def eliminate(work, starts):
+    rank, size = work.shape[0], 64
+    for start in starts:
+        here = slice(start, start + size)
+        strip = dot_f32(lower_inverse(work[here, here]), work[here, :], ((1,), (0,)), highest)
+        work[here, :] = strip
+        if start + size < rank:
+            work[start + size :, :] -= dot_f32(strip[:, start + size : rank], strip, ((0,), (0,)), highest)
+
+
+def gram_kernel(own_ref, other_ref, mixed_ref, work):
+    rows, rank = own_ref.shape[0], mixed_ref.shape[1]
     p = jnp.concatenate([own_ref[:, :rank], other_ref[:, :rank]], axis=0)
     m_own = dot_f32(own_ref[:, rank:], p, ((1,), (0,)), highest)
     m_other = dot_f32(other_ref[:, rank + rows :], p[:rows], ((1,), (0,)), highest)
     m_other += dot_f32(other_ref[:, rank : rank + rows], p[rows:], ((1,), (0,)), highest)
     m = jnp.concatenate([m_own, m_other], axis=0)
+    mixed_ref[...] = m
     work[:, :rank] = dot_f32(p, m, ((0,), (0,)), highest)
     row_ids = lax.broadcasted_iota(jnp.int32, (rank, rank), 0)
     col_ids = lax.broadcasted_iota(jnp.int32, (rank, rank), 1)
     work[:, rank:] = (row_ids == col_ids).astype(jnp.float32)
-    for start in range(0, rank, size):
-        here = slice(start, start + size)
-        strip = dot_f32(lower_inverse(work[here, here]), work[here, :], ((1,), (0,)), highest)
-        work[here, :] = strip
-        if start + size < rank:
-            work[start + size :, :] -= dot_f32(strip[:, start + size : rank], strip, ((0,), (0,)), highest)
+    eliminate(work, (0, 64))
+
+
+def dion_gram(own, other, rank):
+    return pl.pallas_call(
+        gram_kernel,
+        out_shape=[
+            jax.ShapeDtypeStruct((2 * own.shape[0], rank), jnp.float32),
+            jax.ShapeDtypeStruct((rank, 2 * rank), jnp.float32),
+        ],
+        compiler_params=pltpu.CompilerParams(vmem_limit_bytes=40 << 20),
+        cost_estimate=pl.CostEstimate(flops=5 << 30, bytes_accessed=4 << 20, transcendentals=0),
+        name="dion_gram",
+    )(own, other)
+
+
+def mixes_kernel(own_ref, other_ref, mixed_ref, half_ref, left_ref, right_ref, work):
+    rows, rank = own_ref.shape[0], mixed_ref.shape[1]
+    work[...] = half_ref[...]
+    eliminate(work, (128, 192))
     inverse = work[:, rank:]
-    left_ref[...] = dot_f32(p, inverse, ((1,), (1,)), highest) * math.sqrt(D)
-    right_ref[...] = dot_f32(m, inverse, ((1,), (1,)), highest)
-
-
-def dion_mixes(own, other, rank):
-    tokens = 2 * own.shape[0]
-    return pl.pallas_call(
-        dion_kernel,
-        out_shape=[jax.ShapeDtypeStruct((tokens, rank), jnp.float32)] * 2,
-        scratch_shapes=[pltpu.VMEM((rank, 2 * rank), jnp.float32)],
+    left_ref[:rows, :] = dot_f32(own_ref[:, :rank], inverse, ((1,), (1,)), highest) * math.sqrt(D)
+    left_ref[rows:, :] = dot_f32(other_ref[:, :rank], inverse, ((1,), (1,)), highest) * math.sqrt(D)
+    right_ref[...] = dot_f32(mixed_ref[...], inverse, ((1,), (1,)), highest)
+
+
+def dion_mixes(own, other, mixed, half):
+    return pl.pallas_call(
+        mixes_kernel,
+        out_shape=[jax.ShapeDtypeStruct(mixed.shape, jnp.float32)] * 2,
+        scratch_shapes=[pltpu.VMEM(half.shape, jnp.float32)],
         compiler_params=pltpu.CompilerParams(vmem_limit_bytes=40 << 20),
-        cost_estimate=pl.CostEstimate(flops=10 << 30, bytes_accessed=4 << 20, transcendentals=0),
+        cost_estimate=pl.CostEstimate(flops=5 << 30, bytes_accessed=4 << 20, transcendentals=0),
         name="dion_mixes",
-    )(own, other)
+    )(own, other, mixed, half)
 
 
 def factors_kernel(info, left_mix, right_mix, x_ref, x_other_ref, g_ref, left_ref, right_ref):
@@ -346,19 +369,18 @@
     half = up.shape[1] // 2
     last_up, last_down = along_z(up[:, :half], 1), along_z(down[:, half:], -1)
 
-    left_mix, right_mix = dion_mixes(gathered, gathered_other, dion_basis.shape[2])
+    mixed, eliminated = dion_gram(gathered, gathered_other, dion_basis.shape[2])
 
     def total(a, b):
         return (a.astype(jnp.float32) + b.astype(jnp.float32)).astype(jnp.bfloat16)
 
-    last_up, last_down = after((last_up, last_down), left_mix)
+    last_up, last_down = after((last_up, last_down), eliminated)
     summed = jnp.concatenate([total(last_up, down[:, :half]), total(last_down, up[:, half:])], axis=1)
 
     from_own = shift_sections(summed[:CHUNK], 0)
     from_other = shift_sections(summed[CHUNK:], 1)
-    left_factor, right_factor = dion_factors(
-        info, after(left_mix, summed), right_mix, own_columns, other_columns, query_grad
-    )
+    left_mix, right_mix = dion_mixes(gathered, gathered_other, after(mixed, summed), eliminated)
+    left_factor, right_factor = dion_factors(info, left_mix, right_mix, own_columns, other_columns, query_grad)
     from_own, from_other = after((from_own, from_other), left_factor)
     upstream = jnp.where(
         core == 0,

time: 144 us -> 135 us (0.938)
  the two profiles are of different devices: /device:TPU:25 before, /device:TPU:7 now
where the time goes in v4:
time: 135 us
  starting transfers between devices  49.1 us (36%)
  waiting for transfers between devices  38 us (28%)
  Pallas kernels  33.8 us (25%)
  other arithmetic  7.73 us (6%)
  local copies, waits for them, and re-layouts  5.3 us (4%)
    all_to_all x3, waiting for transfers between devices, exchange_z(): lax.all_to_all(value, 'tensor', 0, 0, tiled=True, axis_index_groups=z_gro...  24 us
    all_to_all x3, starting transfers between devices, exchange_z(): lax.all_to_all(value, 'tensor', 0, 0, tiled=True, axis_index_groups=z_gro...  20.8 us
    ppermute x8, waiting for transfers between devices, along_z(): lax.ppermute(value, 'tensor', [(i, (i + 2 * steps) % count) for i in rang...  12.5 us
    ppermute x8, starting transfers between devices, along_z(): lax.ppermute(value, 'tensor', [(i, (i + 2 * steps) % count) for i in rang...  11.1 us
    ppermute x2, starting transfers between devices, shift_sections(): return lax.ppermute(value, ('section', 'tensor'), pairs)  9.67 us
    pallas_call x1, Pallas kernels, layer_partial(): pl.pallas_call(layer_kernel, out_shape=[jax.ShapeDtypeStruct((count, colu...  9.47 us
    pallas_call x1, Pallas kernels, attention(): pl.pallas_call(attention_kernel, out_shape=jax.ShapeDtypeStruct((tokens,...  7.93 us
    ppermute x5, starting transfers between devices, swap_cores(): return lax.ppermute(value, 'tensor', [(i, i ^ 1) for i in range(2 * ZN)])  7.46 us
  transfers between devices with their start and end apart: 18, of which 6 were waited for; matrix products, arithmetic and copies ran while one was open for 7% of the time, Pallas kernels for 25%

profile of v4, /device:TPU:7, one launch (start us, length us, event | category | flops | bytes accessed | tf_op | source)
XLA Modules:
  0.0 134.8 jit_solution(8531808197648402047)
XLA Ops:
  1.4 1.3 copy.12
  2.7 1.1 copy.14
  3.9 8.2 %all-to-all-start = ((bf16[8,32,1024]{2,1,0:T(8,128)(2,1)}), bf16[8,32,1024]{2,1,0:T(8,128)(2,1)S(1)}, u32[]{:S(2)}, u32[]{:S(2)}) async-start(bf16[8,32,1024]{2,1,0:T(8,128)(2,1)} %bitcast.13), calls=%async_computation | async-start | bytes 1048576 | tf_op jit(solution)/shard_map/all_to_all | solution.py:322
  12.6 7.9 %attention_backward.1.mine_ref.g_ref = bf16[512,512]{1,0:T(8,128)(2,1)} custom-call(s32[3]{0:T(128)} %pad_add_fusion.info, s32[1,3]{1,0:T(1,128)} %lens.1, bf16[1,512,512]{2,1,0:T(8,128)(2,1)} %q_ref.1, bf16[1,512,512]{2,1,0:T(8,128)(2,1)} %g_ref.1, bf16[1,512,1024]{2,1,0:T(8,128)(2,1)} %k_ref.1, bf16[1,512,1024]{2,1,0:T(8,128)(2,1)} %v_ref.1), custom_call_target="tpu_custom_call" | custom-call | flops 1048576 | bytes 1048576 | tf_op jit(solution)/shard_map/attention_backward/pallas_call | solution.py:78
  21.1 1.6 %collective-permute-done.other_ref = bf16[512,512]{1,0:T(8,128)(2,1)S(1)} collective-permute-done((bf16[512,512]{1,0:T(8,128)(2,1)}, bf16[512,512]{1,0:T(8,128)(2,1)S(1)}, u32[]{:S(2)}, u32[]{:S(2)}) %collective-permute-start) | collective-permute-done | bytes 524320 | tf_op jit(solution)/shard_map/ppermute | solution.py:313
  23.5 9.5 %layer_partial.1 = (bf16[64,4096]{1,0:T(8,128)(2,1)}, bf16[64,4096]{1,0:T(8,128)(2,1)}, bf16[384,4096]{1,0:T(8,128)(2,1)}) custom-call(s32[3]{0:T(128)} %pad_add_fusion.info, bf16[512,512]{1,0:T(8,128)(2,1)} %attention_backward.1.mine_ref.g_ref, bf16[512,512]{1,0:T(8,128)(2,1)} %copy-done.1, bf16[1,8192,512]{2,1,0:T(8,128)(2,1)} %w_mine_ref.1, ...), custom_call_target="tpu_custom_call" | custom-call | flops 1048576 | bytes 1048576 | tf_op jit(solution)/shard_map/layer_partial/pallas_call | solution.py:131
  33.3 1.7 %collective-permute-start.2 = (bf16[64,4096]{1,0:T(8,128)(2,1)}, bf16[64,4096]{1,0:T(8,128)(2,1)S(1)}, u32[]{:S(2)}, u32[]{:S(2)}) collective-permute-start(bf16[64,4096]{1,0:T(8,128)(2,1)} %get-tuple-element.22), channel_id=1, source_target_pairs={{0,2},{1,3},{2,4},{3,5},{4,6},{5,7},{6,8},{7,9},{8,10},{9,11},{10,... | collective-permute-start | bytes 1572872 | tf_op jit(solution)/shard_map/ppermute | solution.py:318
  35.1 1.2 collective-permute-start.4
  36.3 1.0 copy-done.2
  37.4 1.8 %chip_parts.1 = f32[256,768]{1,0:T(8,128)} custom-call(bf16[512,512]{1,0:T(8,128)(2,1)S(1)} %copy-done, bf16[512,512]{1,0:T(8,128)(2,1)S(1)} %copy-done.2, f32[1,512,256]{2,1,0:T(8,128)S(1)} %copy-done.4, f32[1,512,256]{2,1,0:T(8,128)S(1)} %collective-permute-done.6.basis_other_ref, bf16[256,1024]{1,0:T(8,128)(2,1)S(1)} %bitcast.18, ...), custom_call_target="tpu_custom_call" | custom-call | flops 1073741824 | bytes 4194304 | tf_op jit(solution)/shard_map/chip_parts/pallas_call | solution.py:178
  39.1 6.7 %all-to-all-start.1 = ((f32[8,32,768]{2,1,0:T(8,128)}), f32[8,32,768]{2,1,0:T(8,128)S(1)}, u32[]{:S(2)}, u32[]{:S(2)}) async-start(f32[8,32,768]{2,1,0:T(8,128)} %bitcast.5), calls=%async_computation.1 | async-start | bytes 1572864 | tf_op jit(solution)/shard_map/all_to_all | solution.py:322
  45.8 2.9 %collective-permute-done.2 = bf16[64,4096]{1,0:T(8,128)(2,1)S(1)} collective-permute-done((bf16[64,4096]{1,0:T(8,128)(2,1)}, bf16[64,4096]{1,0:T(8,128)(2,1)S(1)}, u32[]{:S(2)}, u32[]{:S(2)}) %collective-permute-start.2) | collective-permute-done | bytes 524320 | tf_op jit(solution)/shard_map/ppermute | solution.py:318
  48.7 2.4 %slice_add_fusion.4 = (bf16[64,4096]{1,0:T(8,128)(2,1)}, bf16[64,4096]{1,0:T(8,128)(2,1)}) fusion(bf16[64,4096]{1,0:T(8,128)(2,1)} %collective-permute-done.4, bf16[384,4096]{1,0:T(8,128)(2,1)} %get-tuple-element.23, bf16[64,4096]{1,0:T(8,128)(2,1)S(1)} %collective-permute-done.2), kind=kLoop, calls=%fused_computation.13 | loop fusion | flops 524288 | bytes 3145728 | tf_op jit(solution)/shard_map/add | solution.py:368
  51.1 1.0 collective-permute-start.3
  52.1 1.7 %collective-permute-start.5 = (bf16[64,4096]{1,0:T(8,128)(2,1)}, bf16[64,4096]{1,0:T(8,128)(2,1)S(1)}, u32[]{:S(2)}, u32[]{:S(2)}) collective-permute-start(bf16[64,4096]{1,0:T(8,128)(2,1)} %get-tuple-element.45), channel_id=1, source_target_pairs={{0,14},{1,15},{2,0},{3,1},{4,2},{5,3},{6,4},{7,5},{8,6},{9,7},{10,... | collective-permute-start | bytes 1572872 | tf_op jit(solution)/shard_map/ppermute | solution.py:318
  53.8 12.2 %all-to-all-done.1 = f32[8,32,768]{2,1,0:T(8,128)S(1)} async-done(((f32[8,32,768]{2,1,0:T(8,128)}), f32[8,32,768]{2,1,0:T(8,128)S(1)}, u32[]{:S(2)}, u32[]{:S(2)}) %all-to-all-start.1) | async-done | bytes 786464 | tf_op jit(solution)/shard_map/all_to_all | solution.py:322
  66.0 1.0 broadcast_in_dim.2
  67.0 6.0 %all-to-all-start.2 = ((f32[8,32,768]{2,1,0:T(8,128)}), f32[8,32,768]{2,1,0:T(8,128)S(1)}, u32[]{:S(2)}, u32[]{:S(2)}) async-start(f32[8,32,768]{2,1,0:T(8,128)} %broadcast_in_dim.2), calls=%async_computation.2 | async-start | bytes 1572864 | tf_op jit(solution)/shard_map/all_to_all | solution.py:322
  72.9 4.0 %collective-permute-done.3 = bf16[64,4096]{1,0:T(8,128)(2,1)S(1)} collective-permute-done((bf16[64,4096]{1,0:T(8,128)(2,1)}, bf16[64,4096]{1,0:T(8,128)(2,1)S(1)}, u32[]{:S(2)}, u32[]{:S(2)}) %collective-permute-start.3) | collective-permute-done | bytes 524320 | tf_op jit(solution)/shard_map/ppermute | solution.py:318
  76.9 2.3 %slice_add_fusion.2 = (bf16[64,4096]{1,0:T(8,128)(2,1)}, bf16[64,4096]{1,0:T(8,128)(2,1)}) fusion(bf16[64,4096]{1,0:T(8,128)(2,1)S(1)} %collective-permute-done.5, bf16[384,4096]{1,0:T(8,128)(2,1)} %get-tuple-element.23, bf16[64,4096]{1,0:T(8,128)(2,1)S(1)} %collective-permute-done.3), kind=kLoop, calls=%fused_computation.11 | loop fusion | flops 524288 | bytes 3145728 | tf_op jit(solution)/shard_map/add | solution.py:368
  79.8 2.0 %collective-permute-start.9 = (bf16[64,4096]{1,0:T(8,128)(2,1)}, bf16[64,4096]{1,0:T(8,128)(2,1)S(1)}, u32[]{:S(2)}, u32[]{:S(2)}) collective-permute-start(bf16[64,4096]{1,0:T(8,128)(2,1)} %get-tuple-element.43), channel_id=1, source_target_pairs={{0,14},{1,15},{2,0},{3,1},{4,2},{5,3},{6,4},{7,5},{8,6},{9,7},{10,... | collective-permute-start | bytes 1572872 | tf_op jit(solution)/shard_map/ppermute | solution.py:318
  81.9 11.8 %all-to-all-done.2 = f32[8,32,768]{2,1,0:T(8,128)S(1)} async-done(((f32[8,32,768]{2,1,0:T(8,128)}), f32[8,32,768]{2,1,0:T(8,128)S(1)}, u32[]{:S(2)}, u32[]{:S(2)}) %all-to-all-start.2) | async-done | bytes 786464 | tf_op jit(solution)/shard_map/all_to_all | solution.py:322
  93.6 5.8 %collective-permute-start.12 = (f32[256,768]{1,0:T(8,128)S(1)}, f32[256,768]{1,0:T(8,128)S(1)}, u32[]{:S(2)}, u32[]{:S(2)}) collective-permute-start(f32[256,768]{1,0:T(8,128)S(1)} %bitcast.14), channel_id=1, source_target_pairs={{0,1},{1,0},{2,3},{3,2},{4,5},{5,4},{6,7},{7,6},{8,9},{9,8},{10,11... | collective-permute-start | bytes 2359304 | tf_op jit(solution)/shard_map/ppermute | solution.py:313
  99.5 5.6 %collective-permute-done.8 = bf16[64,4096]{1,0:T(8,128)(2,1)S(1)} collective-permute-done((bf16[64,4096]{1,0:T(8,128)(2,1)}, bf16[64,4096]{1,0:T(8,128)(2,1)S(1)}, u32[]{:S(2)}, u32[]{:S(2)}) %collective-permute-start.8) | collective-permute-done | bytes 524320 | tf_op jit(solution)/shard_map/ppermute | solution.py:318
  105.0 1.3 slice_add_fusion
  106.5 2.7 %collective-permute-start.11 = (bf16[64,2048]{1,0:T(8,128)(2,1)S(1)}, bf16[64,2048]{1,0:T(8,128)(2,1)S(1)}, u32[]{:S(2)}, u32[]{:S(2)}) collective-permute-start(bf16[64,2048]{1,0:T(8,128)(2,1)S(1)} %slice.49), channel_id=1, source_target_pairs={{0,14},{1,15},{2,0},{3,1},{4,2},{5,3},{6,4},{7,5},{8,6},{9,7},{10,... | collective-permute-start | bytes 786440 | tf_op jit(solution)/shard_map/ppermute | solution.py:318
  109.2 6.7 %dion_gram.1 = (f32[512,256]{1,0:T(8,128)S(1)}, f32[256,512]{1,0:T(8,128)S(1)}) custom-call(f32[256,768]{1,0:T(8,128)S(1)} %bitcast.15, f32[256,768]{1,0:T(8,128)S(1)} %collective-permute-done.12.other_ref), custom_call_target="tpu_custom_call" | custom-call | flops 5368709120 | bytes 4194304 | tf_op jit(solution)/shard_map/dion_gram/pallas_call | solution.py:248
  116.2 4.9 %collective-permute-start.13 = (bf16[32,4096]{1,0:T(8,128)(2,1)S(1)}, bf16[32,4096]{1,0:T(8,128)(2,1)S(1)}, u32[]{:S(2)}, u32[]{:S(2)}) collective-permute-start(bf16[32,4096]{1,0:T(8,128)(2,1)S(1)} %get-tuple-element.48), channel_id=1, source_target_pairs={{16,0},{17,1},{18,2},{19,3},{20,4},{21,5},{22,6},{23,7},{24,8},{25... | collective-permute-start | bytes 786440 | tf_op jit(solution)/shard_map/ppermute | solution.py:328
  121.1 4.8 %collective-permute-start.14 = (bf16[32,4096]{1,0:T(8,128)(2,1)S(1)}, bf16[32,4096]{1,0:T(8,128)(2,1)S(1)}, u32[]{:S(2)}, u32[]{:S(2)}) collective-permute-start(bf16[32,4096]{1,0:T(8,128)(2,1)S(1)} %get-tuple-element.47), channel_id=1, source_target_pairs={{16,1},{17,0},{18,3},{19,2},{20,5},{21,4},{22,7},{23,6},{24,9},{25... | collective-permute-start | bytes 786440 | tf_op jit(solution)/shard_map/ppermute | solution.py:328
  125.9 5.4 %dion_mixes.1 = (f32[512,256]{1,0:T(8,128)S(1)}, f32[512,256]{1,0:T(8,128)S(1)}) custom-call(f32[256,768]{1,0:T(8,128)S(1)} %bitcast.16, f32[256,768]{1,0:T(8,128)S(1)} %collective-permute-done.12.other_ref, f32[512,256]{1,0:T(8,128)S(1)} %get-tuple-element.34.mixed_ref, f32[256,512]{1,0:T(8,128)S(1)} %get-tuple-element.30.half_ref), custom_call_target="tpu_custom_call" | custom-call | flops 5368709120 | bytes 4194304 | tf_op jit(solution)/shard_map/dion_mixes/pallas_call | solution.py:271
  131.2 2.6 %dion_factors.1 = (f32[1,512,256]{2,1,0:T(8,128)}, f32[1,512,256]{2,1,0:T(8,128)}) custom-call(s32[3]{0:T(128)S(1)} %copy-done.3, f32[512,256]{1,0:T(8,128)S(1)} %get-tuple-element.35.left_mix, f32[512,256]{1,0:T(8,128)S(1)} %get-tuple-element.36.right_mix, bf16[256,1024]{1,0:T(8,128)(2,1)S(1)} %bitcast.19, ...), custom_call_target="tpu_custom_call" | custom-call | flops 2147483648 | bytes 4194304 | tf_op jit(solution)/shard_map/dion_factors/pallas_call | solution.py:293
  133.8 0.9 maximum_select_fusion
  (33 shorter events, 4.1 us)
Async XLA Ops:
  0.6 22.1 %collective-permute-start.1 = (bf16[1,8192,512]{2,1,0:T(8,128)(2,1)}, bf16[1,8192,512]{2,1,0:T(8,128)(2,1)}, u32[]{:S(2)}, u32[]{:S(2)}) collective-permute-start(bf16[1,8192,512]{2,1,0:T(8,128)(2,1)} %w_mine_ref.1), channel_id=1, source_target_pairs={{0,1},{1,0},{2,3},{3,2},{4,5},{5,4},{6,7},{7,6},{8,9},{9,8},{10,11... | collective-permute-start | bytes 25165832 | tf_op jit(solution)/shard_map/ppermute | solution.py:313
  2.7 18.1 %copy-start.4 = (f32[1,512,256]{2,1,0:T(8,128)S(1)}, f32[1,512,256]{2,1,0:T(8,128)}, u32[]{:S(2)}) copy-start(f32[1,512,256]{2,1,0:T(8,128)} %basis_ref.1) | copy-start | bytes 1572868
  3.9 29.1 %all-to-all-start = ((bf16[8,32,1024]{2,1,0:T(8,128)(2,1)}), bf16[8,32,1024]{2,1,0:T(8,128)(2,1)S(1)}, u32[]{:S(2)}, u32[]{:S(2)}) async-start(bf16[8,32,1024]{2,1,0:T(8,128)(2,1)} %bitcast.13), calls=%async_computation | async-start | bytes 1048576 | tf_op jit(solution)/shard_map/all_to_all | solution.py:322
  20.6 15.7 %copy-start = (bf16[512,512]{1,0:T(8,128)(2,1)S(1)}, bf16[512,512]{1,0:T(8,128)(2,1)}, u32[]{:S(2)}) copy-start(bf16[512,512]{1,0:T(8,128)(2,1)} %attention_backward.1.mine_ref.g_ref) | copy-start | bytes 1572868
  20.6 2.1 %collective-permute-start = (bf16[512,512]{1,0:T(8,128)(2,1)}, bf16[512,512]{1,0:T(8,128)(2,1)S(1)}, u32[]{:S(2)}, u32[]{:S(2)}) collective-permute-start(bf16[512,512]{1,0:T(8,128)(2,1)} %attention_backward.1.mine_ref.g_ref), channel_id=1, source_target_pairs={{0,1},{1,0},{2,3},{3,2},{4,5},{5,4},{6,7},{7,6},{8,9},{9,8},{10,11... | collective-permute-start | bytes 1572872 | tf_op jit(solution)/shard_map/ppermute | solution.py:313
  20.9 15.4 %collective-permute-start.6 = (f32[1,512,256]{2,1,0:T(8,128)S(1)}, f32[1,512,256]{2,1,0:T(8,128)S(1)}, u32[]{:S(2)}, u32[]{:S(2)}) collective-permute-start(f32[1,512,256]{2,1,0:T(8,128)S(1)} %copy-done.4), channel_id=1, source_target_pairs={{0,1},{1,0},{2,3},{3,2},{4,5},{5,4},{6,7},{7,6},{8,9},{9,8},{10,11... | collective-permute-start | bytes 1572872 | tf_op jit(solution)/shard_map/ppermute | solution.py:313
  22.7 0.8 copy-start.1
  33.0 3.3 %collective-permute-start.7 = (bf16[256,1024]{1,0:T(8,128)(2,1)S(1)}, bf16[256,1024]{1,0:T(8,128)(2,1)S(1)}, u32[]{:S(2)}, u32[]{:S(2)}) collective-permute-start(bf16[256,1024]{1,0:T(8,128)(2,1)S(1)} %bitcast.17), channel_id=1, source_target_pairs={{0,1},{1,0},{2,3},{3,2},{4,5},{5,4},{6,7},{7,6},{8,9},{9,8},{10,11... | collective-permute-start | bytes 1572872 | tf_op jit(solution)/shard_map/ppermute | solution.py:313
  33.3 15.3 %collective-permute-start.2 = (bf16[64,4096]{1,0:T(8,128)(2,1)}, bf16[64,4096]{1,0:T(8,128)(2,1)S(1)}, u32[]{:S(2)}, u32[]{:S(2)}) collective-permute-start(bf16[64,4096]{1,0:T(8,128)(2,1)} %get-tuple-element.22), channel_id=1, source_target_pairs={{0,2},{1,3},{2,4},{3,5},{4,6},{5,7},{6,8},{7,9},{8,10},{9,11},{10,... | collective-permute-start | bytes 1572872 | tf_op jit(solution)/shard_map/ppermute | solution.py:318
  35.1 13.6 %collective-permute-start.4 = (bf16[64,4096]{1,0:T(8,128)(2,1)}, bf16[64,4096]{1,0:T(8,128)(2,1)}, u32[]{:S(2)}, u32[]{:S(2)}) collective-permute-start(bf16[64,4096]{1,0:T(8,128)(2,1)} %get-tuple-element.24), channel_id=1, source_target_pairs={{0,14},{1,15},{2,0},{3,1},{4,2},{5,3},{6,4},{7,5},{8,6},{9,7},{10,... | collective-permute-start | bytes 1572872 | tf_op jit(solution)/shard_map/ppermute | solution.py:318
  36.3 1.0 copy-start.2
  39.1 26.9 %all-to-all-start.1 = ((f32[8,32,768]{2,1,0:T(8,128)}), f32[8,32,768]{2,1,0:T(8,128)S(1)}, u32[]{:S(2)}, u32[]{:S(2)}) async-start(f32[8,32,768]{2,1,0:T(8,128)} %bitcast.5), calls=%async_computation.1 | async-start | bytes 1572864 | tf_op jit(solution)/shard_map/all_to_all | solution.py:322
  51.1 25.8 %collective-permute-start.3 = (bf16[64,4096]{1,0:T(8,128)(2,1)}, bf16[64,4096]{1,0:T(8,128)(2,1)S(1)}, u32[]{:S(2)}, u32[]{:S(2)}) collective-permute-start(bf16[64,4096]{1,0:T(8,128)(2,1)} %get-tuple-element.46), channel_id=1, source_target_pairs={{0,2},{1,3},{2,4},{3,5},{4,6},{5,7},{6,8},{7,9},{8,10},{9,11},{10,... | collective-permute-start | bytes 1572872 | tf_op jit(solution)/shard_map/ppermute | solution.py:318
  52.1 24.8 %collective-permute-start.5 = (bf16[64,4096]{1,0:T(8,128)(2,1)}, bf16[64,4096]{1,0:T(8,128)(2,1)S(1)}, u32[]{:S(2)}, u32[]{:S(2)}) collective-permute-start(bf16[64,4096]{1,0:T(8,128)(2,1)} %get-tuple-element.45), channel_id=1, source_target_pairs={{0,14},{1,15},{2,0},{3,1},{4,2},{5,3},{6,4},{7,5},{8,6},{9,7},{10,... | collective-permute-start | bytes 1572872 | tf_op jit(solution)/shard_map/ppermute | solution.py:318
  67.0 26.7 %all-to-all-start.2 = ((f32[8,32,768]{2,1,0:T(8,128)}), f32[8,32,768]{2,1,0:T(8,128)S(1)}, u32[]{:S(2)}, u32[]{:S(2)}) async-start(f32[8,32,768]{2,1,0:T(8,128)} %broadcast_in_dim.2), calls=%async_computation.2 | async-start | bytes 1572864 | tf_op jit(solution)/shard_map/all_to_all | solution.py:322
  79.2 25.8 %collective-permute-start.8 = (bf16[64,4096]{1,0:T(8,128)(2,1)}, bf16[64,4096]{1,0:T(8,128)(2,1)S(1)}, u32[]{:S(2)}, u32[]{:S(2)}) collective-permute-start(bf16[64,4096]{1,0:T(8,128)(2,1)} %get-tuple-element.44), channel_id=1, source_target_pairs={{0,2},{1,3},{2,4},{3,5},{4,6},{5,7},{6,8},{7,9},{8,10},{9,11},{10,... | collective-permute-start | bytes 1572872 | tf_op jit(solution)/shard_map/ppermute | solution.py:318
  79.8 25.2 %collective-permute-start.9 = (bf16[64,4096]{1,0:T(8,128)(2,1)}, bf16[64,4096]{1,0:T(8,128)(2,1)S(1)}, u32[]{:S(2)}, u32[]{:S(2)}) collective-permute-start(bf16[64,4096]{1,0:T(8,128)(2,1)} %get-tuple-element.43), channel_id=1, source_target_pairs={{0,14},{1,15},{2,0},{3,1},{4,2},{5,3},{6,4},{7,5},{8,6},{9,7},{10,... | collective-permute-start | bytes 1572872 | tf_op jit(solution)/shard_map/ppermute | solution.py:318
  93.6 15.6 %collective-permute-start.12 = (f32[256,768]{1,0:T(8,128)S(1)}, f32[256,768]{1,0:T(8,128)S(1)}, u32[]{:S(2)}, u32[]{:S(2)}) collective-permute-start(f32[256,768]{1,0:T(8,128)S(1)} %bitcast.14), channel_id=1, source_target_pairs={{0,1},{1,0},{2,3},{3,2},{4,5},{5,4},{6,7},{7,6},{8,9},{9,8},{10,11... | collective-permute-start | bytes 2359304 | tf_op jit(solution)/shard_map/ppermute | solution.py:313
  106.4 9.6 %collective-permute-start.10 = (bf16[64,2048]{1,0:T(8,128)(2,1)S(1)}, bf16[64,2048]{1,0:T(8,128)(2,1)S(1)}, u32[]{:S(2)}, u32[]{:S(2)}) collective-permute-start(bf16[64,2048]{1,0:T(8,128)(2,1)S(1)} %slice.48), channel_id=1, source_target_pairs={{0,2},{1,3},{2,4},{3,5},{4,6},{5,7},{6,8},{7,9},{8,10},{9,11},{10,... | collective-permute-start | bytes 786440 | tf_op jit(solution)/shard_map/ppermute | solution.py:318
  106.5 9.5 %collective-permute-start.11 = (bf16[64,2048]{1,0:T(8,128)(2,1)S(1)}, bf16[64,2048]{1,0:T(8,128)(2,1)S(1)}, u32[]{:S(2)}, u32[]{:S(2)}) collective-permute-start(bf16[64,2048]{1,0:T(8,128)(2,1)S(1)} %slice.49), channel_id=1, source_target_pairs={{0,14},{1,15},{2,0},{3,1},{4,2},{5,3},{6,4},{7,5},{8,6},{9,7},{10,... | collective-permute-start | bytes 786440 | tf_op jit(solution)/shard_map/ppermute | solution.py:318
  116.2 17.7 %collective-permute-start.13 = (bf16[32,4096]{1,0:T(8,128)(2,1)S(1)}, bf16[32,4096]{1,0:T(8,128)(2,1)S(1)}, u32[]{:S(2)}, u32[]{:S(2)}) collective-permute-start(bf16[32,4096]{1,0:T(8,128)(2,1)S(1)} %get-tuple-element.48), channel_id=1, source_target_pairs={{16,0},{17,1},{18,2},{19,3},{20,4},{21,5},{22,6},{23,7},{24,8},{25... | collective-permute-start | bytes 786440 | tf_op jit(solution)/shard_map/ppermute | solution.py:328
  121.1 10.1 %copy-start.3 = (s32[3]{0:T(128)S(1)}, s32[3]{0:T(128)}, u32[]{:S(2)}) copy-start(s32[3]{0:T(128)} %pad_add_fusion.info) | copy-start | bytes 40
  121.1 12.7 %collective-permute-start.14 = (bf16[32,4096]{1,0:T(8,128)(2,1)S(1)}, bf16[32,4096]{1,0:T(8,128)(2,1)S(1)}, u32[]{:S(2)}, u32[]{:S(2)}) collective-permute-start(bf16[32,4096]{1,0:T(8,128)(2,1)S(1)} %get-tuple-element.47), channel_id=1, source_target_pairs={{16,1},{17,0},{18,3},{19,2},{20,5},{21,4},{22,7},{23,6},{24,9},{25... | collective-permute-start | bytes 786440 | tf_op jit(solution)/shard_map/ppermute | solution.py:328

commit v5 on v4

--- a/solution.py
+++ b/solution.py
@@ -305,6 +305,22 @@
     )(info, left_mix, right_mix, inputs, inputs_other, query_grad)
 
 
+def column_kernel(rows_ref, out_ref):
+    width = out_ref.shape[2]
+    for n in range(out_ref.shape[0]):
+        out_ref[n] = rows_ref[0, :, n * width : (n + 1) * width]
+
+
+def column_blocks(rows):
+    return pl.pallas_call(
+        column_kernel,
+        out_shape=jax.ShapeDtypeStruct((ZN, rows.shape[1], rows.shape[2] // ZN), rows.dtype),
+        compiler_params=pltpu.CompilerParams(vmem_limit_bytes=58 << 20),
+        cost_estimate=pl.CostEstimate(flops=0, bytes_accessed=1 << 20, transcendentals=0),
+        name="column_blocks",
+    )(rows)
+
+
 def after(value, other):
     return lax.optimization_barrier((value, other))[0]
 
@@ -339,7 +355,7 @@
     w_other = swap_cores(query_weight)
     basis_other = swap_cores(dion_basis)
 
-    by_column = layer_input[0].reshape(CHUNK, ZN, D // ZN).transpose(1, 0, 2)
+    by_column = column_blocks(layer_input)
     own_columns = exchange_z(by_column).reshape(half_tokens, D // ZN)
 
     query_grad = attention(info, lengths, queries, out_grad, key_rows, value_rows)

time: 135 us -> 135 us (level)
  local copies, waits for them, and re-layouts: 5.3 us -> 2.84 us
  Pallas kernels: 33.8 us -> 35.8 us
    pallas_call x0 -> x1, Pallas kernels: none -> 1.91 us  [column_blocks(): pl.pallas_call(column_kernel, out_shape=jax.ShapeDtypeStruct((ZN, rows.sh...]
    unnamed x11 -> x10, local copies, waits for them, and re-layouts: 3.18 us -> 1.84 us
  transfers between devices with their start and end apart: 18 -> 18, of which waited for: 6 -> 6; matrix products, arithmetic and copies ran while one was open for 7% -> 6% of each run, Pallas kernels for 25% -> 27%
where the time goes in v5:
time: 135 us; the launch traced here: 134 us
  starting transfers between devices  48.9 us (36%)
  waiting for transfers between devices  38 us (28%)
  Pallas kernels  35.8 us (27%)
  other arithmetic  7.73 us (6%)
  local copies, waits for them, and re-layouts  2.84 us (2%)
    all_to_all x3, waiting for transfers between devices, exchange_z(): lax.all_to_all(value, 'tensor', 0, 0, tiled=True, axis_index_groups=z_gro...  23.9 us
    all_to_all x3, starting transfers between devices, exchange_z(): lax.all_to_all(value, 'tensor', 0, 0, tiled=True, axis_index_groups=z_gro...  20.8 us
    ppermute x8, waiting for transfers between devices, along_z(): lax.ppermute(value, 'tensor', [(i, (i + 2 * steps) % count) for i in rang...  12.5 us
    ppermute x8, starting transfers between devices, along_z(): lax.ppermute(value, 'tensor', [(i, (i + 2 * steps) % count) for i in rang...  11.1 us
    pallas_call x1, Pallas kernels, layer_partial(): pl.pallas_call(layer_kernel, out_shape=[jax.ShapeDtypeStruct((count, colu...  9.47 us
    ppermute x2, starting transfers between devices, shift_sections(): return lax.ppermute(value, ('section', 'tensor'), pairs)  9.44 us
    pallas_call x1, Pallas kernels, attention(): pl.pallas_call(attention_kernel, out_shape=jax.ShapeDtypeStruct((tokens,...  7.93 us
    ppermute x5, starting transfers between devices, swap_cores(): return lax.ppermute(value, 'tensor', [(i, i ^ 1) for i in range(2 * ZN)])  7.5 us
  transfers between devices with their start and end apart: 18, of which 6 were waited for; matrix products, arithmetic and copies ran while one was open for 6% of the time, Pallas kernels for 27%

profile of v5, /device:TPU:7, one launch (start us, length us, event | category | flops | bytes accessed | tf_op | source)
XLA Modules:
  0.0 134.0 jit_solution(12285657006317385557)
XLA Ops:
  1.4 1.9 %column_blocks.1 = bf16[8,32,1024]{2,1,0:T(8,128)(2,1)} custom-call(bf16[1,32,8192]{2,1,0:T(8,128)(2,1)} %rows_ref.1), custom_call_target="tpu_custom_call" | custom-call | bytes 1048576 | tf_op jit(solution)/shard_map/column_blocks/pallas_call | solution.py:315
  3.3 8.2 %all-to-all-start = ((bf16[8,32,1024]{2,1,0:T(8,128)(2,1)}), bf16[8,32,1024]{2,1,0:T(8,128)(2,1)S(1)}, u32[]{:S(2)}, u32[]{:S(2)}) async-start(bf16[8,32,1024]{2,1,0:T(8,128)(2,1)} %column_blocks.1), calls=%async_computation | async-start | bytes 1048576 | tf_op jit(solution)/shard_map/all_to_all | solution.py:338
  12.1 7.9 %attention_backward.1.mine_ref.g_ref = bf16[512,512]{1,0:T(8,128)(2,1)} custom-call(s32[3]{0:T(128)} %pad_add_fusion.info, s32[1,3]{1,0:T(1,128)} %lens.1, bf16[1,512,512]{2,1,0:T(8,128)(2,1)} %q_ref.1, bf16[1,512,512]{2,1,0:T(8,128)(2,1)} %g_ref.1, bf16[1,512,1024]{2,1,0:T(8,128)(2,1)} %k_ref.1, bf16[1,512,1024]{2,1,0:T(8,128)(2,1)} %v_ref.1), custom_call_target="tpu_custom_call" | custom-call | flops 1048576 | bytes 1048576 | tf_op jit(solution)/shard_map/attention_backward/pallas_call | solution.py:78
  20.5 1.6 %collective-permute-done.other_ref = bf16[512,512]{1,0:T(8,128)(2,1)S(1)} collective-permute-done((bf16[512,512]{1,0:T(8,128)(2,1)}, bf16[512,512]{1,0:T(8,128)(2,1)S(1)}, u32[]{:S(2)}, u32[]{:S(2)}) %collective-permute-start) | collective-permute-done | bytes 524320 | tf_op jit(solution)/shard_map/ppermute | solution.py:329
  22.1 0.8 copy-done.1
  22.9 9.5 %layer_partial.1 = (bf16[64,4096]{1,0:T(8,128)(2,1)}, bf16[64,4096]{1,0:T(8,128)(2,1)}, bf16[384,4096]{1,0:T(8,128)(2,1)}) custom-call(s32[3]{0:T(128)} %pad_add_fusion.info, bf16[512,512]{1,0:T(8,128)(2,1)} %attention_backward.1.mine_ref.g_ref, bf16[512,512]{1,0:T(8,128)(2,1)} %copy-done.1, bf16[1,8192,512]{2,1,0:T(8,128)(2,1)} %w_mine_ref.1, ...), custom_call_target="tpu_custom_call" | custom-call | flops 1048576 | bytes 1048576 | tf_op jit(solution)/shard_map/layer_partial/pallas_call | solution.py:131
  32.8 1.8 %collective-permute-start.2 = (bf16[64,4096]{1,0:T(8,128)(2,1)}, bf16[64,4096]{1,0:T(8,128)(2,1)S(1)}, u32[]{:S(2)}, u32[]{:S(2)}) collective-permute-start(bf16[64,4096]{1,0:T(8,128)(2,1)} %get-tuple-element.22), channel_id=1, source_target_pairs={{0,2},{1,3},{2,4},{3,5},{4,6},{5,7},{6,8},{7,9},{8,10},{9,11},{10,... | collective-permute-start | bytes 1572872 | tf_op jit(solution)/shard_map/ppermute | solution.py:334
  34.6 1.2 collective-permute-start.4
  35.8 1.0 copy-done.2
  36.8 1.8 %chip_parts.1 = f32[256,768]{1,0:T(8,128)} custom-call(bf16[512,512]{1,0:T(8,128)(2,1)S(1)} %copy-done, bf16[512,512]{1,0:T(8,128)(2,1)S(1)} %copy-done.2, f32[1,512,256]{2,1,0:T(8,128)S(1)} %copy-done.4, f32[1,512,256]{2,1,0:T(8,128)S(1)} %collective-permute-done.6.basis_other_ref, bf16[256,1024]{1,0:T(8,128)(2,1)S(1)} %bitcast.12, ...), custom_call_target="tpu_custom_call" | custom-call | flops 1073741824 | bytes 4194304 | tf_op jit(solution)/shard_map/chip_parts/pallas_call | solution.py:178
  38.6 6.6 %all-to-all-start.1 = ((f32[8,32,768]{2,1,0:T(8,128)}), f32[8,32,768]{2,1,0:T(8,128)S(1)}, u32[]{:S(2)}, u32[]{:S(2)}) async-start(f32[8,32,768]{2,1,0:T(8,128)} %bitcast.4), calls=%async_computation.1 | async-start | bytes 1572864 | tf_op jit(solution)/shard_map/all_to_all | solution.py:338
  45.2 3.0 %collective-permute-done.2 = bf16[64,4096]{1,0:T(8,128)(2,1)S(1)} collective-permute-done((bf16[64,4096]{1,0:T(8,128)(2,1)}, bf16[64,4096]{1,0:T(8,128)(2,1)S(1)}, u32[]{:S(2)}, u32[]{:S(2)}) %collective-permute-start.2) | collective-permute-done | bytes 524320 | tf_op jit(solution)/shard_map/ppermute | solution.py:334
  48.2 2.4 %slice_add_fusion.4 = (bf16[64,4096]{1,0:T(8,128)(2,1)}, bf16[64,4096]{1,0:T(8,128)(2,1)}) fusion(bf16[64,4096]{1,0:T(8,128)(2,1)} %collective-permute-done.4, bf16[384,4096]{1,0:T(8,128)(2,1)} %get-tuple-element.23, bf16[64,4096]{1,0:T(8,128)(2,1)S(1)} %collective-permute-done.2), kind=kLoop, calls=%fused_computation.12 | loop fusion | flops 524288 | bytes 3145728 | tf_op jit(solution)/shard_map/add | solution.py:384
  50.6 0.9 collective-permute-start.3
  51.6 1.8 %collective-permute-start.5 = (bf16[64,4096]{1,0:T(8,128)(2,1)}, bf16[64,4096]{1,0:T(8,128)(2,1)S(1)}, u32[]{:S(2)}, u32[]{:S(2)}) collective-permute-start(bf16[64,4096]{1,0:T(8,128)(2,1)} %get-tuple-element.45), channel_id=1, source_target_pairs={{0,14},{1,15},{2,0},{3,1},{4,2},{5,3},{6,4},{7,5},{8,6},{9,7},{10,... | collective-permute-start | bytes 1572872 | tf_op jit(solution)/shard_map/ppermute | solution.py:334
  53.3 12.1 %all-to-all-done.1 = f32[8,32,768]{2,1,0:T(8,128)S(1)} async-done(((f32[8,32,768]{2,1,0:T(8,128)}), f32[8,32,768]{2,1,0:T(8,128)S(1)}, u32[]{:S(2)}, u32[]{:S(2)}) %all-to-all-start.1) | async-done | bytes 786464 | tf_op jit(solution)/shard_map/all_to_all | solution.py:338
  65.5 1.0 broadcast_in_dim.2
  66.5 6.0 %all-to-all-start.2 = ((f32[8,32,768]{2,1,0:T(8,128)}), f32[8,32,768]{2,1,0:T(8,128)S(1)}, u32[]{:S(2)}, u32[]{:S(2)}) async-start(f32[8,32,768]{2,1,0:T(8,128)} %broadcast_in_dim.2), calls=%async_computation.2 | async-start | bytes 1572864 | tf_op jit(solution)/shard_map/all_to_all | solution.py:338
  72.4 4.0 %collective-permute-done.3 = bf16[64,4096]{1,0:T(8,128)(2,1)S(1)} collective-permute-done((bf16[64,4096]{1,0:T(8,128)(2,1)}, bf16[64,4096]{1,0:T(8,128)(2,1)S(1)}, u32[]{:S(2)}, u32[]{:S(2)}) %collective-permute-start.3) | collective-permute-done | bytes 524320 | tf_op jit(solution)/shard_map/ppermute | solution.py:334
  76.4 2.3 %slice_add_fusion.2 = (bf16[64,4096]{1,0:T(8,128)(2,1)}, bf16[64,4096]{1,0:T(8,128)(2,1)}) fusion(bf16[64,4096]{1,0:T(8,128)(2,1)S(1)} %collective-permute-done.5, bf16[384,4096]{1,0:T(8,128)(2,1)} %get-tuple-element.23, bf16[64,4096]{1,0:T(8,128)(2,1)S(1)} %collective-permute-done.3), kind=kLoop, calls=%fused_computation.10 | loop fusion | flops 524288 | bytes 3145728 | tf_op jit(solution)/shard_map/add | solution.py:384
  79.3 2.0 %collective-permute-start.9 = (bf16[64,4096]{1,0:T(8,128)(2,1)}, bf16[64,4096]{1,0:T(8,128)(2,1)S(1)}, u32[]{:S(2)}, u32[]{:S(2)}) collective-permute-start(bf16[64,4096]{1,0:T(8,128)(2,1)} %get-tuple-element.43), channel_id=1, source_target_pairs={{0,14},{1,15},{2,0},{3,1},{4,2},{5,3},{6,4},{7,5},{8,6},{9,7},{10,... | collective-permute-start | bytes 1572872 | tf_op jit(solution)/shard_map/ppermute | solution.py:334
  81.3 11.8 %all-to-all-done.2 = f32[8,32,768]{2,1,0:T(8,128)S(1)} async-done(((f32[8,32,768]{2,1,0:T(8,128)}), f32[8,32,768]{2,1,0:T(8,128)S(1)}, u32[]{:S(2)}, u32[]{:S(2)}) %all-to-all-start.2) | async-done | bytes 786464 | tf_op jit(solution)/shard_map/all_to_all | solution.py:338
  93.1 5.8 %collective-permute-start.12 = (f32[256,768]{1,0:T(8,128)S(1)}, f32[256,768]{1,0:T(8,128)S(1)}, u32[]{:S(2)}, u32[]{:S(2)}) collective-permute-start(f32[256,768]{1,0:T(8,128)S(1)} %bitcast.8), channel_id=1, source_target_pairs={{0,1},{1,0},{2,3},{3,2},{4,5},{5,4},{6,7},{7,6},{8,9},{9,8},{10,11... | collective-permute-start | bytes 2359304 | tf_op jit(solution)/shard_map/ppermute | solution.py:329
  98.9 5.6 %collective-permute-done.8 = bf16[64,4096]{1,0:T(8,128)(2,1)S(1)} collective-permute-done((bf16[64,4096]{1,0:T(8,128)(2,1)}, bf16[64,4096]{1,0:T(8,128)(2,1)S(1)}, u32[]{:S(2)}, u32[]{:S(2)}) %collective-permute-start.8) | collective-permute-done | bytes 524320 | tf_op jit(solution)/shard_map/ppermute | solution.py:334
  104.5 1.3 slice_add_fusion
  106.0 2.7 %collective-permute-start.11 = (bf16[64,2048]{1,0:T(8,128)(2,1)S(1)}, bf16[64,2048]{1,0:T(8,128)(2,1)S(1)}, u32[]{:S(2)}, u32[]{:S(2)}) collective-permute-start(bf16[64,2048]{1,0:T(8,128)(2,1)S(1)} %slice.49), channel_id=1, source_target_pairs={{0,14},{1,15},{2,0},{3,1},{4,2},{5,3},{6,4},{7,5},{8,6},{9,7},{10,... | collective-permute-start | bytes 786440 | tf_op jit(solution)/shard_map/ppermute | solution.py:334
  108.7 6.7 %dion_gram.1 = (f32[512,256]{1,0:T(8,128)S(1)}, f32[256,512]{1,0:T(8,128)S(1)}) custom-call(f32[256,768]{1,0:T(8,128)S(1)} %bitcast.9, f32[256,768]{1,0:T(8,128)S(1)} %collective-permute-done.12.other_ref), custom_call_target="tpu_custom_call" | custom-call | flops 5368709120 | bytes 4194304 | tf_op jit(solution)/shard_map/dion_gram/pallas_call | solution.py:248
  115.6 4.9 %collective-permute-start.13 = (bf16[32,4096]{1,0:T(8,128)(2,1)S(1)}, bf16[32,4096]{1,0:T(8,128)(2,1)S(1)}, u32[]{:S(2)}, u32[]{:S(2)}) collective-permute-start(bf16[32,4096]{1,0:T(8,128)(2,1)S(1)} %get-tuple-element.48), channel_id=1, source_target_pairs={{16,0},{17,1},{18,2},{19,3},{20,4},{21,5},{22,6},{23,7},{24,8},{25... | collective-permute-start | bytes 786440 | tf_op jit(solution)/shard_map/ppermute | solution.py:344
  120.6 4.5 %collective-permute-start.14 = (bf16[32,4096]{1,0:T(8,128)(2,1)S(1)}, bf16[32,4096]{1,0:T(8,128)(2,1)S(1)}, u32[]{:S(2)}, u32[]{:S(2)}) collective-permute-start(bf16[32,4096]{1,0:T(8,128)(2,1)S(1)} %get-tuple-element.47), channel_id=1, source_target_pairs={{16,1},{17,0},{18,3},{19,2},{20,5},{21,4},{22,7},{23,6},{24,9},{25... | collective-permute-start | bytes 786440 | tf_op jit(solution)/shard_map/ppermute | solution.py:344
  125.1 5.4 %dion_mixes.1 = (f32[512,256]{1,0:T(8,128)S(1)}, f32[512,256]{1,0:T(8,128)S(1)}) custom-call(f32[256,768]{1,0:T(8,128)S(1)} %bitcast.10, f32[256,768]{1,0:T(8,128)S(1)} %collective-permute-done.12.other_ref, f32[512,256]{1,0:T(8,128)S(1)} %get-tuple-element.34.mixed_ref, f32[256,512]{1,0:T(8,128)S(1)} %get-tuple-element.30.half_ref), custom_call_target="tpu_custom_call" | custom-call | flops 5368709120 | bytes 4194304 | tf_op jit(solution)/shard_map/dion_mixes/pallas_call | solution.py:271
  130.5 2.6 %dion_factors.1 = (f32[1,512,256]{2,1,0:T(8,128)}, f32[1,512,256]{2,1,0:T(8,128)}) custom-call(s32[3]{0:T(128)S(1)} %copy-done.3, f32[512,256]{1,0:T(8,128)S(1)} %get-tuple-element.35.left_mix, f32[512,256]{1,0:T(8,128)S(1)} %get-tuple-element.36.right_mix, bf16[256,1024]{1,0:T(8,128)(2,1)S(1)} %bitcast.13, ...), custom_call_target="tpu_custom_call" | custom-call | flops 2147483648 | bytes 4194304 | tf_op jit(solution)/shard_map/dion_factors/pallas_call | solution.py:293
  133.1 0.9 maximum_select_fusion
  (32 shorter events, 3.3 us)
Async XLA Ops:
  0.6 19.7 %copy-start.4 = (f32[1,512,256]{2,1,0:T(8,128)S(1)}, f32[1,512,256]{2,1,0:T(8,128)}, u32[]{:S(2)}) copy-start(f32[1,512,256]{2,1,0:T(8,128)} %basis_ref.1) | copy-start | bytes 1572868
  0.6 21.5 %collective-permute-start.1 = (bf16[1,8192,512]{2,1,0:T(8,128)(2,1)}, bf16[1,8192,512]{2,1,0:T(8,128)(2,1)}, u32[]{:S(2)}, u32[]{:S(2)}) collective-permute-start(bf16[1,8192,512]{2,1,0:T(8,128)(2,1)} %w_mine_ref.1), channel_id=1, source_target_pairs={{0,1},{1,0},{2,3},{3,2},{4,5},{5,4},{6,7},{7,6},{8,9},{9,8},{10,11... | collective-permute-start | bytes 25165832 | tf_op jit(solution)/shard_map/ppermute | solution.py:329
  3.3 29.1 %all-to-all-start = ((bf16[8,32,1024]{2,1,0:T(8,128)(2,1)}), bf16[8,32,1024]{2,1,0:T(8,128)(2,1)S(1)}, u32[]{:S(2)}, u32[]{:S(2)}) async-start(bf16[8,32,1024]{2,1,0:T(8,128)(2,1)} %column_blocks.1), calls=%async_computation | async-start | bytes 1048576 | tf_op jit(solution)/shard_map/all_to_all | solution.py:338
  20.0 15.8 %copy-start = (bf16[512,512]{1,0:T(8,128)(2,1)S(1)}, bf16[512,512]{1,0:T(8,128)(2,1)}, u32[]{:S(2)}) copy-start(bf16[512,512]{1,0:T(8,128)(2,1)} %attention_backward.1.mine_ref.g_ref) | copy-start | bytes 1572868
  20.0 2.1 %collective-permute-start = (bf16[512,512]{1,0:T(8,128)(2,1)}, bf16[512,512]{1,0:T(8,128)(2,1)S(1)}, u32[]{:S(2)}, u32[]{:S(2)}) collective-permute-start(bf16[512,512]{1,0:T(8,128)(2,1)} %attention_backward.1.mine_ref.g_ref), channel_id=1, source_target_pairs={{0,1},{1,0},{2,3},{3,2},{4,5},{5,4},{6,7},{7,6},{8,9},{9,8},{10,11... | collective-permute-start | bytes 1572872 | tf_op jit(solution)/shard_map/ppermute | solution.py:329
  20.4 15.4 %collective-permute-start.6 = (f32[1,512,256]{2,1,0:T(8,128)S(1)}, f32[1,512,256]{2,1,0:T(8,128)S(1)}, u32[]{:S(2)}, u32[]{:S(2)}) collective-permute-start(f32[1,512,256]{2,1,0:T(8,128)S(1)} %copy-done.4), channel_id=1, source_target_pairs={{0,1},{1,0},{2,3},{3,2},{4,5},{5,4},{6,7},{7,6},{8,9},{9,8},{10,11... | collective-permute-start | bytes 1572872 | tf_op jit(solution)/shard_map/ppermute | solution.py:329
  22.1 0.8 copy-start.1
  32.4 3.4 %collective-permute-start.7 = (bf16[256,1024]{1,0:T(8,128)(2,1)S(1)}, bf16[256,1024]{1,0:T(8,128)(2,1)S(1)}, u32[]{:S(2)}, u32[]{:S(2)}) collective-permute-start(bf16[256,1024]{1,0:T(8,128)(2,1)S(1)} %bitcast.11), channel_id=1, source_target_pairs={{0,1},{1,0},{2,3},{3,2},{4,5},{5,4},{6,7},{7,6},{8,9},{9,8},{10,11... | collective-permute-start | bytes 1572872 | tf_op jit(solution)/shard_map/ppermute | solution.py:329
  32.8 15.4 %collective-permute-start.2 = (bf16[64,4096]{1,0:T(8,128)(2,1)}, bf16[64,4096]{1,0:T(8,128)(2,1)S(1)}, u32[]{:S(2)}, u32[]{:S(2)}) collective-permute-start(bf16[64,4096]{1,0:T(8,128)(2,1)} %get-tuple-element.22), channel_id=1, source_target_pairs={{0,2},{1,3},{2,4},{3,5},{4,6},{5,7},{6,8},{7,9},{8,10},{9,11},{10,... | collective-permute-start | bytes 1572872 | tf_op jit(solution)/shard_map/ppermute | solution.py:334
  34.6 13.6 %collective-permute-start.4 = (bf16[64,4096]{1,0:T(8,128)(2,1)}, bf16[64,4096]{1,0:T(8,128)(2,1)}, u32[]{:S(2)}, u32[]{:S(2)}) collective-permute-start(bf16[64,4096]{1,0:T(8,128)(2,1)} %get-tuple-element.24), channel_id=1, source_target_pairs={{0,14},{1,15},{2,0},{3,1},{4,2},{5,3},{6,4},{7,5},{8,6},{9,7},{10,... | collective-permute-start | bytes 1572872 | tf_op jit(solution)/shard_map/ppermute | solution.py:334
  35.8 1.0 copy-start.2
  38.6 26.9 %all-to-all-start.1 = ((f32[8,32,768]{2,1,0:T(8,128)}), f32[8,32,768]{2,1,0:T(8,128)S(1)}, u32[]{:S(2)}, u32[]{:S(2)}) async-start(f32[8,32,768]{2,1,0:T(8,128)} %bitcast.4), calls=%async_computation.1 | async-start | bytes 1572864 | tf_op jit(solution)/shard_map/all_to_all | solution.py:338
  50.6 25.8 %collective-permute-start.3 = (bf16[64,4096]{1,0:T(8,128)(2,1)}, bf16[64,4096]{1,0:T(8,128)(2,1)S(1)}, u32[]{:S(2)}, u32[]{:S(2)}) collective-permute-start(bf16[64,4096]{1,0:T(8,128)(2,1)} %get-tuple-element.46), channel_id=1, source_target_pairs={{0,2},{1,3},{2,4},{3,5},{4,6},{5,7},{6,8},{7,9},{8,10},{9,11},{10,... | collective-permute-start | bytes 1572872 | tf_op jit(solution)/shard_map/ppermute | solution.py:334
  51.6 24.8 %collective-permute-start.5 = (bf16[64,4096]{1,0:T(8,128)(2,1)}, bf16[64,4096]{1,0:T(8,128)(2,1)S(1)}, u32[]{:S(2)}, u32[]{:S(2)}) collective-permute-start(bf16[64,4096]{1,0:T(8,128)(2,1)} %get-tuple-element.45), channel_id=1, source_target_pairs={{0,14},{1,15},{2,0},{3,1},{4,2},{5,3},{6,4},{7,5},{8,6},{9,7},{10,... | collective-permute-start | bytes 1572872 | tf_op jit(solution)/shard_map/ppermute | solution.py:334
  66.5 26.7 %all-to-all-start.2 = ((f32[8,32,768]{2,1,0:T(8,128)}), f32[8,32,768]{2,1,0:T(8,128)S(1)}, u32[]{:S(2)}, u32[]{:S(2)}) async-start(f32[8,32,768]{2,1,0:T(8,128)} %broadcast_in_dim.2), calls=%async_computation.2 | async-start | bytes 1572864 | tf_op jit(solution)/shard_map/all_to_all | solution.py:338
  78.7 25.8 %collective-permute-start.8 = (bf16[64,4096]{1,0:T(8,128)(2,1)}, bf16[64,4096]{1,0:T(8,128)(2,1)S(1)}, u32[]{:S(2)}, u32[]{:S(2)}) collective-permute-start(bf16[64,4096]{1,0:T(8,128)(2,1)} %get-tuple-element.44), channel_id=1, source_target_pairs={{0,2},{1,3},{2,4},{3,5},{4,6},{5,7},{6,8},{7,9},{8,10},{9,11},{10,... | collective-permute-start | bytes 1572872 | tf_op jit(solution)/shard_map/ppermute | solution.py:334
  79.3 25.2 %collective-permute-start.9 = (bf16[64,4096]{1,0:T(8,128)(2,1)}, bf16[64,4096]{1,0:T(8,128)(2,1)S(1)}, u32[]{:S(2)}, u32[]{:S(2)}) collective-permute-start(bf16[64,4096]{1,0:T(8,128)(2,1)} %get-tuple-element.43), channel_id=1, source_target_pairs={{0,14},{1,15},{2,0},{3,1},{4,2},{5,3},{6,4},{7,5},{8,6},{9,7},{10,... | collective-permute-start | bytes 1572872 | tf_op jit(solution)/shard_map/ppermute | solution.py:334
  93.1 15.6 %collective-permute-start.12 = (f32[256,768]{1,0:T(8,128)S(1)}, f32[256,768]{1,0:T(8,128)S(1)}, u32[]{:S(2)}, u32[]{:S(2)}) collective-permute-start(f32[256,768]{1,0:T(8,128)S(1)} %bitcast.8), channel_id=1, source_target_pairs={{0,1},{1,0},{2,3},{3,2},{4,5},{5,4},{6,7},{7,6},{8,9},{9,8},{10,11... | collective-permute-start | bytes 2359304 | tf_op jit(solution)/shard_map/ppermute | solution.py:329
  105.8 9.6 %collective-permute-start.10 = (bf16[64,2048]{1,0:T(8,128)(2,1)S(1)}, bf16[64,2048]{1,0:T(8,128)(2,1)S(1)}, u32[]{:S(2)}, u32[]{:S(2)}) collective-permute-start(bf16[64,2048]{1,0:T(8,128)(2,1)S(1)} %slice.48), channel_id=1, source_target_pairs={{0,2},{1,3},{2,4},{3,5},{4,6},{5,7},{6,8},{7,9},{8,10},{9,11},{10,... | collective-permute-start | bytes 786440 | tf_op jit(solution)/shard_map/ppermute | solution.py:334
  106.0 9.5 %collective-permute-start.11 = (bf16[64,2048]{1,0:T(8,128)(2,1)S(1)}, bf16[64,2048]{1,0:T(8,128)(2,1)S(1)}, u32[]{:S(2)}, u32[]{:S(2)}) collective-permute-start(bf16[64,2048]{1,0:T(8,128)(2,1)S(1)} %slice.49), channel_id=1, source_target_pairs={{0,14},{1,15},{2,0},{3,1},{4,2},{5,3},{6,4},{7,5},{8,6},{9,7},{10,... | collective-permute-start | bytes 786440 | tf_op jit(solution)/shard_map/ppermute | solution.py:334
  115.6 17.4 %collective-permute-start.13 = (bf16[32,4096]{1,0:T(8,128)(2,1)S(1)}, bf16[32,4096]{1,0:T(8,128)(2,1)S(1)}, u32[]{:S(2)}, u32[]{:S(2)}) collective-permute-start(bf16[32,4096]{1,0:T(8,128)(2,1)S(1)} %get-tuple-element.48), channel_id=1, source_target_pairs={{16,0},{17,1},{18,2},{19,3},{20,4},{21,5},{22,6},{23,7},{24,8},{25... | collective-permute-start | bytes 786440 | tf_op jit(solution)/shard_map/ppermute | solution.py:344
  120.5 9.9 %copy-start.3 = (s32[3]{0:T(128)S(1)}, s32[3]{0:T(128)}, u32[]{:S(2)}) copy-start(s32[3]{0:T(128)} %pad_add_fusion.info) | copy-start | bytes 40
  120.6 12.5 %collective-permute-start.14 = (bf16[32,4096]{1,0:T(8,128)(2,1)S(1)}, bf16[32,4096]{1,0:T(8,128)(2,1)S(1)}, u32[]{:S(2)}, u32[]{:S(2)}) collective-permute-start(bf16[32,4096]{1,0:T(8,128)(2,1)S(1)} %get-tuple-element.47), channel_id=1, source_target_pairs={{16,1},{17,0},{18,3},{19,2},{20,5},{21,4},{22,7},{23,6},{24,9},{25... | collective-permute-start | bytes 786440 | tf_op jit(solution)/shard_map/ppermute | solution.py:344
